TPU v7x, 256 devices: a whole 4x4x8 slice. The times are simulated.
256 devices in a mesh: sym: 8 (over x, core), row: 32 (over z, y).
Axes of the slice: x: 4, y: 4, z: 8, core: 2. Of those that a mesh axis runs over, the one named last changes fastest.
Arguments:
- vectors: float32 [8, 131072, 256], P('sym', 'row'), may hold values from -6 to 6
- reflectors: float32 [8, 131072, 512], P('sym', 'row'), may hold values from -0.5 to 0.5
- factors: float32 [8, 4, 128, 128], P('sym'), may hold values from -0.015625 to 0.015625
- tiles: bfloat16 [8, 64, 512, 512], P('sym', 'row'), may hold values from -0.0014648438 to 0.0014648438
- tile_left: int32 [8, 64], P('sym', 'row'), may hold values from 0 to 7
- tile_right: int32 [8, 64], P('sym', 'row'), may hold values from 0 to 7
- tile_occupied_mask: int32 [8, 64], P('sym', 'row'), may hold values 0 or 1
- channels: int32 [8, 256], P('sym', 'row'), may hold values from 256 to 512
Outputs:
- dipole: float32 [8, 256, 256], P('sym', 'row')
All inputs are finite; a program needn't handle non-finite values. No bound on the sum of `tile_occupied_mask` on one device may be relied on, other than what follows from the above.
Results may differ from a plain program's by a relative error of at most 0.0049.
Values may be sent and summed in bfloat16 or wider, within the bound.
No kernel may reach another device: no remote copies, remote signals or barrier semaphores. Data moves between devices by JAX's collectives and lax.ppermute only.
A program may use at most 64 MiB of HBM per device.

v0:
```python
import jax
import jax.numpy as jnp
from jax import lax
from jax.sharding import PartitionSpec as P

BLOCK = 512


PRECISE = lax.Precision.HIGHEST


def rows_for(lines, count):
    spare = -lines.shape[0] % count
    if not spare:
        return lines
    return jnp.concatenate([lines, jnp.zeros((spare, *lines.shape[1:]), lines.dtype)])


def from_everyone(array, axis):
    copies = jnp.broadcast_to(array, (lax.axis_size(axis), *array.shape))
    return lax.all_to_all(copies, axis, split_axis=0, concat_axis=0, tiled=True)


def joined_along(tiles, dim):
    lengths = list(tiles.shape[1:])
    lengths[dim] *= tiles.shape[0]
    return jnp.moveaxis(tiles, 0, dim).reshape(lengths)


def gather_directly(array, axis, dim):
    tiles = from_everyone(array, axis)
    return joined_along(tiles, dim)


def split_up(array, dim, count):
    lengths = array.shape
    tiles = array.reshape(*lengths[:dim], count, lengths[dim] // count, *lengths[dim + 1 :])
    return jnp.moveaxis(tiles, dim, 0)


def sum_at_owner(array, axis, dim):
    count = lax.axis_size(axis)
    tiles = lax.all_to_all(split_up(array, dim, count), axis, 0, 0, tiled=True)
    return jnp.sum(tiles, axis=0)


def sum_by_parts(array, axes):
    padded = rows_for(array, lax.axis_size(axes))
    whole = gather_directly(sum_at_owner(padded, axes, 0), axes, 0)
    return lax.slice_in_dim(whole, 0, len(array)).reshape(array.shape)


def together(arrays, axis):
    ends = [0]
    for a in arrays:
        ends.append(ends[-1] + a.size)
    total = sum_by_parts(jnp.concatenate([a.ravel() for a in arrays]), axis)
    return tuple((total[b:e].reshape(a.shape) for a, b, e in zip(arrays, ends, ends[1:])))


def passed_along(block, axis, distance):
    devices = range(lax.axis_size(axis))
    route = [((i - distance) % len(devices), i) for i in devices]
    return lax.ppermute(block, axis, route)


def row_inner(first, second):
    return lax.dot_general(first, second, (((0,), (0,)), ((), ())), precision=PRECISE)


def on_device(
    vectors, reflectors, factors, tiles, tile_left, tile_right, tile_occupied_mask, channels
):
    start = vectors[0]
    panels = reflectors[0]
    factor_set = factors[0]
    panel_count = factor_set.shape[0]
    panel_width = factor_set.shape[1]
    pieces = []
    for level in range(panel_count - 1):
        panel = panels[:, level * panel_width : (level + 1) * panel_width]
        pieces.append(row_inner(panel, panels[:, (level + 1) * panel_width :]).reshape(-1))
    coupled, projected = together(
        (jnp.concatenate(pieces, axis=0), row_inner(panels, start)), "row"
    )
    uppers = []
    offset = 0
    for level in range(panel_count - 1):
        later_width = (panel_count - 1 - level) * panel_width
        uppers.append(
            coupled[offset : offset + panel_width * later_width].reshape(panel_width, later_width)
        )
        offset = offset + panel_width * later_width
    updates = [None] * panel_count
    for level in reversed(range(panel_count)):
        current = projected[level * panel_width : (level + 1) * panel_width]
        for later in range(level + 1, panel_count):
            begin = (later - level - 1) * panel_width
            coupling = uppers[level][:, begin : begin + panel_width]
            current = current - jnp.dot(coupling, updates[later], precision=PRECISE)
        updates[level] = jnp.dot(factor_set[level], current, precision=PRECISE)
    result = start - jnp.dot(panels, jnp.concatenate(updates, axis=0), precision=PRECISE)
    eigen_count = result.shape[1]
    position = jnp.arange(BLOCK, dtype=jnp.int32)
    keeper = (position[None, :] < channels[0][:, None]).astype(jnp.float32)
    masked = (result.reshape(-1, BLOCK, eigen_count) * keeper[:, :, None]).astype(jnp.bfloat16)
    slots = tile_right[0]
    wanted = passed_along(slots, "sym", 1)
    packed = jnp.take(masked, wanted, axis=0)
    right_rows = passed_along(packed, "sym", -1)
    bra_state_rows = (
        jnp.take(masked, tile_left[0], axis=0)
        * tile_occupied_mask[0].astype(jnp.bfloat16)[:, None, None]
    )
    bra_ket_product = jnp.einsum(
        "tij,tjk->tik", tiles[0], right_rows, preferred_element_type=jnp.float32
    ).astype(jnp.bfloat16)
    partial_sum = jnp.einsum(
        "tji,tjk->ik", bra_state_rows, bra_ket_product, preferred_element_type=jnp.float32
    )
    shares = sum_at_owner(partial_sum, "row", 0)
    return shares[None]


def solution(mesh):
    return jax.shard_map(
        on_device,
        mesh=mesh,
        in_specs=(
            P("sym", "row", None),
            P("sym", "row", None),
            P("sym", None, None, None),
            P("sym", "row", None, None),
            P("sym", "row"),
            P("sym", "row"),
            P("sym", "row"),
            P("sym", "row"),
        ),
        out_specs=P("sym", "row", None),
        check_vma=False,
    )
```

profile of v0, /device:TPU:1, one launch (start us, length us, event | category | flops | bytes accessed | tf_op | source)
XLA Modules:
  0.0 172.8 jit_solution(15568137027823879488)
XLA Ops:
  0.0 8.1 %fusion = f32[128,384]{1,0:T(8,128)S(1)} fusion(f32[4096,512]{1,0:T(8,128)} %bitcast.78), kind=kOutput, calls=%fused_computation.2 | convolution fusion | flops 2415919104 | bytes 8585216 | tf_op jit(solution)/shard_map/dot_general | solution.py:68
  8.1 3.5 %fusion.17 = f32[16,2,8,128]{3,2,1,0:T(8,128)S(1)} fusion(f32[4096,512]{1,0:T(8,128)S(1)} %bitcast.79), kind=kOutput, calls=%fused_computation.21 | convolution fusion | flops 1610612736 | bytes 6422528 | tf_op jit(solution)/shard_map/dot_general | solution.py:68
  11.7 3.4 %convolution_bitcast_fusion.1 = f32[16384]{0:T(1024)S(1)} fusion(f32[4096,512]{1,0:T(8,128)S(1)} %bitcast.80), kind=kOutput, calls=%fused_computation.11 | convolution fusion | flops 805306368 | bytes 4259840 | tf_op jit(solution)/shard_map/dot_general | solution.py:68
  15.2 16.4 %fusion.13 = f32[64,2,8,128]{3,2,1,0:T(8,128)S(1)} fusion(f32[1,4096,256]{2,1,0:T(8,128)} %param.10, f32[1,4096,512]{2,1,0:T(8,128)} %param.11), kind=kOutput, calls=%fused_computation.19 | convolution fusion | flops 6442450944 | bytes 13107200 | tf_op jit(solution)/shard_map/dot_general | solution.py:68
  31.7 0.3 copy.29
  32.0 35.3 %all_to_all.20 = f32[32,1,7168]{2,1,0:T(1,128)S(1)} all-to-all(f32[32,1,7168]{2,1,0:T(1,128)S(1)} %bitcast.84), channel_id=1, replica_groups=mesh['sym'=8,'row'=32] {'row'}, dimensions={0} | all-to-all | bytes 1835008 | tf_op jit(solution)/shard_map/all_to_all | solution.py:43
  67.3 0.5 reduce_sum.18
  67.8 1.4 broadcast_in_dim.18
  69.2 6.4 %all-to-all-start.1 = ((f32[32,1,7168]{2,1,0:T(1,128)}), f32[32,1,7168]{2,1,0:T(1,128)S(1)}, u32[]{:S(2)}, u32[]{:S(2)}) async-start(f32[32,1,7168]{2,1,0:T(1,128)} %broadcast_in_dim.18), calls=%async_computation.1 | async-start | bytes 1835008 | tf_op jit(solution)/shard_map/all_to_all | solution.py:21
  75.6 3.3 %collective-permute-start = (s32[2]{0:T(128)S(1)}, s32[2]{0:T(128)S(1)}, u32[]{:S(2)}, u32[]{:S(2)}) collective-permute-start(s32[2]{0:T(128)S(1)} %bitcast.91), channel_id=1, source_target_pairs={{224,0},{0,32},{32,64},{64,96},{96,128},{128,160},{160,192},{192,2... | collective-permute-start | bytes 32 | tf_op jit(solution)/shard_map/ppermute | solution.py:64
  78.9 5.6 %copy.18 = f32[1,4096,256]{1,2,0:T(8,128)} copy(f32[1,4096,256]{2,1,0:T(8,128)} %param.10) | data formatting | bytes 8388608 | tf_op args[0]
  84.7 13.2 %all-to-all-done.1 = f32[32,1,7168]{2,1,0:T(1,128)S(1)} async-done(((f32[32,1,7168]{2,1,0:T(1,128)}), f32[32,1,7168]{2,1,0:T(1,128)S(1)}, u32[]{:S(2)}, u32[]{:S(2)}) %all-to-all-start.1) | async-done | bytes 917536 | tf_op jit(solution)/shard_map/all_to_all | solution.py:21
  97.9 2.2 %reduce.1 = f32[32,7168]{1,0:T(8,128)S(1)} reduce(f32[32,1,7168]{2,1,0:T(1,128)S(1)} %all-to-all-done.1, f32[]{:T(128)} %constant.20), dimensions={1}, to_apply=%all_to_all.15.reduce_sub_computation | reduce | bytes 1835012 | tf_op jit(solution)/shard_map/all_to_all | solution.py:21
  100.1 1.2 slice.102
  101.2 1.2 fusion.34
  102.4 1.2 convolution_subtract_fusion.5
  103.6 0.3 fusion.45
  103.9 1.2 convolution_subtract_fusion.4
  105.1 1.1 convolution_subtract_fusion.3
  106.5 1.2 convolution_subtract_fusion.2
  108.5 18.1 %fusion.2 = f32[4096,256]{0,1:T(8,128)} fusion(f32[1,4096,256]{1,2,0:T(8,128)} %copy.18, f32[128,256]{1,0:T(8,128)S(1)} %bitcast.85, f32[128,256]{1,0:T(8,128)S(1)} %bitcast.86, f32[128,256]{1,0:T(8,128)S(1)} %bitcast.88, f32[128,256]{1,0:T(8,128)S(1)} %convolution_bitcast_fusion.2, f32[1,4096,512]{2,1,0:T(8,128)} %param.11), kind=kOutput, calls=%fused_computation.5 | convolution fusion | flops 6443892736 | bytes 17301504 | tf_op jit(solution)/shard_map/dot_general | solution.py:102
  126.6 5.6 %copy.26 = f32[4096,256]{1,0:T(8,128)} copy(f32[4096,256]{0,1:T(8,128)} %fusion.2) | data formatting | bytes 8388608 | tf_op jit(solution)/shard_map/reshape | solution.py:106
  132.2 2.6 %multiply_convert_fusion = bf16[8,512,256]{2,1,0:T(8,128)(2,1)S(1)} fusion(f32[8,512,256]{2,1,0:T(8,128)} %bitcast.81, f32[8,512]{1,0:T(8,128)S(1)} %fusion.52), kind=kLoop, calls=%fused_computation.10 | loop fusion | flops 2097152 | bytes 6307840 | tf_op jit(solution)/shard_map/convert_element_type | solution.py:106
  134.8 1.4 gather_fusion.1
  136.2 2.0 %copy.21 = bf16[2,512,256]{1,2,0:T(8,128)(2,1)} copy(bf16[2,512,256]{2,1,0:T(8,128)(2,1)} %gather_fusion.1) | data formatting | bytes 1048576 | tf_op jit(solution)/shard_map/jit(_take)/gather | solution.py:109
  138.2 2.0 %broadcast_select_fusion = bf16[2,512,256]{1,2,0:T(8,128)(2,1)} fusion(bf16[2,512,256]{1,2,0:T(8,128)(2,1)} %copy.21, pred[2]{0:T(512)(128)(4,1)S(1)} %compare_and_fusion), kind=kLoop, calls=%fused_computation.39 | loop fusion | flops 262144 | bytes 1048578 | tf_op jit(solution)/shard_map/jit(_take)/select_n | solution.py:109
  140.2 3.8 %collective-permute-start.1 = (bf16[2,512,256]{1,2,0:T(8,128)(2,1)}, bf16[2,512,256]{1,2,0:T(8,128)(2,1)}, u32[]{:S(2)}, u32[]{:S(2)}) collective-permute-start(bf16[2,512,256]{1,2,0:T(8,128)(2,1)} %broadcast_select_fusion), channel_id=1, source_target_pairs={{32,0},{64,32},{96,64},{128,96},{160,128},{192,160},{224,192},{0,2... | collective-permute-start | bytes 1572872 | tf_op jit(solution)/shard_map/ppermute | solution.py:64
  144.0 1.4 gather_fusion
  145.4 6.9 %collective-permute-done.1 = bf16[2,512,256]{1,2,0:T(8,128)(2,1)} collective-permute-done((bf16[2,512,256]{1,2,0:T(8,128)(2,1)}, bf16[2,512,256]{1,2,0:T(8,128)(2,1)}, u32[]{:S(2)}, u32[]{:S(2)}) %collective-permute-start.1) | collective-permute-done | bytes 524320 | tf_op jit(solution)/shard_map/ppermute | solution.py:64
  152.3 2.0 %fusion.16 = f32[32,8,256]{2,1,0:T(8,128)S(1)} fusion(bf16[2,512,256]{1,2,0:T(8,128)(2,1)} %collective-permute-done.1, bf16[1,2,512,512]{3,2,1,0:T(8,128)(2,1)S(1)} %copy-done, bf16[2,512,256]{2,1,0:T(8,128)(2,1)} %gather_fusion, pred[2]{0:T(512)(128)(4,1)S(1)} %compare_and_fusion.1, bf16[2]{0:T(256)(128)(2,1)S(1)} %convert_bitcast_fusion), kind=kOutput, calls=%fused_computation.20 | convolution fusion | flops 403439616 | bytes 2359302 | tf_op jit(solution)/shard_map/tji,tjk->ik/dot_general | solution.py:118
  154.3 17.9 %all_to_all.21 = f32[32,8,256]{2,1,0:T(8,128)S(1)} all-to-all(f32[32,8,256]{2,1,0:T(8,128)S(1)} %fusion.16), channel_id=1, replica_groups=mesh['sym'=8,'row'=32] {'row'}, dimensions={0} | all-to-all | bytes 524288 | tf_op jit(solution)/shard_map/all_to_all | solution.py:43
  172.2 0.6 reduce_sum.19
  (32 shorter events, 1.4 us)
Async XLA Ops:
  0.0 152.3 %copy-start = (bf16[1,2,512,512]{3,2,1,0:T(8,128)(2,1)S(1)}, bf16[1,2,512,512]{3,2,1,0:T(8,128)(2,1)}, u32[]{:S(2)}) copy-start(bf16[1,2,512,512]{3,2,1,0:T(8,128)(2,1)} %param.13) | copy-start | bytes 3145732
  0.0 8.1 %copy-start.1 = (f32[1,4096,512]{2,1,0:T(8,128)S(1)}, f32[1,4096,512]{2,1,0:T(8,128)}, u32[]{:S(2)}) copy-start(f32[1,4096,512]{2,1,0:T(8,128)} %param.11) | copy-start | bytes 25165828
  31.7 43.9 %copy-start.4 = (s32[1,2]{1,0:T(1,128)S(1)}, s32[1,2]{1,0:T(1,128)}, u32[]{:S(2)}) copy-start(s32[1,2]{1,0:T(1,128)} %param.15) | copy-start | bytes 28
  69.2 28.7 %all-to-all-start.1 = ((f32[32,1,7168]{2,1,0:T(1,128)}), f32[32,1,7168]{2,1,0:T(1,128)S(1)}, u32[]{:S(2)}, u32[]{:S(2)}) async-start(f32[32,1,7168]{2,1,0:T(1,128)} %broadcast_in_dim.18), calls=%async_computation.1 | async-start | bytes 1835008 | tf_op jit(solution)/shard_map/all_to_all | solution.py:21
  75.6 8.9 %copy-start.5 = (s32[1,2]{1,0:T(1,128)S(1)}, s32[1,2]{1,0:T(1,128)}, u32[]{:S(2)}) copy-start(s32[1,2]{1,0:T(1,128)} %param.14) | copy-start | bytes 28
  75.6 8.9 %copy-start.3 = (s32[1,8]{1,0:T(1,128)S(1)}, s32[1,8]{1,0:T(1,128)}, u32[]{:S(2)}) copy-start(s32[1,8]{1,0:T(1,128)} %param.17) | copy-start | bytes 100
  75.6 25.6 %copy-start.2 = (f32[1,4,128,128]{3,2,1,0:T(8,128)S(1)}, f32[1,4,128,128]{3,2,1,0:T(8,128)}, u32[]{:S(2)}) copy-start(f32[1,4,128,128]{3,2,1,0:T(8,128)} %param.12) | copy-start | bytes 786436
  75.6 9.0 %collective-permute-start = (s32[2]{0:T(128)S(1)}, s32[2]{0:T(128)S(1)}, u32[]{:S(2)}, u32[]{:S(2)}) collective-permute-start(s32[2]{0:T(128)S(1)} %bitcast.91), channel_id=1, source_target_pairs={{224,0},{0,32},{32,64},{64,96},{96,128},{128,160},{160,192},{192,2... | collective-permute-start | bytes 32 | tf_op jit(solution)/shard_map/ppermute | solution.py:64
  132.2 11.8 %copy-start.6 = (s32[1,2]{1,0:T(1,128)S(1)}, s32[1,2]{1,0:T(1,128)}, u32[]{:S(2)}) copy-start(s32[1,2]{1,0:T(1,128)} %param.16) | copy-start | bytes 28
  140.2 12.1 %collective-permute-start.1 = (bf16[2,512,256]{1,2,0:T(8,128)(2,1)}, bf16[2,512,256]{1,2,0:T(8,128)(2,1)}, u32[]{:S(2)}, u32[]{:S(2)}) collective-permute-start(bf16[2,512,256]{1,2,0:T(8,128)(2,1)} %broadcast_select_fusion), channel_id=1, source_target_pairs={{32,0},{64,32},{96,64},{128,96},{160,128},{192,160},{224,192},{0,2... | collective-permute-start | bytes 1572872 | tf_op jit(solution)/shard_map/ppermute | solution.py:64
where the time goes:
time: 173 us
  matrix products  58.7 us (34%)
  blocking collectives  53.2 us (31%)
  waiting for transfers between devices  20.1 us (12%)
  local copies, waits for them, and re-layouts  19 us (11%)
  starting transfers between devices  13.5 us (8%)
  other arithmetic  8.06 us (5%)
    all_to_all x2, blocking collectives, sum_at_owner(): tiles = lax.all_to_all(split_up(array, dim, count), axis, 0, 0, tiled=True)  53.2 us
    dot_general x4, matrix products, row_inner(): lax.dot_general(first, second, (((0,), (0,)), ((), ())), precision=PRECISE)  31.5 us
    dot_general x1, matrix products, on_device(): jnp.dot(panels, jnp.concatenate(updates, axis=0), precision=PRECISE)  18.1 us
    all_to_all x1, waiting for transfers between devices, from_everyone(): return lax.all_to_all(copies, axis, split_axis=0, concat_axis=0, tiled=True)  13.2 us
    ppermute x2, starting transfers between devices, passed_along(): return lax.ppermute(block, axis, route)  7.08 us
    ppermute x2, waiting for transfers between devices, passed_along(): return lax.ppermute(block, axis, route)  6.88 us
    all_to_all x1, starting transfers between devices, from_everyone(): return lax.all_to_all(copies, axis, split_axis=0, concat_axis=0, tiled=True)  6.37 us
    unnamed x17, local copies, waits for them, and re-layouts  6 us
  transfers between devices with their start and end apart: 3, of which 2 were waited for; matrix products, arithmetic and copies ran while one was open for 4% of the time, Pallas kernels for 0%

commit v1 on v0

v1 whole, which is shorter than its diff:
```python
import jax
import jax.numpy as jnp
from jax import lax
from jax.experimental import pallas as pl
from jax.experimental.pallas import tpu as pltpu
from jax.sharding import PartitionSpec as P

F32 = jnp.float32
BF16 = jnp.bfloat16
F16 = jnp.float16
BLOCK = 512
STEP = 512
HALF = 16
PROJ = 2 * HALF
COUP = 24
SHARE = PROJ + COUP + 8
COUPLING_SCALE = 32.0


def split(x):
    high = x.astype(BF16)
    return high, (x - high.astype(F32)).astype(BF16)


def dot(a, b, dims=((1,), (0,))):
    return lax.dot_general(a, b, (dims, ((), ())), preferred_element_type=F32)


def dot3(a, b, dims=((1,), (0,))):
    (ah, al), (bh, bl) = a, b
    return dot(ah, bh, dims) + (dot(ah, bl, dims) + dot(al, bh, dims))


def gram_kernel(start_ref, panel_ref, out_ref, proj, coup, first):
    step = pl.program_id(0)

    @pl.when(step == 0)
    def _():
        proj[...] = jnp.zeros_like(proj)
        coup[...] = jnp.zeros_like(coup)
        first[...] = jnp.zeros_like(first)

    panels = panel_ref[0]
    width = panels.shape[1] // 4
    turned = split(panels.T)
    late = split(panels[:, 2 * width :])
    second = split(panels[:, width : 2 * width])
    start = split(start_ref[0])

    def rows(pair, begin, end):
        return tuple(p[begin:end] for p in pair)

    proj[...] += dot3(turned, start)
    coup[...] += dot3(rows(turned, 0, 3 * width), late)
    first[...] += dot3(rows(turned, 0, width), second)

    @pl.when(step == pl.num_programs(0) - 1)
    def _():
        inner = proj[...]
        top = jnp.max(jnp.abs(inner), axis=(0, 1), keepdims=True)
        exponent = jnp.ceil(jnp.log2(jnp.maximum(top, 1e-30))) - 14.0
        inner = inner * jnp.exp2(-exponent)
        count = out_ref.shape[0]
        out_ref[:, :HALF, :] = inner[:, :128].reshape(count, HALF, 128)
        out_ref[:, HALF:PROJ, :] = inner[:, 128:].reshape(count, HALF, 128)
        lines = jnp.concatenate(
            [
                coup[: 2 * width, :width],
                first[...],
                coup[:, width:],
            ],
            axis=0,
        )
        lines = lines * COUPLING_SCALE
        out_ref[:, PROJ : PROJ + COUP, :] = lines.reshape(count, COUP, 128)
        out_ref[:, PROJ + COUP :, :] = jnp.broadcast_to(
            exponent.reshape(1, 1, 1), (count, 8, 128)
        )


def local_grams(start, panels, count):
    rows, eigen = start.shape[1:]
    columns = panels.shape[2]
    return pl.pallas_call(
        gram_kernel,
        out_shape=jax.ShapeDtypeStruct((count, SHARE, 128), F32),
        grid=(rows // STEP,),
        in_specs=[
            pl.BlockSpec((1, STEP, eigen), lambda i: (0, i, 0)),
            pl.BlockSpec((1, STEP, columns), lambda i: (0, i, 0)),
        ],
        out_specs=pl.BlockSpec((count, SHARE, 128), lambda i: (0, 0, 0)),
        scratch_shapes=[
            pltpu.VMEM((columns, eigen), F32),
            pltpu.VMEM((3 * columns // 4, columns // 2), F32),
            pltpu.VMEM((columns // 4, columns // 4), F32),
        ],
        compiler_params=pltpu.CompilerParams(vmem_limit_bytes=40 << 20),
        cost_estimate=pl.CostEstimate(
            flops=6 * rows * columns * (eigen + columns // 2),
            bytes_accessed=4 * rows * (eigen + columns),
            transcendentals=0,
        ),
        name="grams",
    )(start, panels)


def updated_block(start_ref, panel_ref, upper, lower, limit):
    high, low = split(panel_ref[0])
    back = start_ref[0] - (
        dot(high, upper[...]) + (dot(high, lower[...]) + dot(low, upper[...]))
    )
    line = lax.broadcasted_iota(jnp.int32, back.shape, 0)
    return jnp.where(line < limit, back, 0.0).astype(BF16)


def solve_kernel(
    want_ref, limit_ref, sums_ref, factor_ref, start_ref, panel_ref, out_ref, upper, lower
):
    turn = pl.program_id(0)
    count = sums_ref.shape[0]
    width = factor_ref.shape[2]

    @pl.when(turn == 0)
    def _():
        scale = jnp.exp2(sums_ref[:, PROJ + COUP : PROJ + COUP + 1, :])
        size = (count * HALF, 128)
        inner = jnp.concatenate(
            [
                (sums_ref[:, :HALF, :] * scale).reshape(size),
                (sums_ref[:, HALF:PROJ, :] * scale).reshape(size),
            ],
            axis=1,
        )
        links = split(sums_ref[:, PROJ : PROJ + COUP, :].reshape(count * COUP, 128))

        def link(begin, end):
            return tuple(p[begin * width : end * width] for p in links)

        current = [inner[k * width : (k + 1) * width] for k in range(4)]
        parts = [None] * 4
        reach = {3: (3, 6), 2: (0, 2), 1: (2, 3)}
        for level in (3, 2, 1, 0):
            update = split(dot3(split(factor_ref[0, level]), split(current[level])))
            parts[level] = update
            if level:
                moved = dot3(link(*reach[level]), update)
                for k in range(level):
                    current[k] = current[k] - moved[k * width : (k + 1) * width]
        upper[...] = jnp.concatenate([p[0] for p in parts], axis=0)
        lower[...] = jnp.concatenate([p[1] for p in parts], axis=0)

    out_ref[0] = updated_block(
        start_ref, panel_ref, upper, lower, limit_ref[want_ref[turn]]
    )


def left_kernel(
    left_ref, occupied_ref, limit_ref, upper, lower, start_ref, panel_ref, out_ref
):
    turn = pl.program_id(0)
    limit = limit_ref[left_ref[turn]] * occupied_ref[turn]
    out_ref[0] = updated_block(start_ref, panel_ref, upper, lower, limit)


def blocks_of(width):
    return pl.BlockSpec((1, BLOCK, width), lambda t, which, *_: (0, which[t], 0))


def whole(shape):
    return pl.BlockSpec(shape, lambda t, *_: (0,) * len(shape))


def solve_and_update(want, limits, sums, factors, start, panels):
    count = want.shape[0]
    eigen, columns = start.shape[2], panels.shape[2]
    coefficients = jax.ShapeDtypeStruct((columns, eigen), BF16)
    return pl.pallas_call(
        solve_kernel,
        out_shape=(
            jax.ShapeDtypeStruct((count, BLOCK, eigen), BF16),
            coefficients,
            coefficients,
        ),
        grid_spec=pltpu.PrefetchScalarGridSpec(
            num_scalar_prefetch=2,
            grid=(count,),
            in_specs=[
                whole(sums.shape),
                whole(factors.shape),
                blocks_of(eigen),
                blocks_of(columns),
            ],
            out_specs=(
                pl.BlockSpec((1, BLOCK, eigen), lambda t, *_: (t, 0, 0)),
                whole((columns, eigen)),
                whole((columns, eigen)),
            ),
        ),
        compiler_params=pltpu.CompilerParams(vmem_limit_bytes=32 << 20),
        cost_estimate=pl.CostEstimate(
            flops=6 * count * BLOCK * columns * eigen,
            bytes_accessed=4 * count * BLOCK * (columns + eigen),
            transcendentals=0,
        ),
        name="solve",
    )(want, limits, sums, factors, start, panels)


def left_blocks(left, occupied, limits, upper, lower, start, panels):
    count = left.shape[0]
    eigen, columns = start.shape[2], panels.shape[2]
    return pl.pallas_call(
        left_kernel,
        out_shape=jax.ShapeDtypeStruct((count, BLOCK, eigen), BF16),
        grid_spec=pltpu.PrefetchScalarGridSpec(
            num_scalar_prefetch=3,
            grid=(count,),
            in_specs=[
                whole((columns, eigen)),
                whole((columns, eigen)),
                blocks_of(eigen),
                blocks_of(columns),
            ],
            out_specs=pl.BlockSpec((1, BLOCK, eigen), lambda t, *_: (t, 0, 0)),
        ),
        compiler_params=pltpu.CompilerParams(vmem_limit_bytes=32 << 20),
        cost_estimate=pl.CostEstimate(
            flops=6 * count * BLOCK * columns * eigen,
            bytes_accessed=4 * count * BLOCK * (columns + eigen),
            transcendentals=0,
        ),
        name="left",
    )(left, occupied, limits, upper, lower, start, panels)


def dipole_kernel(tile_ref, right_ref, left_ref, out_ref):
    total = None
    for t in range(tile_ref.shape[1]):
        product = dot(tile_ref[0, t], right_ref[t]).astype(BF16)
        term = dot(left_ref[t], product, ((0,), (0,)))
        total = term if total is None else total + term
    out_ref[...] = total.astype(BF16)


def tile_products(tiles, right, left):
    eigen = right.shape[2]
    return pl.pallas_call(
        dipole_kernel,
        out_shape=jax.ShapeDtypeStruct((eigen, eigen), BF16),
        compiler_params=pltpu.CompilerParams(vmem_limit_bytes=32 << 20),
        name="dipole",
    )(tiles, right, left)


def passed_along(block, axis, distance):
    devices = range(lax.axis_size(axis))
    route = [((i - distance) % len(devices), i) for i in devices]
    return lax.ppermute(block, axis, route)


def exchanged(shares):
    return lax.all_to_all(shares, "row", 0, 0, tiled=True)


def on_device(
    vectors, reflectors, factors, tiles, tile_left, tile_right, tile_occupied_mask, channels
):
    count = lax.axis_size("row")
    vectors = pltpu.with_memory_space_constraint(vectors, pltpu.HBM)
    reflectors = pltpu.with_memory_space_constraint(reflectors, pltpu.HBM)
    want = passed_along(tile_right[0], "sym", 1)
    shares = local_grams(vectors, reflectors, count)
    terms = exchanged(shares.astype(F16)).astype(F32)
    exponents = terms[:, PROJ + COUP :]
    proj = jnp.sum(terms[:, :PROJ] * jnp.exp2(exponents[:, :1]), axis=0)
    coup = jnp.sum(terms[:, PROJ : PROJ + COUP], axis=0) * (1.0 / COUPLING_SCALE)
    exponent = jnp.max(exponents, axis=0) + 5.0
    owned = jnp.concatenate([proj * jnp.exp2(-exponent[:1]), coup, exponent], axis=0)
    copies = jnp.broadcast_to(owned.astype(F16), (count, SHARE, 128))
    sums = exchanged(copies).astype(F32)
    packed, upper, lower = solve_and_update(
        want, channels[0], sums, factors, vectors, reflectors
    )
    right = passed_along(packed, "sym", -1)
    left = left_blocks(
        tile_left[0], tile_occupied_mask[0], channels[0], upper, lower, vectors, reflectors
    )
    partial = tile_products(tiles, right, left)
    eigen = partial.shape[1]
    owned = exchanged(partial.reshape(count, eigen // count, eigen))
    return jnp.sum(owned.astype(F32), axis=0)[None]


def solution(mesh):
    return jax.shard_map(
        on_device,
        mesh=mesh,
        in_specs=(
            P("sym", "row", None),
            P("sym", "row", None),
            P("sym", None, None, None),
            P("sym", "row", None, None),
            P("sym", "row"),
            P("sym", "row"),
            P("sym", "row"),
            P("sym", "row"),
        ),
        out_specs=P("sym", "row", None),
        check_vma=False,
    )
```

time: 173 us -> 94.3 us (0.55)
  matrix products: 58.7 us -> 0 us
  Pallas kernels: 0 us -> 20.6 us
  local copies, waits for them, and re-layouts: 19 us -> 0.94 us
  blocking collectives: 53.2 us -> 42.1 us
  other arithmetic: 8.06 us -> 1.1 us
  waiting for transfers between devices: 20.1 us -> 16.8 us
    dot_general x16 -> x0, matrix products: 58.7 us -> none  [the longest x4 31.5 us: row_inner(): lax.dot_general(first, second, (((0,), (0,)), ((), ())), precision=PRECISE)]
    pallas_call x0 -> x4, Pallas kernels: none -> 20.6 us  [the longest x1 11.4 us: local_grams(): pl.pallas_call(gram_kernel, out_shape=jax.ShapeDtypeStruct((count, SHARE,...]
    all_to_all x2, blocking collectives: 53.2 us -> 42.1 us  [exchanged(): return lax.all_to_all(shares, 'row', 0, 0, tiled=True)]
    unnamed x17 -> x12, local copies, waits for them, and re-layouts: 6 us -> 0.03 us
    reshape x3 -> x0, local copies, waits for them, and re-layouts: 5.67 us -> none  [the longest x1 5.6 us: on_device(): result.reshape(-1, BLOCK, eigen_count) * keeper[:, :, None]]
    gather x3 -> x0, local copies, waits for them, and re-layouts: 4.8 us -> none  [the longest x2 3.42 us: on_device(): packed = jnp.take(masked, wanted, axis=0)]
    convert_element_type x3, other arithmetic: 2.68 us -> 0.25 us  [the longest x2 0.17 us: on_device(): terms = exchanged(shares.astype(F16)).astype(F32)]
    all_to_all x1 -> x0, other arithmetic: 2.17 us -> none  [from_everyone(): return lax.all_to_all(copies, axis, split_axis=0, concat_axis=0, tiled=True)]
  transfers between devices with their start and end apart: 3 -> 3, of which waited for: 2 -> 2; matrix products, arithmetic and copies ran while one was open for 4% -> 0% of each run, Pallas kernels for 0% -> 3%
where the time goes in v1:
time: 94.3 us; the launch traced here: 93.8 us
  blocking collectives  42.1 us (45%)
  Pallas kernels  20.6 us (22%)
  waiting for transfers between devices  16.8 us (18%)
  starting transfers between devices  12.1 us (13%)
  other arithmetic  1.1 us (1%)
    all_to_all x2, blocking collectives, exchanged(): return lax.all_to_all(shares, 'row', 0, 0, tiled=True)  42.1 us
    all_to_all x1, waiting for transfers between devices, exchanged(): return lax.all_to_all(shares, 'row', 0, 0, tiled=True)  12.1 us
    pallas_call x1, Pallas kernels, local_grams(): pl.pallas_call(gram_kernel, out_shape=jax.ShapeDtypeStruct((count, SHARE,...  11.4 us
    ppermute x2, starting transfers between devices, passed_along(): return lax.ppermute(block, axis, route)  6.75 us
    all_to_all x1, starting transfers between devices, exchanged(): return lax.all_to_all(shares, 'row', 0, 0, tiled=True)  5.36 us
    pallas_call x1, Pallas kernels, solve_and_update(): pl.pallas_call(solve_kernel, out_shape=(jax.ShapeDtypeStruct((count, BLOC...  5.08 us
    ppermute x2, waiting for transfers between devices, passed_along(): return lax.ppermute(block, axis, route)  4.73 us
    pallas_call x1, Pallas kernels, left_blocks(): pl.pallas_call(left_kernel, out_shape=jax.ShapeDtypeStruct((count, BLOCK,...  3.24 us
  transfers between devices with their start and end apart: 3, of which 2 were waited for; matrix products, arithmetic and copies ran while one was open for 0% of the time, Pallas kernels for 3%

profile of v1, /device:TPU:1, one launch (start us, length us, event | category | flops | bytes accessed | tf_op | source)
XLA Modules:
  0.0 93.8 jit_solution(13883049472864890086)
XLA Ops:
  0.0 0.0 copy-start.5
  0.0 11.4 %grams.1 = f32[32,64,128]{2,1,0:T(8,128)S(1)} custom-call(f32[1,4096,256]{2,1,0:T(8,128)} %start_ref.5, f32[1,4096,512]{2,1,0:T(8,128)} %panel_ref.5), custom_call_target="tpu_custom_call" | custom-call | flops 6442450944 | bytes 12582912 | tf_op jit(solution)/shard_map/grams/pallas_call | solution.py:84
  11.4 0.0 copy-start.1
  11.4 0.0 copy-start.2
  11.4 0.1 convert_element_type.13
  11.5 28.1 %all_to_all.15 = f16[32,64,128]{2,1,0:T(8,128)(2,1)S(1)} all-to-all(f16[32,64,128]{2,1,0:T(8,128)(2,1)S(1)} %convert_element_type.13), channel_id=1, replica_groups=mesh['sym'=8,'row'=32] {'row'}, dimensions={0} | all-to-all | bytes 1048576 | tf_op jit(solution)/shard_map/all_to_all | solution.py:263
  39.6 0.1 convert_element_type.14
  39.9 0.1 fusion
  40.0 0.9 broadcast_in_dim.6
  40.9 0.0 copy-start.3
  40.9 0.0 copy-start.4
  40.9 5.4 %all-to-all-start.1 = ((f16[32,64,128]{2,1,0:T(8,128)(2,1)}), f16[32,64,128]{2,1,0:T(8,128)(2,1)S(1)}, u32[]{:S(2)}, u32[]{:S(2)}) async-start(f16[32,64,128]{2,1,0:T(8,128)(2,1)} %broadcast_in_dim.6), calls=%async_computation.1 | async-start | bytes 1048576 | tf_op jit(solution)/shard_map/all_to_all | solution.py:263
  46.3 0.0 copy-done.5
  46.3 3.0 %collective-permute-start = (s32[2]{0:T(128)S(1)}, s32[2]{0:T(128)S(1)}, u32[]{:S(2)}, u32[]{:S(2)}) collective-permute-start(s32[2]{0:T(128)S(1)} %bitcast.15), channel_id=1, source_target_pairs={{224,0},{0,32},{32,64},{64,96},{96,128},{128,160},{160,192},{192,2... | collective-permute-start | bytes 32 | tf_op jit(solution)/shard_map/ppermute | solution.py:259
  49.2 12.1 %all-to-all-done.1 = f16[32,64,128]{2,1,0:T(8,128)(2,1)S(1)} async-done(((f16[32,64,128]{2,1,0:T(8,128)(2,1)}), f16[32,64,128]{2,1,0:T(8,128)(2,1)S(1)}, u32[]{:S(2)}, u32[]{:S(2)}) %all-to-all-start.1) | async-done | bytes 524320 | tf_op jit(solution)/shard_map/all_to_all | solution.py:263
  61.3 0.1 convert_element_type.15.sums_ref
  61.4 0.0 collective-permute-done.want_ref
  61.4 0.0 copy-done.1
  61.4 0.0 copy-done.2
  61.4 5.1 %solve.1 = (bf16[2,512,256]{2,1,0:T(8,128)(2,1)S(1)}, bf16[512,256]{1,0:T(8,128)(2,1)S(1)}, bf16[512,256]{1,0:T(8,128)(2,1)S(1)}) custom-call(s32[2]{0:T(128)S(1)} %collective-permute-done.want_ref, s32[8]{0:T(128)S(1)} %bitcast.10, f32[32,64,128]{2,1,0:T(8,128)S(1)} %convert_element_type.15.sums_ref, f32[1,4,128,128]{3,2,1,0:T(8,128)S(1)} %copy-done.1, ...), custom_call_target="tpu_custom_call" | custom-call | flops 805306368 | bytes 3145728 | tf_op jit(solution)/shard_map/solve/pallas_call | solution.py:178
  66.5 0.0 copy-start
  66.5 3.8 %collective-permute-start.1 = (bf16[2,512,256]{2,1,0:T(8,128)(2,1)S(1)}, bf16[2,512,256]{2,1,0:T(8,128)(2,1)S(1)}, u32[]{:S(2)}, u32[]{:S(2)}) collective-permute-start(bf16[2,512,256]{2,1,0:T(8,128)(2,1)S(1)} %get-tuple-element.8), channel_id=1, source_target_pairs={{32,0},{64,32},{96,64},{128,96},{160,128},{192,160},{224,192},{0,2... | collective-permute-start | bytes 1572872 | tf_op jit(solution)/shard_map/ppermute | solution.py:259
  70.3 0.0 copy-done.3
  70.3 0.0 copy-done.4
  70.3 3.2 %left.1.left_ref = bf16[2,512,256]{2,1,0:T(8,128)(2,1)S(1)} custom-call(s32[2]{0:T(128)S(1)} %bitcast.12, s32[2]{0:T(128)S(1)} %bitcast.13, s32[8]{0:T(128)S(1)} %bitcast.11, bf16[512,256]{1,0:T(8,128)(2,1)S(1)} %get-tuple-element.9.upper, bf16[512,256]{1,0:T(8,128)(2,1)S(1)} %get-tuple-element.10.lower, f32[1,4096,256]{2,1,0:T(8,128)} %start_ref.5, ...), custom_call_target="tpu_custom_call" | custom-call | flops 805306368 | bytes 3145728 | tf_op jit(solution)/shard_map/left/pallas_call | solution.py:213
  73.5 4.7 %collective-permute-done.1.right_ref = bf16[2,512,256]{2,1,0:T(8,128)(2,1)S(1)} collective-permute-done((bf16[2,512,256]{2,1,0:T(8,128)(2,1)S(1)}, bf16[2,512,256]{2,1,0:T(8,128)(2,1)S(1)}, u32[]{:S(2)}, u32[]{:S(2)}) %collective-permute-start.1) | collective-permute-done | bytes 524320 | tf_op jit(solution)/shard_map/ppermute | solution.py:259
  78.3 0.0 copy-done
  78.3 0.9 dipole.1
  79.2 14.0 %all_to_all.16 = bf16[32,8,256]{2,1,0:T(8,128)(2,1)S(1)} all-to-all(bf16[32,8,256]{2,1,0:T(8,128)(2,1)S(1)} %bitcast.9), channel_id=1, replica_groups=mesh['sym'=8,'row'=32] {'row'}, dimensions={0} | all-to-all | bytes 262144 | tf_op jit(solution)/shard_map/all_to_all | solution.py:263
  93.2 0.6 convert_reduce_fusion
  (8 shorter events, 0.1 us)
Async XLA Ops:
  0.0 46.3 %copy-start.5 = (s32[1,2]{1,0:T(1,128)S(1)}, s32[1,2]{1,0:T(1,128)}, u32[]{:S(2)}) copy-start(s32[1,2]{1,0:T(1,128)} %param.13) | copy-start | bytes 28
  11.4 50.0 %copy-start.1 = (f32[1,4,128,128]{3,2,1,0:T(8,128)S(1)}, f32[1,4,128,128]{3,2,1,0:T(8,128)}, u32[]{:S(2)}) copy-start(f32[1,4,128,128]{3,2,1,0:T(8,128)} %factor_ref.1) | copy-start | bytes 786436
  11.4 50.0 %copy-start.2 = (s32[1,8]{1,0:T(1,128)S(1)}, s32[1,8]{1,0:T(1,128)}, u32[]{:S(2)}) copy-start(s32[1,8]{1,0:T(1,128)} %param.15) | copy-start | bytes 100
  40.9 29.4 %copy-start.3 = (s32[1,2]{1,0:T(1,128)S(1)}, s32[1,2]{1,0:T(1,128)}, u32[]{:S(2)}) copy-start(s32[1,2]{1,0:T(1,128)} %param.12) | copy-start | bytes 28
  40.9 29.4 %copy-start.4 = (s32[1,2]{1,0:T(1,128)S(1)}, s32[1,2]{1,0:T(1,128)}, u32[]{:S(2)}) copy-start(s32[1,2]{1,0:T(1,128)} %param.14) | copy-start | bytes 28
  40.9 20.4 %all-to-all-start.1 = ((f16[32,64,128]{2,1,0:T(8,128)(2,1)}), f16[32,64,128]{2,1,0:T(8,128)(2,1)S(1)}, u32[]{:S(2)}, u32[]{:S(2)}) async-start(f16[32,64,128]{2,1,0:T(8,128)(2,1)} %broadcast_in_dim.6), calls=%async_computation.1 | async-start | bytes 1048576 | tf_op jit(solution)/shard_map/all_to_all | solution.py:263
  46.3 15.1 %collective-permute-start = (s32[2]{0:T(128)S(1)}, s32[2]{0:T(128)S(1)}, u32[]{:S(2)}, u32[]{:S(2)}) collective-permute-start(s32[2]{0:T(128)S(1)} %bitcast.15), channel_id=1, source_target_pairs={{224,0},{0,32},{32,64},{64,96},{96,128},{128,160},{160,192},{192,2... | collective-permute-start | bytes 32 | tf_op jit(solution)/shard_map/ppermute | solution.py:259
  66.5 11.8 %copy-start = (bf16[1,2,512,512]{3,2,1,0:T(8,128)(2,1)S(1)}, bf16[1,2,512,512]{3,2,1,0:T(8,128)(2,1)}, u32[]{:S(2)}) copy-start(bf16[1,2,512,512]{3,2,1,0:T(8,128)(2,1)} %tile_ref.1) | copy-start | bytes 3145732
  66.5 11.8 %collective-permute-start.1 = (bf16[2,512,256]{2,1,0:T(8,128)(2,1)S(1)}, bf16[2,512,256]{2,1,0:T(8,128)(2,1)S(1)}, u32[]{:S(2)}, u32[]{:S(2)}) collective-permute-start(bf16[2,512,256]{2,1,0:T(8,128)(2,1)S(1)} %get-tuple-element.8), channel_id=1, source_target_pairs={{32,0},{64,32},{96,64},{128,96},{160,128},{192,160},{224,192},{0,2... | collective-permute-start | bytes 1572872 | tf_op jit(solution)/shard_map/ppermute | solution.py:259

commit v2 on v1

--- a/solution.py
+++ b/solution.py
@@ -9,7 +9,7 @@
 BF16 = jnp.bfloat16
 F16 = jnp.float16
 BLOCK = 512
-STEP = 512
+STEP = 1024
 HALF = 16
 PROJ = 2 * HALF
 COUP = 24
@@ -17,6 +17,9 @@
 COUPLING_SCALE = 32.0
 
 
+ROWS = ((0,), (0,))
+
+
 def split(x):
     high = x.astype(BF16)
     return high, (x - high.astype(F32)).astype(BF16)
@@ -40,19 +43,16 @@
         coup[...] = jnp.zeros_like(coup)
         first[...] = jnp.zeros_like(first)
 
-    panels = panel_ref[0]
-    width = panels.shape[1] // 4
-    turned = split(panels.T)
-    late = split(panels[:, 2 * width :])
-    second = split(panels[:, width : 2 * width])
+    panels = split(panel_ref[0])
     start = split(start_ref[0])
-
-    def rows(pair, begin, end):
-        return tuple(p[begin:end] for p in pair)
-
-    proj[...] += dot3(turned, start)
-    coup[...] += dot3(rows(turned, 0, 3 * width), late)
-    first[...] += dot3(rows(turned, 0, width), second)
+    width = panel_ref.shape[2] // 4
+
+    def columns(begin, end):
+        return tuple(p[:, begin * width : end * width] for p in panels)
+
+    proj[...] += dot3(panels, start, ROWS)
+    coup[...] += dot3(columns(0, 3), columns(2, 4), ROWS)
+    first[...] += dot3(columns(0, 1), columns(1, 2), ROWS)
 
     @pl.when(step == pl.num_programs(0) - 1)
     def _():
@@ -105,70 +105,103 @@
     )(start, panels)
 
 
-def updated_block(start_ref, panel_ref, upper, lower, limit):
-    high, low = split(panel_ref[0])
-    back = start_ref[0] - (
-        dot(high, upper[...]) + (dot(high, lower[...]) + dot(low, upper[...]))
-    )
+def updated_block(start, panels, upper, lower, limit):
+    high, low = split(panels)
+    back = start - (dot(high, upper) + (dot(high, lower) + dot(low, upper)))
     line = lax.broadcasted_iota(jnp.int32, back.shape, 0)
     return jnp.where(line < limit, back, 0.0).astype(BF16)
 
 
 def solve_kernel(
-    want_ref, limit_ref, sums_ref, factor_ref, start_ref, panel_ref, out_ref, upper, lower
+    want_ref,
+    limit_ref,
+    sums_ref,
+    factor_ref,
+    start_ref,
+    panel_ref,
+    out_ref,
+    upper,
+    lower,
+    starts,
+    panels,
+    arrived,
 ):
-    turn = pl.program_id(0)
+    copies = []
+    for t in range(out_ref.shape[0]):
+        rows = pl.ds(pl.multiple_of(want_ref[t] * BLOCK, BLOCK), BLOCK)
+        for source, target, kind in ((panel_ref, panels, 0), (start_ref, starts, 1)):
+            copy = pltpu.make_async_copy(
+                source.at[0, rows], target.at[t], arrived.at[kind, t]
+            )
+            copy.start()
+            copies.append(copy)
     count = sums_ref.shape[0]
     width = factor_ref.shape[2]
-
-    @pl.when(turn == 0)
-    def _():
-        scale = jnp.exp2(sums_ref[:, PROJ + COUP : PROJ + COUP + 1, :])
-        size = (count * HALF, 128)
-        inner = jnp.concatenate(
+    scale = jnp.exp2(sums_ref[:, PROJ + COUP : PROJ + COUP + 1, :])
+    size = (count * HALF, 128)
+    inner = split(
+        jnp.concatenate(
             [
                 (sums_ref[:, :HALF, :] * scale).reshape(size),
                 (sums_ref[:, HALF:PROJ, :] * scale).reshape(size),
             ],
             axis=1,
         )
-        links = split(sums_ref[:, PROJ : PROJ + COUP, :].reshape(count * COUP, 128))
-
-        def link(begin, end):
-            return tuple(p[begin * width : end * width] for p in links)
-
-        current = [inner[k * width : (k + 1) * width] for k in range(4)]
-        parts = [None] * 4
-        reach = {3: (3, 6), 2: (0, 2), 1: (2, 3)}
-        for level in (3, 2, 1, 0):
-            update = split(dot3(split(factor_ref[0, level]), split(current[level])))
-            parts[level] = update
-            if level:
-                moved = dot3(link(*reach[level]), update)
-                for k in range(level):
-                    current[k] = current[k] - moved[k * width : (k + 1) * width]
-        upper[...] = jnp.concatenate([p[0] for p in parts], axis=0)
-        lower[...] = jnp.concatenate([p[1] for p in parts], axis=0)
-
-    out_ref[0] = updated_block(
-        start_ref, panel_ref, upper, lower, limit_ref[want_ref[turn]]
-    )
+    )
+    links = split(sums_ref[:, PROJ : PROJ + COUP, :].reshape(count * COUP, 128))
+
+    def part(pair, k):
+        return tuple(p[k * width : (k + 1) * width] for p in pair)
+
+    factors = [split(factor_ref[0, level]) for level in range(4)]
+    current = [dot3(factors[level], part(inner, level)) for level in range(4)]
+    places = {3: ((0, 3), (1, 4), (2, 5)), 2: ((0, 0), (1, 1)), 1: ((0, 2),)}
+    chained = {}
+    for later, pairs in places.items():
+        chained[later] = split(
+            jnp.concatenate([dot3(factors[k], part(links, at)) for k, at in pairs], axis=0)
+        )
+    parts = [None] * 4
+    for level in (3, 2, 1, 0):
+        parts[level] = split(current[level])
+        if level:
+            moved = dot3(chained[level], parts[level])
+            for k in range(level):
+                current[k] = current[k] - moved[k * width : (k + 1) * width]
+    upper[...] = jnp.concatenate([p[0] for p in parts], axis=0)
+    lower[...] = jnp.concatenate([p[1] for p in parts], axis=0)
+    for t in range(out_ref.shape[0]):
+        copies[2 * t].wait()
+        copies[2 * t + 1].wait()
+        out_ref[t] = updated_block(
+            starts[t], panels[t], upper[...], lower[...], limit_ref[want_ref[t]]
+        )
 
 
 def left_kernel(
     left_ref, occupied_ref, limit_ref, upper, lower, start_ref, panel_ref, out_ref
 ):
     turn = pl.program_id(0)
-    limit = limit_ref[left_ref[turn]] * occupied_ref[turn]
-    out_ref[0] = updated_block(start_ref, panel_ref, upper, lower, limit)
-
-
-def blocks_of(width):
-    return pl.BlockSpec((1, BLOCK, width), lambda t, which, *_: (0, which[t], 0))
-
-
-def whole(shape):
-    return pl.BlockSpec(shape, lambda t, *_: (0,) * len(shape))
+    out_ref[0] = updated_block(
+        start_ref[0],
+        panel_ref[0],
+        upper[...],
+        lower[...],
+        limit_ref[left_ref[turn]] * occupied_ref[turn],
+    )
+
+
+SCALARS = pl.BlockSpec(memory_space=pltpu.SMEM)
+ARRAY = pl.BlockSpec(memory_space=pltpu.VMEM)
+FAR = pl.BlockSpec(memory_space=pltpu.HBM)
+
+
+def update_cost(blocks, columns, eigen):
+    return pl.CostEstimate(
+        flops=6 * blocks * BLOCK * columns * eigen,
+        bytes_accessed=4 * blocks * BLOCK * (columns + eigen),
+        transcendentals=0,
+    )
 
 
 def solve_and_update(want, limits, sums, factors, start, panels):
@@ -182,27 +215,15 @@
             coefficients,
             coefficients,
         ),
-        grid_spec=pltpu.PrefetchScalarGridSpec(
-            num_scalar_prefetch=2,
-            grid=(count,),
-            in_specs=[
-                whole(sums.shape),
-                whole(factors.shape),
-                blocks_of(eigen),
-                blocks_of(columns),
-            ],
-            out_specs=(
-                pl.BlockSpec((1, BLOCK, eigen), lambda t, *_: (t, 0, 0)),
-                whole((columns, eigen)),
-                whole((columns, eigen)),
-            ),
-        ),
-        compiler_params=pltpu.CompilerParams(vmem_limit_bytes=32 << 20),
-        cost_estimate=pl.CostEstimate(
-            flops=6 * count * BLOCK * columns * eigen,
-            bytes_accessed=4 * count * BLOCK * (columns + eigen),
-            transcendentals=0,
-        ),
+        in_specs=[SCALARS, SCALARS, ARRAY, ARRAY, FAR, FAR],
+        out_specs=(ARRAY,) * 3,
+        scratch_shapes=[
+            pltpu.VMEM((count, BLOCK, eigen), F32),
+            pltpu.VMEM((count, BLOCK, columns), F32),
+            pltpu.SemaphoreType.DMA((2, count)),
+        ],
+        compiler_params=pltpu.CompilerParams(vmem_limit_bytes=16 << 20),
+        cost_estimate=update_cost(count, columns, eigen),
         name="solve",
     )(want, limits, sums, factors, start, panels)
 
@@ -210,6 +231,13 @@
 def left_blocks(left, occupied, limits, upper, lower, start, panels):
     count = left.shape[0]
     eigen, columns = start.shape[2], panels.shape[2]
+
+    def named(width):
+        return pl.BlockSpec((1, BLOCK, width), lambda t, which, *_: (0, which[t], 0))
+
+    def whole(shape):
+        return pl.BlockSpec(shape, lambda t, *_: (0, 0))
+
     return pl.pallas_call(
         left_kernel,
         out_shape=jax.ShapeDtypeStruct((count, BLOCK, eigen), BF16),
@@ -219,17 +247,13 @@
             in_specs=[
                 whole((columns, eigen)),
                 whole((columns, eigen)),
-                blocks_of(eigen),
-                blocks_of(columns),
+                named(eigen),
+                named(columns),
             ],
             out_specs=pl.BlockSpec((1, BLOCK, eigen), lambda t, *_: (t, 0, 0)),
         ),
-        compiler_params=pltpu.CompilerParams(vmem_limit_bytes=32 << 20),
-        cost_estimate=pl.CostEstimate(
-            flops=6 * count * BLOCK * columns * eigen,
-            bytes_accessed=4 * count * BLOCK * (columns + eigen),
-            transcendentals=0,
-        ),
+        compiler_params=pltpu.CompilerParams(vmem_limit_bytes=16 << 20),
+        cost_estimate=update_cost(count, columns, eigen),
         name="left",
     )(left, occupied, limits, upper, lower, start, panels)
 
@@ -248,7 +272,7 @@
     return pl.pallas_call(
         dipole_kernel,
         out_shape=jax.ShapeDtypeStruct((eigen, eigen), BF16),
-        compiler_params=pltpu.CompilerParams(vmem_limit_bytes=32 << 20),
+        compiler_params=pltpu.CompilerParams(vmem_limit_bytes=8 << 20),
         name="dipole",
     )(tiles, right, left)
 
@@ -270,8 +294,9 @@
     vectors = pltpu.with_memory_space_constraint(vectors, pltpu.HBM)
     reflectors = pltpu.with_memory_space_constraint(reflectors, pltpu.HBM)
     want = passed_along(tile_right[0], "sym", 1)
-    shares = local_grams(vectors, reflectors, count)
-    terms = exchanged(shares.astype(F16)).astype(F32)
+    shares = local_grams(vectors, reflectors, count).astype(F16)
+    want, shares = lax.optimization_barrier((want, shares))
+    terms = exchanged(shares).astype(F32)
     exponents = terms[:, PROJ + COUP :]
     proj = jnp.sum(terms[:, :PROJ] * jnp.exp2(exponents[:, :1]), axis=0)
     coup = jnp.sum(terms[:, PROJ : PROJ + COUP], axis=0) * (1.0 / COUPLING_SCALE)

time: 94.3 us -> 93.4 us (level)
  blocking collectives: 42.1 us -> 64.1 us
  waiting for transfers between devices: 16.8 us -> 4.75 us
  starting transfers between devices: 12.1 us -> 4.57 us
  Pallas kernels: 20.6 us -> 18.3 us
    all_to_all x2 -> x3, blocking collectives: 42.1 us -> 64.1 us  [exchanged(): return lax.all_to_all(shares, 'row', 0, 0, tiled=True)]
    all_to_all x1 -> x0, waiting for transfers between devices: 12.1 us -> none  [exchanged(): return lax.all_to_all(shares, 'row', 0, 0, tiled=True)]
    all_to_all x1 -> x0, starting transfers between devices: 5.36 us -> none  [exchanged(): return lax.all_to_all(shares, 'row', 0, 0, tiled=True)]
    ppermute x2, starting transfers between devices: 6.75 us -> 4.57 us  [passed_along(): return lax.ppermute(block, axis, route)]
    pallas_call x1, Pallas kernels: 11.4 us -> 9.7 us  [local_grams(): pl.pallas_call(gram_kernel, out_shape=jax.ShapeDtypeStruct((count, SHARE,...]
  transfers between devices with their start and end apart: 3 -> 2, of which waited for: 2 -> 1; matrix products, arithmetic and copies ran while one was open for 0% -> 0% of each run, Pallas kernels for 3% -> 14%
where the time goes in v2:
time: 93.4 us; the launch traced here: 93.2 us
  blocking collectives  64.1 us (69%)
  Pallas kernels  18.3 us (20%)
  waiting for transfers between devices  4.75 us (5%)
  starting transfers between devices  4.57 us (5%)
  other arithmetic  1.1 us (1%)
    all_to_all x3, blocking collectives, exchanged(): return lax.all_to_all(shares, 'row', 0, 0, tiled=True)  64.1 us
    pallas_call x1, Pallas kernels, local_grams(): pl.pallas_call(gram_kernel, out_shape=jax.ShapeDtypeStruct((count, SHARE,...  9.7 us
    ppermute x2, waiting for transfers between devices, passed_along(): return lax.ppermute(block, axis, route)  4.75 us
    ppermute x2, starting transfers between devices, passed_along(): return lax.ppermute(block, axis, route)  4.57 us
    pallas_call x1, Pallas kernels, solve_and_update(): pl.pallas_call(solve_kernel, out_shape=(jax.ShapeDtypeStruct((count, BLOC...  4.55 us
    pallas_call x1, Pallas kernels, left_blocks(): pl.pallas_call(left_kernel, out_shape=jax.ShapeDtypeStruct((count, BLOCK,...  3.2 us
  transfers between devices with their start and end apart: 2, of which 1 were waited for; matrix products, arithmetic and copies ran while one was open for 0% of the time, Pallas kernels for 14%

profile of v2, /device:TPU:1, one launch (start us, length us, event | category | flops | bytes accessed | tf_op | source)
XLA Modules:
  0.0 93.2 jit_solution(10879661477765291931)
XLA Ops:
  0.0 2.6 %collective-permute-start = (s32[2]{0:T(128)}, s32[2]{0:T(128)S(1)}, u32[]{:S(2)}, u32[]{:S(2)}) collective-permute-start(s32[2]{0:T(128)} %bitcast.15), channel_id=1, source_target_pairs={{224,0},{0,32},{32,64},{64,96},{96,128},{128,160},{160,192},{192,2... | collective-permute-start | bytes 32 | tf_op jit(solution)/shard_map/ppermute | solution.py:283
  2.6 9.7 %grams.1 = f32[32,64,128]{2,1,0:T(8,128)S(1)} custom-call(f32[1,4096,256]{2,1,0:T(8,128)} %start_ref.5, f32[1,4096,512]{2,1,0:T(8,128)} %panel_ref.5), custom_call_target="tpu_custom_call" | custom-call | flops 6442450944 | bytes 12582912 | tf_op jit(solution)/shard_map/grams/pallas_call | solution.py:84
  12.3 0.0 copy-start.1
  12.3 0.0 copy-start.2
  12.3 0.1 convert_element_type.13
  12.4 0.0 collective-permute-done.want_ref
  12.4 28.1 %all_to_all.15 = f16[32,64,128]{2,1,0:T(8,128)(2,1)S(1)} all-to-all(f16[32,64,128]{2,1,0:T(8,128)(2,1)S(1)} %convert_element_type.13), channel_id=1, replica_groups=mesh['sym'=8,'row'=32] {'row'}, dimensions={0} | all-to-all | bytes 1048576 | tf_op jit(solution)/shard_map/all_to_all | solution.py:287
  40.5 0.1 convert_element_type.14
  40.8 0.1 fusion
  40.9 0.1 broadcast_in_dim.6
  41.0 0.0 copy-start.3
  41.0 0.0 copy-start.4
  41.0 21.5 %all_to_all.16 = f16[32,64,128]{2,1,0:T(8,128)(2,1)S(1)} all-to-all(f16[32,64,128]{2,1,0:T(8,128)(2,1)S(1)} %broadcast_in_dim.6), channel_id=1, replica_groups=mesh['sym'=8,'row'=32] {'row'}, dimensions={0} | all-to-all | bytes 1048576 | tf_op jit(solution)/shard_map/all_to_all | solution.py:287
  62.5 0.1 convert_element_type.15.sums_ref
  62.6 0.0 copy-done.1
  62.6 0.0 copy-done.2
  62.6 4.6 %solve.1 = (bf16[2,512,256]{2,1,0:T(8,128)(2,1)S(1)}, bf16[512,256]{1,0:T(8,128)(2,1)S(1)}, bf16[512,256]{1,0:T(8,128)(2,1)S(1)}) custom-call(s32[2]{0:T(128)S(1)} %collective-permute-done.want_ref, s32[8]{0:T(128)S(1)} %bitcast.10, f32[32,64,128]{2,1,0:T(8,128)S(1)} %convert_element_type.15.sums_ref, f32[1,4,128,128]{3,2,1,0:T(8,128)S(1)} %copy-done.1, ...), custom_call_target="tpu_custom_call" | custom-call | flops 805306368 | bytes 3145728 | tf_op jit(solution)/shard_map/solve/pallas_call | solution.py:211
  67.2 0.0 copy-start
  67.2 2.0 %collective-permute-start.1 = (bf16[2,512,256]{2,1,0:T(8,128)(2,1)S(1)}, bf16[2,512,256]{2,1,0:T(8,128)(2,1)S(1)}, u32[]{:S(2)}, u32[]{:S(2)}) collective-permute-start(bf16[2,512,256]{2,1,0:T(8,128)(2,1)S(1)} %get-tuple-element.12), channel_id=1, source_target_pairs={{32,0},{64,32},{96,64},{128,96},{160,128},{192,160},{224,192},{0,2... | collective-permute-start | bytes 1572872 | tf_op jit(solution)/shard_map/ppermute | solution.py:283
  69.1 0.0 copy-done.3
  69.1 0.0 copy-done.4
  69.1 3.2 %left.1.left_ref = bf16[2,512,256]{2,1,0:T(8,128)(2,1)S(1)} custom-call(s32[2]{0:T(128)S(1)} %bitcast.12, s32[2]{0:T(128)S(1)} %bitcast.13, s32[8]{0:T(128)S(1)} %bitcast.11, bf16[512,256]{1,0:T(8,128)(2,1)S(1)} %get-tuple-element.13.upper, bf16[512,256]{1,0:T(8,128)(2,1)S(1)} %get-tuple-element.14.lower, f32[1,4096,256]{2,1,0:T(8,128)} %start_ref.5, ...), custom_call_target="tpu_custom_call" | custom-call | flops 805306368 | bytes 3145728 | tf_op jit(solution)/shard_map/left/pallas_call | solution.py:241
  72.4 4.7 %collective-permute-done.1.right_ref = bf16[2,512,256]{2,1,0:T(8,128)(2,1)S(1)} collective-permute-done((bf16[2,512,256]{2,1,0:T(8,128)(2,1)S(1)}, bf16[2,512,256]{2,1,0:T(8,128)(2,1)S(1)}, u32[]{:S(2)}, u32[]{:S(2)}) %collective-permute-start.1) | collective-permute-done | bytes 524320 | tf_op jit(solution)/shard_map/ppermute | solution.py:283
  77.1 0.0 copy-done
  77.1 0.9 dipole.1
  78.0 14.5 %all_to_all.17 = bf16[32,8,256]{2,1,0:T(8,128)(2,1)S(1)} all-to-all(bf16[32,8,256]{2,1,0:T(8,128)(2,1)S(1)} %bitcast.9), channel_id=1, replica_groups=mesh['sym'=8,'row'=32] {'row'}, dimensions={0} | all-to-all | bytes 262144 | tf_op jit(solution)/shard_map/all_to_all | solution.py:287
  92.6 0.6 convert_reduce_fusion
  (8 shorter events, 0.1 us)
Async XLA Ops:
  0.0 12.4 %collective-permute-start = (s32[2]{0:T(128)}, s32[2]{0:T(128)S(1)}, u32[]{:S(2)}, u32[]{:S(2)}) collective-permute-start(s32[2]{0:T(128)} %bitcast.15), channel_id=1, source_target_pairs={{224,0},{0,32},{32,64},{64,96},{96,128},{128,160},{160,192},{192,2... | collective-permute-start | bytes 32 | tf_op jit(solution)/shard_map/ppermute | solution.py:283
  12.3 50.3 %copy-start.1 = (f32[1,4,128,128]{3,2,1,0:T(8,128)S(1)}, f32[1,4,128,128]{3,2,1,0:T(8,128)}, u32[]{:S(2)}) copy-start(f32[1,4,128,128]{3,2,1,0:T(8,128)} %factor_ref.1) | copy-start | bytes 786436
  12.3 50.3 %copy-start.2 = (s32[1,8]{1,0:T(1,128)S(1)}, s32[1,8]{1,0:T(1,128)}, u32[]{:S(2)}) copy-start(s32[1,8]{1,0:T(1,128)} %param.15) | copy-start | bytes 100
  41.0 28.1 %copy-start.3 = (s32[1,2]{1,0:T(1,128)S(1)}, s32[1,2]{1,0:T(1,128)}, u32[]{:S(2)}) copy-start(s32[1,2]{1,0:T(1,128)} %param.12) | copy-start | bytes 28
  41.0 28.1 %copy-start.4 = (s32[1,2]{1,0:T(1,128)S(1)}, s32[1,2]{1,0:T(1,128)}, u32[]{:S(2)}) copy-start(s32[1,2]{1,0:T(1,128)} %param.14) | copy-start | bytes 28
  67.2 9.9 %copy-start = (bf16[1,2,512,512]{3,2,1,0:T(8,128)(2,1)S(1)}, bf16[1,2,512,512]{3,2,1,0:T(8,128)(2,1)}, u32[]{:S(2)}) copy-start(bf16[1,2,512,512]{3,2,1,0:T(8,128)(2,1)} %tile_ref.1) | copy-start | bytes 3145732
  67.2 9.9 %collective-permute-start.1 = (bf16[2,512,256]{2,1,0:T(8,128)(2,1)S(1)}, bf16[2,512,256]{2,1,0:T(8,128)(2,1)S(1)}, u32[]{:S(2)}, u32[]{:S(2)}) collective-permute-start(bf16[2,512,256]{2,1,0:T(8,128)(2,1)S(1)} %get-tuple-element.12), channel_id=1, source_target_pairs={{32,0},{64,32},{96,64},{128,96},{160,128},{192,160},{224,192},{0,2... | collective-permute-start | bytes 1572872 | tf_op jit(solution)/shard_map/ppermute | solution.py:283

commit v3 on v2

--- a/solution.py
+++ b/solution.py
@@ -10,13 +10,13 @@
 F16 = jnp.float16
 BLOCK = 512
 STEP = 1024
-HALF = 16
+NEAR = 8
+HALF = 64
 PROJ = 2 * HALF
-COUP = 24
-SHARE = PROJ + COUP + 8
+COUP = 96
+BODY = PROJ + COUP
+SHARE = BODY + 8
 COUPLING_SCALE = 32.0
-
-
 ROWS = ((0,), (0,))
 
 
@@ -72,8 +72,8 @@
             axis=0,
         )
         lines = lines * COUPLING_SCALE
-        out_ref[:, PROJ : PROJ + COUP, :] = lines.reshape(count, COUP, 128)
-        out_ref[:, PROJ + COUP :, :] = jnp.broadcast_to(
+        out_ref[:, PROJ:BODY, :] = lines.reshape(count, COUP, 128)
+        out_ref[:, BODY:, :] = jnp.broadcast_to(
             exponent.reshape(1, 1, 1), (count, 8, 128)
         )
 
@@ -106,7 +106,7 @@
 
 
 def updated_block(start, panels, upper, lower, limit):
-    high, low = split(panels)
+    high, low = panels
     back = start - (dot(high, upper) + (dot(high, lower) + dot(low, upper)))
     line = lax.broadcasted_iota(jnp.int32, back.shape, 0)
     return jnp.where(line < limit, back, 0.0).astype(BF16)
@@ -116,6 +116,7 @@
     want_ref,
     limit_ref,
     sums_ref,
+    exponent_ref,
     factor_ref,
     start_ref,
     panel_ref,
@@ -137,18 +138,18 @@
             copies.append(copy)
     count = sums_ref.shape[0]
     width = factor_ref.shape[2]
-    scale = jnp.exp2(sums_ref[:, PROJ + COUP : PROJ + COUP + 1, :])
+    scale = jnp.exp2(exponent_ref[:1, :])
     size = (count * HALF, 128)
     inner = split(
         jnp.concatenate(
             [
-                (sums_ref[:, :HALF, :] * scale).reshape(size),
-                (sums_ref[:, HALF:PROJ, :] * scale).reshape(size),
+                sums_ref[:, :HALF, :].reshape(size) * scale,
+                sums_ref[:, HALF:PROJ, :].reshape(size) * scale,
             ],
             axis=1,
         )
     )
-    links = split(sums_ref[:, PROJ : PROJ + COUP, :].reshape(count * COUP, 128))
+    links = split(sums_ref[:, PROJ:BODY, :].reshape(count * COUP, 128))
 
     def part(pair, k):
         return tuple(p[k * width : (k + 1) * width] for p in pair)
@@ -161,6 +162,9 @@
         chained[later] = split(
             jnp.concatenate([dot3(factors[k], part(links, at)) for k, at in pairs], axis=0)
         )
+    for copy in copies:
+        copy.wait()
+    fetched = [split(panels[t]) for t in range(out_ref.shape[0])]
     parts = [None] * 4
     for level in (3, 2, 1, 0):
         parts[level] = split(current[level])
@@ -171,10 +175,8 @@
     upper[...] = jnp.concatenate([p[0] for p in parts], axis=0)
     lower[...] = jnp.concatenate([p[1] for p in parts], axis=0)
     for t in range(out_ref.shape[0]):
-        copies[2 * t].wait()
-        copies[2 * t + 1].wait()
         out_ref[t] = updated_block(
-            starts[t], panels[t], upper[...], lower[...], limit_ref[want_ref[t]]
+            starts[t], fetched[t], upper[...], lower[...], limit_ref[want_ref[t]]
         )
 
 
@@ -184,7 +186,7 @@
     turn = pl.program_id(0)
     out_ref[0] = updated_block(
         start_ref[0],
-        panel_ref[0],
+        split(panel_ref[0]),
         upper[...],
         lower[...],
         limit_ref[left_ref[turn]] * occupied_ref[turn],
@@ -204,7 +206,7 @@
     )
 
 
-def solve_and_update(want, limits, sums, factors, start, panels):
+def solve_and_update(want, limits, sums, exponent, factors, start, panels):
     count = want.shape[0]
     eigen, columns = start.shape[2], panels.shape[2]
     coefficients = jax.ShapeDtypeStruct((columns, eigen), BF16)
@@ -215,7 +217,7 @@
             coefficients,
             coefficients,
         ),
-        in_specs=[SCALARS, SCALARS, ARRAY, ARRAY, FAR, FAR],
+        in_specs=[SCALARS, SCALARS, ARRAY, ARRAY, ARRAY, FAR, FAR],
         out_specs=(ARRAY,) * 3,
         scratch_shapes=[
             pltpu.VMEM((count, BLOCK, eigen), F32),
@@ -225,7 +227,7 @@
         compiler_params=pltpu.CompilerParams(vmem_limit_bytes=16 << 20),
         cost_estimate=update_cost(count, columns, eigen),
         name="solve",
-    )(want, limits, sums, factors, start, panels)
+    )(want, limits, sums, exponent, factors, start, panels)
 
 
 def left_blocks(left, occupied, limits, upper, lower, start, panels):
@@ -283,8 +285,23 @@
     return lax.ppermute(block, axis, route)
 
 
-def exchanged(shares):
-    return lax.all_to_all(shares, "row", 0, 0, tiled=True)
+def exchanged(shares, groups=None):
+    return lax.all_to_all(shares, "row", 0, 0, axis_index_groups=groups, tiled=True)
+
+
+def combined(terms):
+    count = terms.shape[0]
+    terms = terms.astype(F32)
+    exponents = terms[:, BODY:]
+    proj = jnp.sum(terms[:, :PROJ] * jnp.exp2(exponents[:, :1]), axis=0)
+    coup = jnp.sum(terms[:, PROJ:BODY], axis=0) * (1.0 / count)
+    exponent = jnp.max(exponents, axis=0) + float(count.bit_length() - 1)
+    return proj * jnp.exp2(-exponent[:1]), coup, exponent
+
+
+def copies_of(parts, count):
+    lines = jnp.concatenate(parts, axis=0).astype(F16)
+    return jnp.broadcast_to(lines, (count, *lines.shape))
 
 
 def on_device(
@@ -294,18 +311,16 @@
     vectors = pltpu.with_memory_space_constraint(vectors, pltpu.HBM)
     reflectors = pltpu.with_memory_space_constraint(reflectors, pltpu.HBM)
     want = passed_along(tile_right[0], "sym", 1)
-    shares = local_grams(vectors, reflectors, count).astype(F16)
+    far = count // NEAR
+    inside = [[far_at * NEAR + at for at in range(NEAR)] for far_at in range(far)]
+    across = [[far_at * NEAR + at for far_at in range(far)] for at in range(NEAR)]
+    shares = local_grams(vectors, reflectors, NEAR).astype(F16)
     want, shares = lax.optimization_barrier((want, shares))
-    terms = exchanged(shares).astype(F32)
-    exponents = terms[:, PROJ + COUP :]
-    proj = jnp.sum(terms[:, :PROJ] * jnp.exp2(exponents[:, :1]), axis=0)
-    coup = jnp.sum(terms[:, PROJ : PROJ + COUP], axis=0) * (1.0 / COUPLING_SCALE)
-    exponent = jnp.max(exponents, axis=0) + 5.0
-    owned = jnp.concatenate([proj * jnp.exp2(-exponent[:1]), coup, exponent], axis=0)
-    copies = jnp.broadcast_to(owned.astype(F16), (count, SHARE, 128))
-    sums = exchanged(copies).astype(F32)
+    owned = combined(exchanged(shares, inside))
+    proj, coup, exponent = combined(exchanged(copies_of(owned, far), across))
+    sums = exchanged(copies_of((proj, coup), NEAR), inside).astype(F32)
     packed, upper, lower = solve_and_update(
-        want, channels[0], sums, factors, vectors, reflectors
+        want, channels[0], sums, exponent, factors, vectors, reflectors
     )
     right = passed_along(packed, "sym", -1)
     left = left_blocks(

time: 93.4 us -> 85.9 us (0.920)
  blocking collectives: 64.1 us -> 54.6 us
  starting transfers between devices: 4.57 us -> 6.15 us
    all_to_all x3 -> x4, blocking collectives: 64.1 us -> 54.6 us  [exchanged(): lax.all_to_all(shares, 'row', 0, 0, axis_index_groups=groups, tiled=True)]
    ppermute x2, starting transfers between devices: 4.57 us -> 6.15 us  [passed_along(): return lax.ppermute(block, axis, route)]
  transfers between devices with their start and end apart: 2 -> 2, of which waited for: 1 -> 1; matrix products, arithmetic and copies ran while one was open for 0% -> 0% of each run, Pallas kernels for 14% -> 15%
where the time goes in v3:
time: 85.9 us; the launch traced here: 85.5 us
  blocking collectives  54.6 us (64%)
  Pallas kernels  18.5 us (22%)
  starting transfers between devices  6.15 us (7%)
  waiting for transfers between devices  4.78 us (6%)
  other arithmetic  1.1 us (1%)
    all_to_all x4, blocking collectives, exchanged(): lax.all_to_all(shares, 'row', 0, 0, axis_index_groups=groups, tiled=True)  54.6 us
    pallas_call x1, Pallas kernels, local_grams(): pl.pallas_call(gram_kernel, out_shape=jax.ShapeDtypeStruct((count, SHARE,...  9.7 us
    ppermute x2, starting transfers between devices, passed_along(): return lax.ppermute(block, axis, route)  6.15 us
    ppermute x2, waiting for transfers between devices, passed_along(): return lax.ppermute(block, axis, route)  4.78 us
    pallas_call x1, Pallas kernels, solve_and_update(): pl.pallas_call(solve_kernel, out_shape=(jax.ShapeDtypeStruct((count, BLOC...  4.73 us
    pallas_call x1, Pallas kernels, left_blocks(): pl.pallas_call(left_kernel, out_shape=jax.ShapeDtypeStruct((count, BLOCK,...  3.19 us
  transfers between devices with their start and end apart: 2, of which 1 were waited for; matrix products, arithmetic and copies ran while one was open for 0% of the time, Pallas kernels for 15%

profile of v3, /device:TPU:1, one launch (start us, length us, event | category | flops | bytes accessed | tf_op | source)
XLA Modules:
  0.0 85.5 jit_solution(6142505784490459054)
XLA Ops:
  0.0 2.6 %collective-permute-start = (s32[2]{0:T(128)}, s32[2]{0:T(128)S(1)}, u32[]{:S(2)}, u32[]{:S(2)}) collective-permute-start(s32[2]{0:T(128)} %bitcast.19), channel_id=1, source_target_pairs={{224,0},{0,32},{32,64},{64,96},{96,128},{128,160},{160,192},{192,2... | collective-permute-start | bytes 32 | tf_op jit(solution)/shard_map/ppermute | solution.py:285
  2.6 9.7 %grams.1 = f32[8,232,128]{2,1,0:T(8,128)S(1)} custom-call(f32[1,4096,256]{2,1,0:T(8,128)} %start_ref.5, f32[1,4096,512]{2,1,0:T(8,128)} %panel_ref.5), custom_call_target="tpu_custom_call" | custom-call | flops 6442450944 | bytes 12582912 | tf_op jit(solution)/shard_map/grams/pallas_call | solution.py:84
  12.3 0.0 copy-start.1
  12.3 0.0 copy-start.2
  12.3 0.1 convert_element_type.17
  12.4 0.0 collective-permute-done.want_ref
  12.4 14.5 %all_to_all.20 = f16[8,232,128]{2,1,0:T(8,128)(2,1)S(1)} all-to-all(f16[8,232,128]{2,1,0:T(8,128)(2,1)S(1)} %convert_element_type.17), channel_id=1, replica_groups={{0,1,2,3,4,5,6,7},{8,9,10,11,12,13,14,15},{16,17,18,19,20,21,22,23},{24..., dimensions={0} | all-to-all | bytes 950272 | tf_op jit(solution)/shard_map/all_to_all | solution.py:289
  27.0 0.1 convert_element_type.18
  27.3 16.1 %all_to_all.21 = f16[4,232,128]{2,1,0:T(8,128)(2,1)S(1)} all-to-all(f16[4,232,128]{2,1,0:T(8,128)(2,1)S(1)} %broadcast_in_dim.9), channel_id=1, replica_groups={{0,8,16,24},{1,9,17,25},{2,10,18,26},{3,11,19,27},{4,12,20,28},{5,13,21..., dimensions={0} | all-to-all | bytes 475136 | tf_op jit(solution)/shard_map/all_to_all | solution.py:289
  43.5 0.0 copy-start.3
  43.5 0.0 copy-start.4
  43.6 0.1 broadcast_in_dim.10
  43.7 10.5 %all_to_all.22 = f16[8,224,128]{2,1,0:T(8,128)(2,1)S(1)} all-to-all(f16[8,224,128]{2,1,0:T(8,128)(2,1)S(1)} %broadcast_in_dim.10), channel_id=1, replica_groups={{0,1,2,3,4,5,6,7},{8,9,10,11,12,13,14,15},{16,17,18,19,20,21,22,23},{24..., dimensions={0} | all-to-all | bytes 917504 | tf_op jit(solution)/shard_map/all_to_all | solution.py:289
  54.2 0.1 convert_element_type.20.sums_ref
  54.3 0.0 copy-done.1
  54.3 0.0 copy-done.2
  54.3 4.7 %solve.1 = (bf16[2,512,256]{2,1,0:T(8,128)(2,1)S(1)}, bf16[512,256]{1,0:T(8,128)(2,1)S(1)}, bf16[512,256]{1,0:T(8,128)(2,1)S(1)}) custom-call(s32[2]{0:T(128)S(1)} %collective-permute-done.want_ref, s32[8]{0:T(128)S(1)} %bitcast.13, f32[8,224,128]{2,1,0:T(8,128)S(1)} %convert_element_type.20.sums_ref, f32[8,128]{1,0:T(8,128)S(1)} %broadcast_add_fusion.exponent_ref, ...), custom_call_target="tpu_custom_call" | custom-call | flops 805306368 | bytes 3145728 | tf_op jit(solution)/shard_map/solve/pallas_call | solution.py:213
  59.0 0.0 copy-start
  59.0 3.5 %collective-permute-start.1 = (bf16[2,512,256]{2,1,0:T(8,128)(2,1)S(1)}, bf16[2,512,256]{2,1,0:T(8,128)(2,1)S(1)}, u32[]{:S(2)}, u32[]{:S(2)}) collective-permute-start(bf16[2,512,256]{2,1,0:T(8,128)(2,1)S(1)} %get-tuple-element.12), channel_id=1, source_target_pairs={{32,0},{64,32},{96,64},{128,96},{160,128},{192,160},{224,192},{0,2... | collective-permute-start | bytes 1572872 | tf_op jit(solution)/shard_map/ppermute | solution.py:285
  62.6 0.0 copy-done.3
  62.6 0.0 copy-done.4
  62.6 3.2 %left.1.left_ref = bf16[2,512,256]{2,1,0:T(8,128)(2,1)S(1)} custom-call(s32[2]{0:T(128)S(1)} %bitcast.15, s32[2]{0:T(128)S(1)} %bitcast.16, s32[8]{0:T(128)S(1)} %bitcast.14, bf16[512,256]{1,0:T(8,128)(2,1)S(1)} %get-tuple-element.13.upper, bf16[512,256]{1,0:T(8,128)(2,1)S(1)} %get-tuple-element.14.lower, f32[1,4096,256]{2,1,0:T(8,128)} %start_ref.5, ...), custom_call_target="tpu_custom_call" | custom-call | flops 805306368 | bytes 3145728 | tf_op jit(solution)/shard_map/left/pallas_call | solution.py:243
  65.8 4.8 %collective-permute-done.1.right_ref = bf16[2,512,256]{2,1,0:T(8,128)(2,1)S(1)} collective-permute-done((bf16[2,512,256]{2,1,0:T(8,128)(2,1)S(1)}, bf16[2,512,256]{2,1,0:T(8,128)(2,1)S(1)}, u32[]{:S(2)}, u32[]{:S(2)}) %collective-permute-start.1) | collective-permute-done | bytes 524320 | tf_op jit(solution)/shard_map/ppermute | solution.py:285
  70.6 0.0 copy-done
  70.6 0.9 %dipole.1 = bf16[256,256]{1,0:T(8,128)(2,1)S(1)} custom-call(bf16[1,2,512,512]{3,2,1,0:T(8,128)(2,1)S(1)} %copy-done, bf16[2,512,256]{2,1,0:T(8,128)(2,1)S(1)} %collective-permute-done.1.right_ref, bf16[2,512,256]{2,1,0:T(8,128)(2,1)S(1)} %left.1.left_ref), custom_call_target="tpu_custom_call" | custom-call | tf_op jit(solution)/shard_map/dipole/pallas_call | solution.py:274
  71.5 13.4 %all_to_all.23 = bf16[32,8,256]{2,1,0:T(8,128)(2,1)S(1)} all-to-all(bf16[32,8,256]{2,1,0:T(8,128)(2,1)S(1)} %bitcast.12), channel_id=1, replica_groups=mesh['sym'=8,'row'=32] {'row'}, dimensions={0} | all-to-all | bytes 262144 | tf_op jit(solution)/shard_map/all_to_all | solution.py:289
  84.9 0.6 convert_reduce_fusion
  (20 shorter events, 0.3 us)
Async XLA Ops:
  0.0 12.4 %collective-permute-start = (s32[2]{0:T(128)}, s32[2]{0:T(128)S(1)}, u32[]{:S(2)}, u32[]{:S(2)}) collective-permute-start(s32[2]{0:T(128)} %bitcast.19), channel_id=1, source_target_pairs={{224,0},{0,32},{32,64},{64,96},{96,128},{128,160},{160,192},{192,2... | collective-permute-start | bytes 32 | tf_op jit(solution)/shard_map/ppermute | solution.py:285
  12.3 41.9 %copy-start.1 = (f32[1,4,128,128]{3,2,1,0:T(8,128)S(1)}, f32[1,4,128,128]{3,2,1,0:T(8,128)}, u32[]{:S(2)}) copy-start(f32[1,4,128,128]{3,2,1,0:T(8,128)} %factor_ref.1) | copy-start | bytes 786436
  12.3 41.9 %copy-start.2 = (s32[1,8]{1,0:T(1,128)S(1)}, s32[1,8]{1,0:T(1,128)}, u32[]{:S(2)}) copy-start(s32[1,8]{1,0:T(1,128)} %param.15) | copy-start | bytes 100
  43.5 19.0 %copy-start.3 = (s32[1,2]{1,0:T(1,128)S(1)}, s32[1,2]{1,0:T(1,128)}, u32[]{:S(2)}) copy-start(s32[1,2]{1,0:T(1,128)} %param.12) | copy-start | bytes 28
  43.5 19.0 %copy-start.4 = (s32[1,2]{1,0:T(1,128)S(1)}, s32[1,2]{1,0:T(1,128)}, u32[]{:S(2)}) copy-start(s32[1,2]{1,0:T(1,128)} %param.14) | copy-start | bytes 28
  59.0 11.5 %copy-start = (bf16[1,2,512,512]{3,2,1,0:T(8,128)(2,1)S(1)}, bf16[1,2,512,512]{3,2,1,0:T(8,128)(2,1)}, u32[]{:S(2)}) copy-start(bf16[1,2,512,512]{3,2,1,0:T(8,128)(2,1)} %tile_ref.1) | copy-start | bytes 3145732
  59.0 11.5 %collective-permute-start.1 = (bf16[2,512,256]{2,1,0:T(8,128)(2,1)S(1)}, bf16[2,512,256]{2,1,0:T(8,128)(2,1)S(1)}, u32[]{:S(2)}, u32[]{:S(2)}) collective-permute-start(bf16[2,512,256]{2,1,0:T(8,128)(2,1)S(1)} %get-tuple-element.12), channel_id=1, source_target_pairs={{32,0},{64,32},{96,64},{128,96},{160,128},{192,160},{224,192},{0,2... | collective-permute-start | bytes 1572872 | tf_op jit(solution)/shard_map/ppermute | solution.py:285

commit v4 on v3

--- a/solution.py
+++ b/solution.py
@@ -1,3 +1,5 @@
+import functools
+
 import jax
 import jax.numpy as jnp
 from jax import lax
@@ -105,6 +107,46 @@
     )(start, panels)
 
 
+def fetch_kernel(which_ref, start_ref, panel_ref, start_out, high_out, low_out):
+    high, low = split(panel_ref[0])
+    start_out[0] = start_ref[0]
+    high_out[0] = high
+    low_out[0] = low
+
+
+def fetched_blocks(which, start, panels):
+    count = which.shape[0]
+    eigen, columns = start.shape[2], panels.shape[2]
+
+    def named(width):
+        return pl.BlockSpec((1, BLOCK, width), lambda t, which: (0, which[t], 0))
+
+    def kept(width):
+        return pl.BlockSpec((1, BLOCK, width), lambda t, which: (t, 0, 0))
+
+    return pl.pallas_call(
+        fetch_kernel,
+        out_shape=(
+            jax.ShapeDtypeStruct((count, BLOCK, eigen), F32),
+            jax.ShapeDtypeStruct((count, BLOCK, columns), BF16),
+            jax.ShapeDtypeStruct((count, BLOCK, columns), BF16),
+        ),
+        grid_spec=pltpu.PrefetchScalarGridSpec(
+            num_scalar_prefetch=1,
+            grid=(count,),
+            in_specs=[named(eigen), named(columns)],
+            out_specs=(kept(eigen), kept(columns), kept(columns)),
+        ),
+        compiler_params=pltpu.CompilerParams(vmem_limit_bytes=10 << 20),
+        cost_estimate=pl.CostEstimate(
+            flops=count * BLOCK * columns,
+            bytes_accessed=8 * count * BLOCK * (columns + eigen),
+            transcendentals=0,
+        ),
+        name="fetch",
+    )(which, start, panels)
+
+
 def updated_block(start, panels, upper, lower, limit):
     high, low = panels
     back = start - (dot(high, upper) + (dot(high, lower) + dot(low, upper)))
@@ -119,23 +161,12 @@
     exponent_ref,
     factor_ref,
     start_ref,
-    panel_ref,
+    high_ref,
+    low_ref,
     out_ref,
     upper,
     lower,
-    starts,
-    panels,
-    arrived,
 ):
-    copies = []
-    for t in range(out_ref.shape[0]):
-        rows = pl.ds(pl.multiple_of(want_ref[t] * BLOCK, BLOCK), BLOCK)
-        for source, target, kind in ((panel_ref, panels, 0), (start_ref, starts, 1)):
-            copy = pltpu.make_async_copy(
-                source.at[0, rows], target.at[t], arrived.at[kind, t]
-            )
-            copy.start()
-            copies.append(copy)
     count = sums_ref.shape[0]
     width = factor_ref.shape[2]
     scale = jnp.exp2(exponent_ref[:1, :])
@@ -162,9 +193,6 @@
         chained[later] = split(
             jnp.concatenate([dot3(factors[k], part(links, at)) for k, at in pairs], axis=0)
         )
-    for copy in copies:
-        copy.wait()
-    fetched = [split(panels[t]) for t in range(out_ref.shape[0])]
     parts = [None] * 4
     for level in (3, 2, 1, 0):
         parts[level] = split(current[level])
@@ -176,7 +204,7 @@
     lower[...] = jnp.concatenate([p[1] for p in parts], axis=0)
     for t in range(out_ref.shape[0]):
         out_ref[t] = updated_block(
-            starts[t], fetched[t], upper[...], lower[...], limit_ref[want_ref[t]]
+            start_ref[t], (high_ref[t], low_ref[t]), upper[...], lower[...], limit_ref[want_ref[t]]
         )
 
 
@@ -195,7 +223,6 @@
 
 SCALARS = pl.BlockSpec(memory_space=pltpu.SMEM)
 ARRAY = pl.BlockSpec(memory_space=pltpu.VMEM)
-FAR = pl.BlockSpec(memory_space=pltpu.HBM)
 
 
 def update_cost(blocks, columns, eigen):
@@ -206,9 +233,9 @@
     )
 
 
-def solve_and_update(want, limits, sums, exponent, factors, start, panels):
+def solve_and_update(want, limits, sums, exponent, factors, start, high, low):
     count = want.shape[0]
-    eigen, columns = start.shape[2], panels.shape[2]
+    eigen, columns = start.shape[2], high.shape[2]
     coefficients = jax.ShapeDtypeStruct((columns, eigen), BF16)
     return pl.pallas_call(
         solve_kernel,
@@ -217,17 +244,12 @@
             coefficients,
             coefficients,
         ),
-        in_specs=[SCALARS, SCALARS, ARRAY, ARRAY, ARRAY, FAR, FAR],
+        in_specs=[SCALARS] * 2 + [ARRAY] * 6,
         out_specs=(ARRAY,) * 3,
-        scratch_shapes=[
-            pltpu.VMEM((count, BLOCK, eigen), F32),
-            pltpu.VMEM((count, BLOCK, columns), F32),
-            pltpu.SemaphoreType.DMA((2, count)),
-        ],
-        compiler_params=pltpu.CompilerParams(vmem_limit_bytes=16 << 20),
+        compiler_params=pltpu.CompilerParams(vmem_limit_bytes=12 << 20),
         cost_estimate=update_cost(count, columns, eigen),
         name="solve",
-    )(want, limits, sums, exponent, factors, start, panels)
+    )(want, limits, sums, exponent, factors, start, high, low)
 
 
 def left_blocks(left, occupied, limits, upper, lower, start, panels):
@@ -296,12 +318,22 @@
     proj = jnp.sum(terms[:, :PROJ] * jnp.exp2(exponents[:, :1]), axis=0)
     coup = jnp.sum(terms[:, PROJ:BODY], axis=0) * (1.0 / count)
     exponent = jnp.max(exponents, axis=0) + float(count.bit_length() - 1)
-    return proj * jnp.exp2(-exponent[:1]), coup, exponent
-
-
-def copies_of(parts, count):
-    lines = jnp.concatenate(parts, axis=0).astype(F16)
-    return jnp.broadcast_to(lines, (count, *lines.shape))
+    return jnp.concatenate([proj * jnp.exp2(-exponent[:1]), coup, exponent], axis=0)
+
+
+def added(shares):
+    exponents = [share[BODY:] for share in shares]
+    proj = sum(s[:PROJ] * jnp.exp2(e[:1]) for s, e in zip(shares, exponents))
+    coup = sum(s[PROJ:BODY] for s in shares) * (1.0 / len(shares))
+    exponent = functools.reduce(jnp.maximum, exponents)
+    exponent = exponent + float(len(shares).bit_length() - 1)
+    return jnp.concatenate([proj * jnp.exp2(-exponent[:1]), coup, exponent], axis=0)
+
+
+def around(share, step):
+    count = lax.axis_size("row")
+    route = [((i + step) % count, i) for i in range(count)]
+    return lax.ppermute(share, "row", route)
 
 
 def on_device(
@@ -313,14 +345,19 @@
     want = passed_along(tile_right[0], "sym", 1)
     far = count // NEAR
     inside = [[far_at * NEAR + at for at in range(NEAR)] for far_at in range(far)]
-    across = [[far_at * NEAR + at for far_at in range(far)] for at in range(NEAR)]
     shares = local_grams(vectors, reflectors, NEAR).astype(F16)
     want, shares = lax.optimization_barrier((want, shares))
-    owned = combined(exchanged(shares, inside))
-    proj, coup, exponent = combined(exchanged(copies_of(owned, far), across))
-    sums = exchanged(copies_of((proj, coup), NEAR), inside).astype(F32)
+    owned = combined(exchanged(shares, inside)).astype(F16)
+    want, owned = lax.optimization_barrier((want, owned))
+    named = fetched_blocks(want, vectors, reflectors)
+    others = [around(owned, NEAR * step) for step in (1, far - 1, *range(2, far - 1))]
+    others, named = lax.optimization_barrier((others, named))
+    owned = added([share.astype(F32) for share in (owned, *others)])
+    copies = jnp.broadcast_to(owned[:BODY].astype(F16), (NEAR, BODY, 128))
+    sums = exchanged(copies, inside).astype(F32)
+    exponent = owned[BODY:]
     packed, upper, lower = solve_and_update(
-        want, channels[0], sums, exponent, factors, vectors, reflectors
+        want, channels[0], sums, exponent, factors, *named
     )
     right = passed_along(packed, "sym", -1)
     left = left_blocks(

time: 85.9 us -> 82.3 us (0.958)
  blocking collectives: 54.6 us -> 41.5 us
  starting transfers between devices: 6.15 us -> 15 us
    all_to_all x4 -> x3, blocking collectives: 54.6 us -> 41.5 us  [exchanged(): lax.all_to_all(shares, 'row', 0, 0, axis_index_groups=groups, tiled=True)]
    ppermute x0 -> x3, starting transfers between devices: none -> 9.67 us  [around(): return lax.ppermute(share, 'row', route)]
    pallas_call x0 -> x1, Pallas kernels: none -> 2.63 us  [fetched_blocks(): pl.pallas_call(fetch_kernel, out_shape=(jax.ShapeDtypeStruct((count, BLOC...]
    pallas_call x1, Pallas kernels: 4.73 us -> 2.89 us  [solve_and_update(): pl.pallas_call(solve_kernel, out_shape=(jax.ShapeDtypeStruct((count, BLOC...]
  transfers between devices with their start and end apart: 2 -> 5, of which waited for: 1 -> 1; matrix products, arithmetic and copies ran while one was open for 0% -> 0% of each run, Pallas kernels for 15% -> 19%
where the time goes in v4:
time: 82.3 us; the launch traced here: 82 us
  blocking collectives  41.5 us (50%)
  Pallas kernels  19.3 us (23%)
  starting transfers between devices  15 us (18%)
  waiting for transfers between devices  4.77 us (6%)
  other arithmetic  1.13 us (1%)
    all_to_all x3, blocking collectives, exchanged(): lax.all_to_all(shares, 'row', 0, 0, axis_index_groups=groups, tiled=True)  41.5 us
    pallas_call x1, Pallas kernels, local_grams(): pl.pallas_call(gram_kernel, out_shape=jax.ShapeDtypeStruct((count, SHARE,...  9.7 us
    ppermute x3, starting transfers between devices, around(): return lax.ppermute(share, 'row', route)  9.67 us
    ppermute x2, starting transfers between devices, passed_along(): return lax.ppermute(block, axis, route)  5.32 us
    ppermute x2, waiting for transfers between devices, passed_along(): return lax.ppermute(block, axis, route)  4.76 us
    pallas_call x1, Pallas kernels, left_blocks(): pl.pallas_call(left_kernel, out_shape=jax.ShapeDtypeStruct((count, BLOCK,...  3.19 us
    pallas_call x1, Pallas kernels, solve_and_update(): pl.pallas_call(solve_kernel, out_shape=(jax.ShapeDtypeStruct((count, BLOC...  2.89 us
    pallas_call x1, Pallas kernels, fetched_blocks(): pl.pallas_call(fetch_kernel, out_shape=(jax.ShapeDtypeStruct((count, BLOC...  2.63 us
  transfers between devices with their start and end apart: 5, of which 1 were waited for; matrix products, arithmetic and copies ran while one was open for 0% of the time, Pallas kernels for 19%

profile of v4, /device:TPU:1, one launch (start us, length us, event | category | flops | bytes accessed | tf_op | source)
XLA Modules:
  0.0 82.0 jit_solution(11781882651774920875)
XLA Ops:
  0.0 2.6 %collective-permute-start = (s32[2]{0:T(128)}, s32[2]{0:T(128)S(1)}, u32[]{:S(2)}, u32[]{:S(2)}) collective-permute-start(s32[2]{0:T(128)} %bitcast.25), channel_id=1, source_target_pairs={{224,0},{0,32},{32,64},{64,96},{96,128},{128,160},{160,192},{192,2... | collective-permute-start | bytes 32 | tf_op jit(solution)/shard_map/ppermute | solution.py:307
  2.6 9.7 %grams.1 = f32[8,232,128]{2,1,0:T(8,128)S(1)} custom-call(f32[1,4096,256]{2,1,0:T(8,128)} %start_ref.5, f32[1,4096,512]{2,1,0:T(8,128)} %panel_ref.5), custom_call_target="tpu_custom_call" | custom-call | flops 6442450944 | bytes 12582912 | tf_op jit(solution)/shard_map/grams/pallas_call | solution.py:86
  12.3 0.1 convert_element_type.26
  12.4 0.0 collective-permute-done.which_ref.want_ref
  12.4 14.5 %all_to_all.15 = f16[8,232,128]{2,1,0:T(8,128)(2,1)S(1)} all-to-all(f16[8,232,128]{2,1,0:T(8,128)(2,1)S(1)} %convert_element_type.26), channel_id=1, replica_groups={{0,1,2,3,4,5,6,7},{8,9,10,11,12,13,14,15},{16,17,18,19,20,21,22,23},{24..., dimensions={0} | all-to-all | bytes 950272 | tf_op jit(solution)/shard_map/all_to_all | solution.py:311
  26.9 0.1 convert_element_type.27
  27.2 0.0 copy-start.1
  27.2 0.0 copy-start.2
  27.2 6.1 %collective-permute-start.3 = (f16[232,128]{1,0:T(8,128)(2,1)S(1)}, f16[232,128]{1,0:T(8,128)(2,1)S(1)}, u32[]{:S(2)}, u32[]{:S(2)}) collective-permute-start(f16[232,128]{1,0:T(8,128)(2,1)S(1)} %pad_maximum_fusion), channel_id=1, source_target_pairs={{16,0},{17,1},{18,2},{19,3},{20,4},{21,5},{22,6},{23,7},{24,8},{25... | collective-permute-start | bytes 178184 | tf_op jit(solution)/shard_map/ppermute | solution.py:336
  33.3 1.2 %collective-permute-start.2 = (f16[232,128]{1,0:T(8,128)(2,1)S(1)}, f16[232,128]{1,0:T(8,128)(2,1)S(1)}, u32[]{:S(2)}, u32[]{:S(2)}) collective-permute-start(f16[232,128]{1,0:T(8,128)(2,1)S(1)} %pad_maximum_fusion), channel_id=1, source_target_pairs={{24,0},{25,1},{26,2},{27,3},{28,4},{29,5},{30,6},{31,7},{0,8},{1,9... | collective-permute-start | bytes 178184 | tf_op jit(solution)/shard_map/ppermute | solution.py:336
  34.5 2.4 %collective-permute-start.1 = (f16[232,128]{1,0:T(8,128)(2,1)S(1)}, f16[232,128]{1,0:T(8,128)(2,1)S(1)}, u32[]{:S(2)}, u32[]{:S(2)}) collective-permute-start(f16[232,128]{1,0:T(8,128)(2,1)S(1)} %pad_maximum_fusion), channel_id=1, source_target_pairs={{8,0},{9,1},{10,2},{11,3},{12,4},{13,5},{14,6},{15,7},{16,8},{17,9... | collective-permute-start | bytes 178184 | tf_op jit(solution)/shard_map/ppermute | solution.py:336
  36.9 0.0 copy-start.3
  36.9 0.0 copy-start.4
  37.0 2.6 %fetch.1 = (f32[2,512,256]{2,1,0:T(8,128)S(1)}, bf16[2,512,512]{2,1,0:T(8,128)(2,1)S(1)}, bf16[2,512,512]{2,1,0:T(8,128)(2,1)S(1)}) custom-call(s32[2]{0:T(128)S(1)} %collective-permute-done.which_ref.want_ref, f32[1,4096,256]{2,1,0:T(8,128)} %start_ref.5, f32[1,4096,512]{2,1,0:T(8,128)} %panel_ref.5), custom_call_target="tpu_custom_call" | custom-call | flops 524288 | bytes 6291456 | tf_op jit(solution)/shard_map/fetch/pallas_call | solution.py:127
  39.6 0.0 collective-permute-done.3
  39.6 0.0 collective-permute-done.2
  39.6 0.0 collective-permute-done.1
  39.8 0.1 broadcast_in_dim.6
  39.9 10.7 %all_to_all.16 = f16[8,224,128]{2,1,0:T(8,128)(2,1)S(1)} all-to-all(f16[8,224,128]{2,1,0:T(8,128)(2,1)S(1)} %broadcast_in_dim.6), channel_id=1, replica_groups={{0,1,2,3,4,5,6,7},{8,9,10,11,12,13,14,15},{16,17,18,19,20,21,22,23},{24..., dimensions={0} | all-to-all | bytes 917504 | tf_op jit(solution)/shard_map/all_to_all | solution.py:311
  50.6 0.1 convert_element_type.32.sums_ref
  50.7 0.0 copy-done.1
  50.7 0.0 copy-done.2
  50.7 0.0 copy-start
  50.7 2.9 %solve.1 = (bf16[2,512,256]{2,1,0:T(8,128)(2,1)S(1)}, bf16[512,256]{1,0:T(8,128)(2,1)S(1)}, bf16[512,256]{1,0:T(8,128)(2,1)S(1)}) custom-call(s32[2]{0:T(128)S(1)} %collective-permute-done.which_ref.want_ref, s32[8]{0:T(128)S(1)} %bitcast.20, f32[8,224,128]{2,1,0:T(8,128)S(1)} %convert_element_type.32.sums_ref, f32[8,128]{1,0:T(8,128)S(1)} %fusion.8.exponent_ref, ...), custom_call_target="tpu_custom_call" | custom-call | flops 805306368 | bytes 3145728 | tf_op jit(solution)/shard_map/solve/pallas_call | solution.py:240
  53.6 2.7 %collective-permute-start.4 = (bf16[2,512,256]{2,1,0:T(8,128)(2,1)S(1)}, bf16[2,512,256]{2,1,0:T(8,128)(2,1)S(1)}, u32[]{:S(2)}, u32[]{:S(2)}) collective-permute-start(bf16[2,512,256]{2,1,0:T(8,128)(2,1)S(1)} %get-tuple-element.34), channel_id=1, source_target_pairs={{32,0},{64,32},{96,64},{128,96},{160,128},{192,160},{224,192},{0,2... | collective-permute-start | bytes 1572872 | tf_op jit(solution)/shard_map/ppermute | solution.py:307
  56.4 0.0 copy-done.3
  56.4 0.0 copy-done.4
  56.4 3.2 %left.1.left_ref = bf16[2,512,256]{2,1,0:T(8,128)(2,1)S(1)} custom-call(s32[2]{0:T(128)S(1)} %bitcast.22, s32[2]{0:T(128)S(1)} %bitcast.23, s32[8]{0:T(128)S(1)} %bitcast.21, bf16[512,256]{1,0:T(8,128)(2,1)S(1)} %get-tuple-element.35.upper, bf16[512,256]{1,0:T(8,128)(2,1)S(1)} %get-tuple-element.36.lower, f32[1,4096,256]{2,1,0:T(8,128)} %start_ref.5, ...), custom_call_target="tpu_custom_call" | custom-call | flops 805306368 | bytes 3145728 | tf_op jit(solution)/shard_map/left/pallas_call | solution.py:265
  59.6 4.8 %collective-permute-done.4.right_ref = bf16[2,512,256]{2,1,0:T(8,128)(2,1)S(1)} collective-permute-done((bf16[2,512,256]{2,1,0:T(8,128)(2,1)S(1)}, bf16[2,512,256]{2,1,0:T(8,128)(2,1)S(1)}, u32[]{:S(2)}, u32[]{:S(2)}) %collective-permute-start.4) | collective-permute-done | bytes 524320 | tf_op jit(solution)/shard_map/ppermute | solution.py:307
  64.3 0.9 %dipole.1 = bf16[256,256]{1,0:T(8,128)(2,1)S(1)} custom-call(bf16[1,2,512,512]{3,2,1,0:T(8,128)(2,1)S(1)} %copy-done, bf16[2,512,256]{2,1,0:T(8,128)(2,1)S(1)} %collective-permute-done.4.right_ref, bf16[2,512,256]{2,1,0:T(8,128)(2,1)S(1)} %left.1.left_ref), custom_call_target="tpu_custom_call" | custom-call | tf_op jit(solution)/shard_map/dipole/pallas_call | solution.py:296
  65.2 16.2 %all_to_all.17 = bf16[32,8,256]{2,1,0:T(8,128)(2,1)S(1)} all-to-all(bf16[32,8,256]{2,1,0:T(8,128)(2,1)S(1)} %bitcast.19), channel_id=1, replica_groups=mesh['sym'=8,'row'=32] {'row'}, dimensions={0} | all-to-all | bytes 262144 | tf_op jit(solution)/shard_map/all_to_all | solution.py:311
  81.4 0.6 convert_reduce_fusion
  (21 shorter events, 0.3 us)
Async XLA Ops:
  0.0 12.4 %collective-permute-start = (s32[2]{0:T(128)}, s32[2]{0:T(128)S(1)}, u32[]{:S(2)}, u32[]{:S(2)}) collective-permute-start(s32[2]{0:T(128)} %bitcast.25), channel_id=1, source_target_pairs={{224,0},{0,32},{32,64},{64,96},{96,128},{128,160},{160,192},{192,2... | collective-permute-start | bytes 32 | tf_op jit(solution)/shard_map/ppermute | solution.py:307
  27.2 23.5 %copy-start.1 = (f32[1,4,128,128]{3,2,1,0:T(8,128)S(1)}, f32[1,4,128,128]{3,2,1,0:T(8,128)}, u32[]{:S(2)}) copy-start(f32[1,4,128,128]{3,2,1,0:T(8,128)} %factor_ref.1) | copy-start | bytes 786436
  27.2 23.5 %copy-start.2 = (s32[1,8]{1,0:T(1,128)S(1)}, s32[1,8]{1,0:T(1,128)}, u32[]{:S(2)}) copy-start(s32[1,8]{1,0:T(1,128)} %param.15) | copy-start | bytes 100
  27.2 12.4 %collective-permute-start.3 = (f16[232,128]{1,0:T(8,128)(2,1)S(1)}, f16[232,128]{1,0:T(8,128)(2,1)S(1)}, u32[]{:S(2)}, u32[]{:S(2)}) collective-permute-start(f16[232,128]{1,0:T(8,128)(2,1)S(1)} %pad_maximum_fusion), channel_id=1, source_target_pairs={{16,0},{17,1},{18,2},{19,3},{20,4},{21,5},{22,6},{23,7},{24,8},{25... | collective-permute-start | bytes 178184 | tf_op jit(solution)/shard_map/ppermute | solution.py:336
  33.3 6.3 %collective-permute-start.2 = (f16[232,128]{1,0:T(8,128)(2,1)S(1)}, f16[232,128]{1,0:T(8,128)(2,1)S(1)}, u32[]{:S(2)}, u32[]{:S(2)}) collective-permute-start(f16[232,128]{1,0:T(8,128)(2,1)S(1)} %pad_maximum_fusion), channel_id=1, source_target_pairs={{24,0},{25,1},{26,2},{27,3},{28,4},{29,5},{30,6},{31,7},{0,8},{1,9... | collective-permute-start | bytes 178184 | tf_op jit(solution)/shard_map/ppermute | solution.py:336
  34.5 5.1 %collective-permute-start.1 = (f16[232,128]{1,0:T(8,128)(2,1)S(1)}, f16[232,128]{1,0:T(8,128)(2,1)S(1)}, u32[]{:S(2)}, u32[]{:S(2)}) collective-permute-start(f16[232,128]{1,0:T(8,128)(2,1)S(1)} %pad_maximum_fusion), channel_id=1, source_target_pairs={{8,0},{9,1},{10,2},{11,3},{12,4},{13,5},{14,6},{15,7},{16,8},{17,9... | collective-permute-start | bytes 178184 | tf_op jit(solution)/shard_map/ppermute | solution.py:336
  36.9 19.4 %copy-start.3 = (s32[1,2]{1,0:T(1,128)S(1)}, s32[1,2]{1,0:T(1,128)}, u32[]{:S(2)}) copy-start(s32[1,2]{1,0:T(1,128)} %param.12) | copy-start | bytes 28
  36.9 19.4 %copy-start.4 = (s32[1,2]{1,0:T(1,128)S(1)}, s32[1,2]{1,0:T(1,128)}, u32[]{:S(2)}) copy-start(s32[1,2]{1,0:T(1,128)} %param.14) | copy-start | bytes 28
  50.7 13.6 %copy-start = (bf16[1,2,512,512]{3,2,1,0:T(8,128)(2,1)S(1)}, bf16[1,2,512,512]{3,2,1,0:T(8,128)(2,1)}, u32[]{:S(2)}) copy-start(bf16[1,2,512,512]{3,2,1,0:T(8,128)(2,1)} %tile_ref.1) | copy-start | bytes 3145732
  53.6 10.7 %collective-permute-start.4 = (bf16[2,512,256]{2,1,0:T(8,128)(2,1)S(1)}, bf16[2,512,256]{2,1,0:T(8,128)(2,1)S(1)}, u32[]{:S(2)}, u32[]{:S(2)}) collective-permute-start(bf16[2,512,256]{2,1,0:T(8,128)(2,1)S(1)} %get-tuple-element.34), channel_id=1, source_target_pairs={{32,0},{64,32},{96,64},{128,96},{160,128},{192,160},{224,192},{0,2... | collective-permute-start | bytes 1572872 | tf_op jit(solution)/shard_map/ppermute | solution.py:307

commit v5 on v4

--- a/solution.py
+++ b/solution.py
@@ -20,6 +20,7 @@
 SHARE = BODY + 8
 COUPLING_SCALE = 32.0
 ROWS = ((0,), (0,))
+PLAIN = ((1,), (0,))
 
 
 def split(x):
@@ -27,34 +28,38 @@
     return high, (x - high.astype(F32)).astype(BF16)
 
 
-def dot(a, b, dims=((1,), (0,))):
+def dot(a, b, dims=PLAIN):
     return lax.dot_general(a, b, (dims, ((), ())), preferred_element_type=F32)
 
 
-def dot3(a, b, dims=((1,), (0,))):
+def dot3(a, b, dims=PLAIN):
     (ah, al), (bh, bl) = a, b
     return dot(ah, bh, dims) + (dot(ah, bl, dims) + dot(al, bh, dims))
 
 
-def gram_kernel(start_ref, panel_ref, out_ref, proj, coup, first):
+def gram_kernel(start_ref, panel_ref, out_ref, proj, coup):
     step = pl.program_id(0)
 
     @pl.when(step == 0)
     def _():
         proj[...] = jnp.zeros_like(proj)
         coup[...] = jnp.zeros_like(coup)
-        first[...] = jnp.zeros_like(first)
 
     panels = split(panel_ref[0])
     start = split(start_ref[0])
     width = panel_ref.shape[2] // 4
 
-    def columns(begin, end):
-        return tuple(p[:, begin * width : end * width] for p in panels)
+    def columns(*which):
+        return tuple(
+            jnp.concatenate([p[:, k * width : (k + 1) * width] for k in which], axis=1)
+            for p in panels
+        )
 
     proj[...] += dot3(panels, start, ROWS)
-    coup[...] += dot3(columns(0, 3), columns(2, 4), ROWS)
-    first[...] += dot3(columns(0, 1), columns(1, 2), ROWS)
+    for place, (one, pair) in enumerate(((0, (1, 2)), (1, (2, 3)), (3, (2, 0)))):
+        coup[place * width : (place + 1) * width] += dot3(
+            columns(one), columns(*pair), ROWS
+        )
 
     @pl.when(step == pl.num_programs(0) - 1)
     def _():
@@ -65,14 +70,7 @@
         count = out_ref.shape[0]
         out_ref[:, :HALF, :] = inner[:, :128].reshape(count, HALF, 128)
         out_ref[:, HALF:PROJ, :] = inner[:, 128:].reshape(count, HALF, 128)
-        lines = jnp.concatenate(
-            [
-                coup[: 2 * width, :width],
-                first[...],
-                coup[:, width:],
-            ],
-            axis=0,
-        )
+        lines = jnp.concatenate([coup[:, :width], coup[:, width:]], axis=0)
         lines = lines * COUPLING_SCALE
         out_ref[:, PROJ:BODY, :] = lines.reshape(count, COUP, 128)
         out_ref[:, BODY:, :] = jnp.broadcast_to(
@@ -95,7 +93,6 @@
         scratch_shapes=[
             pltpu.VMEM((columns, eigen), F32),
             pltpu.VMEM((3 * columns // 4, columns // 2), F32),
-            pltpu.VMEM((columns // 4, columns // 4), F32),
         ],
         compiler_params=pltpu.CompilerParams(vmem_limit_bytes=40 << 20),
         cost_estimate=pl.CostEstimate(
@@ -187,12 +184,16 @@
 
     factors = [split(factor_ref[0, level]) for level in range(4)]
     current = [dot3(factors[level], part(inner, level)) for level in range(4)]
-    places = {3: ((0, 3), (1, 4), (2, 5)), 2: ((0, 0), (1, 1)), 1: ((0, 2),)}
+    turned = ((1,), (1,))
+    places = {
+        3: ((0, 5, turned), (1, 4, PLAIN), (2, 2, turned)),
+        2: ((0, 3, PLAIN), (1, 1, PLAIN)),
+        1: ((0, 0, PLAIN),),
+    }
     chained = {}
-    for later, pairs in places.items():
-        chained[later] = split(
-            jnp.concatenate([dot3(factors[k], part(links, at)) for k, at in pairs], axis=0)
-        )
+    for later, entries in places.items():
+        products = [dot3(factors[k], part(links, at), dims) for k, at, dims in entries]
+        chained[later] = split(jnp.concatenate(products, axis=0))
     parts = [None] * 4
     for level in (3, 2, 1, 0):
         parts[level] = split(current[level])
@@ -209,16 +210,26 @@
 
 
 def left_kernel(
-    left_ref, occupied_ref, limit_ref, upper, lower, start_ref, panel_ref, out_ref
+    left_ref,
+    occupied_ref,
+    limit_ref,
+    upper,
+    lower,
+    start_ref,
+    panel_ref,
+    tile_ref,
+    high_out,
+    low_out,
 ):
     turn = pl.program_id(0)
-    out_ref[0] = updated_block(
+    block = updated_block(
         start_ref[0],
         split(panel_ref[0]),
         upper[...],
         lower[...],
         limit_ref[left_ref[turn]] * occupied_ref[turn],
     )
+    high_out[...], low_out[...] = split(dot(block, tile_ref[0, 0], ROWS))
 
 
 SCALARS = pl.BlockSpec(memory_space=pltpu.SMEM)
@@ -252,7 +263,7 @@
     )(want, limits, sums, exponent, factors, start, high, low)
 
 
-def left_blocks(left, occupied, limits, upper, lower, start, panels):
+def left_products(left, occupied, limits, upper, lower, start, panels, tiles):
     count = left.shape[0]
     eigen, columns = start.shape[2], panels.shape[2]
 
@@ -262,9 +273,10 @@
     def whole(shape):
         return pl.BlockSpec(shape, lambda t, *_: (0, 0))
 
+    wide = pl.BlockSpec((eigen, BLOCK), lambda t, *_: (0, t))
     return pl.pallas_call(
         left_kernel,
-        out_shape=jax.ShapeDtypeStruct((count, BLOCK, eigen), BF16),
+        out_shape=(jax.ShapeDtypeStruct((eigen, count * BLOCK), BF16),) * 2,
         grid_spec=pltpu.PrefetchScalarGridSpec(
             num_scalar_prefetch=3,
             grid=(count,),
@@ -273,32 +285,31 @@
                 whole((columns, eigen)),
                 named(eigen),
                 named(columns),
+                pl.BlockSpec((1, 1, BLOCK, BLOCK), lambda t, *_: (0, t, 0, 0)),
             ],
-            out_specs=pl.BlockSpec((1, BLOCK, eigen), lambda t, *_: (t, 0, 0)),
+            out_specs=(wide, wide),
         ),
         compiler_params=pltpu.CompilerParams(vmem_limit_bytes=16 << 20),
         cost_estimate=update_cost(count, columns, eigen),
         name="left",
-    )(left, occupied, limits, upper, lower, start, panels)
-
-
-def dipole_kernel(tile_ref, right_ref, left_ref, out_ref):
-    total = None
-    for t in range(tile_ref.shape[1]):
-        product = dot(tile_ref[0, t], right_ref[t]).astype(BF16)
-        term = dot(left_ref[t], product, ((0,), (0,)))
-        total = term if total is None else total + term
-    out_ref[...] = total.astype(BF16)
-
-
-def tile_products(tiles, right, left):
+    )(left, occupied, limits, upper, lower, start, panels, tiles)
+
+
+def dipole_kernel(high_ref, low_ref, right_ref, out_ref):
+    right = right_ref[...].reshape(-1, right_ref.shape[2])
+    out_ref[...] = (dot(high_ref[...], right) + dot(low_ref[...], right)).astype(BF16)
+
+
+def tile_products(high, low, right):
     eigen = right.shape[2]
     return pl.pallas_call(
         dipole_kernel,
         out_shape=jax.ShapeDtypeStruct((eigen, eigen), BF16),
+        in_specs=[ARRAY] * 3,
+        out_specs=ARRAY,
         compiler_params=pltpu.CompilerParams(vmem_limit_bytes=8 << 20),
         name="dipole",
-    )(tiles, right, left)
+    )(high, low, right)
 
 
 def passed_along(block, axis, distance):
@@ -360,10 +371,17 @@
         want, channels[0], sums, exponent, factors, *named
     )
     right = passed_along(packed, "sym", -1)
-    left = left_blocks(
-        tile_left[0], tile_occupied_mask[0], channels[0], upper, lower, vectors, reflectors
-    )
-    partial = tile_products(tiles, right, left)
+    left = left_products(
+        tile_left[0],
+        tile_occupied_mask[0],
+        channels[0],
+        upper,
+        lower,
+        vectors,
+        reflectors,
+        tiles,
+    )
+    partial = tile_products(*left, right)
     eigen = partial.shape[1]
     owned = exchanged(partial.reshape(count, eigen // count, eigen))
     return jnp.sum(owned.astype(F32), axis=0)[None]

time: 82.3 us -> 81.3 us (0.988)
  waiting for transfers between devices: 4.77 us -> 3.73 us
    ppermute x2, waiting for transfers between devices: 4.76 us -> 3.72 us  [passed_along(): return lax.ppermute(block, axis, route)]
    pallas_call x1, Pallas kernels: 3.19 us -> 4.23 us  [left_products(): pl.pallas_call(left_kernel, out_shape=(jax.ShapeDtypeStruct((eigen, count...]
  transfers between devices with their start and end apart: 5 -> 5, of which waited for: 1 -> 1; matrix products, arithmetic and copies ran while one was open for 0% -> 0% of each run, Pallas kernels for 19% -> 20%
where the time goes in v5:
time: 81.3 us; the launch traced here: 81 us
  blocking collectives  41.5 us (51%)
  Pallas kernels  19.4 us (24%)
  starting transfers between devices  15 us (18%)
  waiting for transfers between devices  3.73 us (5%)
  other arithmetic  1.13 us (1%)
    all_to_all x3, blocking collectives, exchanged(): lax.all_to_all(shares, 'row', 0, 0, axis_index_groups=groups, tiled=True)  41.5 us
    ppermute x3, starting transfers between devices, around(): return lax.ppermute(share, 'row', route)  9.63 us
    pallas_call x1, Pallas kernels, local_grams(): pl.pallas_call(gram_kernel, out_shape=jax.ShapeDtypeStruct((count, SHARE,...  9.11 us
    ppermute x2, starting transfers between devices, passed_along(): return lax.ppermute(block, axis, route)  5.32 us
    pallas_call x1, Pallas kernels, left_products(): pl.pallas_call(left_kernel, out_shape=(jax.ShapeDtypeStruct((eigen, count...  4.23 us
    ppermute x2, waiting for transfers between devices, passed_along(): return lax.ppermute(block, axis, route)  3.72 us
    pallas_call x1, Pallas kernels, solve_and_update(): pl.pallas_call(solve_kernel, out_shape=(jax.ShapeDtypeStruct((count, BLOC...  2.96 us
    pallas_call x1, Pallas kernels, fetched_blocks(): pl.pallas_call(fetch_kernel, out_shape=(jax.ShapeDtypeStruct((count, BLOC...  2.63 us
  transfers between devices with their start and end apart: 5, of which 1 were waited for; matrix products, arithmetic and copies ran while one was open for 0% of the time, Pallas kernels for 20%

profile of v5, /device:TPU:1, one launch (start us, length us, event | category | flops | bytes accessed | tf_op | source)
XLA Modules:
  0.0 81.0 jit_solution(16015420855653997894)
XLA Ops:
  0.0 2.6 %collective-permute-start = (s32[2]{0:T(128)}, s32[2]{0:T(128)S(1)}, u32[]{:S(2)}, u32[]{:S(2)}) collective-permute-start(s32[2]{0:T(128)} %bitcast.25), channel_id=1, source_target_pairs={{224,0},{0,32},{32,64},{64,96},{96,128},{128,160},{160,192},{192,2... | collective-permute-start | bytes 32 | tf_op jit(solution)/shard_map/ppermute | solution.py:318
  2.6 9.1 %grams.1 = f32[8,232,128]{2,1,0:T(8,128)S(1)} custom-call(f32[1,4096,256]{2,1,0:T(8,128)} %start_ref.5, f32[1,4096,512]{2,1,0:T(8,128)} %panel_ref.5), custom_call_target="tpu_custom_call" | custom-call | flops 6442450944 | bytes 12582912 | tf_op jit(solution)/shard_map/grams/pallas_call | solution.py:84
  11.7 0.1 convert_element_type.26
  11.8 0.0 collective-permute-done.which_ref.want_ref
  11.8 14.6 %all_to_all.15 = f16[8,232,128]{2,1,0:T(8,128)(2,1)S(1)} all-to-all(f16[8,232,128]{2,1,0:T(8,128)(2,1)S(1)} %convert_element_type.26), channel_id=1, replica_groups={{0,1,2,3,4,5,6,7},{8,9,10,11,12,13,14,15},{16,17,18,19,20,21,22,23},{24..., dimensions={0} | all-to-all | bytes 950272 | tf_op jit(solution)/shard_map/all_to_all | solution.py:322
  26.4 0.1 convert_element_type.27
  26.7 0.0 copy-start.1
  26.7 0.0 copy-start.2
  26.7 6.1 %collective-permute-start.3 = (f16[232,128]{1,0:T(8,128)(2,1)S(1)}, f16[232,128]{1,0:T(8,128)(2,1)S(1)}, u32[]{:S(2)}, u32[]{:S(2)}) collective-permute-start(f16[232,128]{1,0:T(8,128)(2,1)S(1)} %pad_maximum_fusion), channel_id=1, source_target_pairs={{16,0},{17,1},{18,2},{19,3},{20,4},{21,5},{22,6},{23,7},{24,8},{25... | collective-permute-start | bytes 178184 | tf_op jit(solution)/shard_map/ppermute | solution.py:347
  32.7 1.2 %collective-permute-start.2 = (f16[232,128]{1,0:T(8,128)(2,1)S(1)}, f16[232,128]{1,0:T(8,128)(2,1)S(1)}, u32[]{:S(2)}, u32[]{:S(2)}) collective-permute-start(f16[232,128]{1,0:T(8,128)(2,1)S(1)} %pad_maximum_fusion), channel_id=1, source_target_pairs={{24,0},{25,1},{26,2},{27,3},{28,4},{29,5},{30,6},{31,7},{0,8},{1,9... | collective-permute-start | bytes 178184 | tf_op jit(solution)/shard_map/ppermute | solution.py:347
  33.9 2.4 %collective-permute-start.1 = (f16[232,128]{1,0:T(8,128)(2,1)S(1)}, f16[232,128]{1,0:T(8,128)(2,1)S(1)}, u32[]{:S(2)}, u32[]{:S(2)}) collective-permute-start(f16[232,128]{1,0:T(8,128)(2,1)S(1)} %pad_maximum_fusion), channel_id=1, source_target_pairs={{8,0},{9,1},{10,2},{11,3},{12,4},{13,5},{14,6},{15,7},{16,8},{17,9... | collective-permute-start | bytes 178184 | tf_op jit(solution)/shard_map/ppermute | solution.py:347
  36.3 0.0 copy-start
  36.4 0.0 copy-start.3
  36.4 0.0 copy-start.4
  36.4 2.6 %fetch.1 = (f32[2,512,256]{2,1,0:T(8,128)S(1)}, bf16[2,512,512]{2,1,0:T(8,128)(2,1)S(1)}, bf16[2,512,512]{2,1,0:T(8,128)(2,1)S(1)}) custom-call(s32[2]{0:T(128)S(1)} %collective-permute-done.which_ref.want_ref, f32[1,4096,256]{2,1,0:T(8,128)} %start_ref.5, f32[1,4096,512]{2,1,0:T(8,128)} %panel_ref.5), custom_call_target="tpu_custom_call" | custom-call | flops 524288 | bytes 6291456 | tf_op jit(solution)/shard_map/fetch/pallas_call | solution.py:124
  39.0 0.0 collective-permute-done.3
  39.0 0.0 collective-permute-done.2
  39.0 0.0 collective-permute-done.1
  39.2 0.1 broadcast_in_dim.6
  39.3 10.7 %all_to_all.16 = f16[8,224,128]{2,1,0:T(8,128)(2,1)S(1)} all-to-all(f16[8,224,128]{2,1,0:T(8,128)(2,1)S(1)} %broadcast_in_dim.6), channel_id=1, replica_groups={{0,1,2,3,4,5,6,7},{8,9,10,11,12,13,14,15},{16,17,18,19,20,21,22,23},{24..., dimensions={0} | all-to-all | bytes 917504 | tf_op jit(solution)/shard_map/all_to_all | solution.py:322
  50.1 0.1 convert_element_type.32.sums_ref
  50.1 0.0 copy-done.1
  50.1 0.0 copy-done.2
  50.1 3.0 %solve.1 = (bf16[2,512,256]{2,1,0:T(8,128)(2,1)S(1)}, bf16[512,256]{1,0:T(8,128)(2,1)S(1)}, bf16[512,256]{1,0:T(8,128)(2,1)S(1)}) custom-call(s32[2]{0:T(128)S(1)} %collective-permute-done.which_ref.want_ref, s32[8]{0:T(128)S(1)} %bitcast.20, f32[8,224,128]{2,1,0:T(8,128)S(1)} %convert_element_type.32.sums_ref, f32[8,128]{1,0:T(8,128)S(1)} %fusion.8.exponent_ref, ...), custom_call_target="tpu_custom_call" | custom-call | flops 805306368 | bytes 3145728 | tf_op jit(solution)/shard_map/solve/pallas_call | solution.py:251
  53.1 2.7 %collective-permute-start.4 = (bf16[2,512,256]{2,1,0:T(8,128)(2,1)S(1)}, bf16[2,512,256]{2,1,0:T(8,128)(2,1)S(1)}, u32[]{:S(2)}, u32[]{:S(2)}) collective-permute-start(bf16[2,512,256]{2,1,0:T(8,128)(2,1)S(1)} %get-tuple-element.40), channel_id=1, source_target_pairs={{32,0},{64,32},{96,64},{128,96},{160,128},{192,160},{224,192},{0,2... | collective-permute-start | bytes 1572872 | tf_op jit(solution)/shard_map/ppermute | solution.py:318
  55.8 0.0 copy-done
  55.8 0.0 copy-done.4
  55.8 4.2 %left.1 = (bf16[256,1024]{1,0:T(8,128)(2,1)S(1)}, bf16[256,1024]{1,0:T(8,128)(2,1)S(1)}) custom-call(s32[2]{0:T(128)S(1)} %bitcast.22, s32[2]{0:T(128)S(1)} %bitcast.23, s32[8]{0:T(128)S(1)} %bitcast.21, bf16[512,256]{1,0:T(8,128)(2,1)S(1)} %get-tuple-element.36.upper, bf16[512,256]{1,0:T(8,128)(2,1)S(1)} %get-tuple-element.37.lower, ...), custom_call_target="tpu_custom_call" | custom-call | flops 805306368 | bytes 3145728 | tf_op jit(solution)/shard_map/left/pallas_call | solution.py:277
  60.1 3.7 %collective-permute-done.4.right_ref = bf16[2,512,256]{2,1,0:T(8,128)(2,1)S(1)} collective-permute-done((bf16[2,512,256]{2,1,0:T(8,128)(2,1)S(1)}, bf16[2,512,256]{2,1,0:T(8,128)(2,1)S(1)}, u32[]{:S(2)}, u32[]{:S(2)}) %collective-permute-start.4) | collective-permute-done | bytes 524320 | tf_op jit(solution)/shard_map/ppermute | solution.py:318
  63.8 0.4 dipole.1
  64.2 16.2 %all_to_all.17 = bf16[32,8,256]{2,1,0:T(8,128)(2,1)S(1)} all-to-all(bf16[32,8,256]{2,1,0:T(8,128)(2,1)S(1)} %bitcast.19), channel_id=1, replica_groups=mesh['sym'=8,'row'=32] {'row'}, dimensions={0} | all-to-all | bytes 262144 | tf_op jit(solution)/shard_map/all_to_all | solution.py:322
  80.4 0.6 convert_reduce_fusion
  (21 shorter events, 0.3 us)
Async XLA Ops:
  0.0 11.8 %collective-permute-start = (s32[2]{0:T(128)}, s32[2]{0:T(128)S(1)}, u32[]{:S(2)}, u32[]{:S(2)}) collective-permute-start(s32[2]{0:T(128)} %bitcast.25), channel_id=1, source_target_pairs={{224,0},{0,32},{32,64},{64,96},{96,128},{128,160},{160,192},{192,2... | collective-permute-start | bytes 32 | tf_op jit(solution)/shard_map/ppermute | solution.py:318
  26.7 23.5 %copy-start.1 = (f32[1,4,128,128]{3,2,1,0:T(8,128)S(1)}, f32[1,4,128,128]{3,2,1,0:T(8,128)}, u32[]{:S(2)}) copy-start(f32[1,4,128,128]{3,2,1,0:T(8,128)} %factor_ref.1) | copy-start | bytes 786436
  26.7 23.5 %copy-start.2 = (s32[1,8]{1,0:T(1,128)S(1)}, s32[1,8]{1,0:T(1,128)}, u32[]{:S(2)}) copy-start(s32[1,8]{1,0:T(1,128)} %param.15) | copy-start | bytes 100
  26.7 12.3 %collective-permute-start.3 = (f16[232,128]{1,0:T(8,128)(2,1)S(1)}, f16[232,128]{1,0:T(8,128)(2,1)S(1)}, u32[]{:S(2)}, u32[]{:S(2)}) collective-permute-start(f16[232,128]{1,0:T(8,128)(2,1)S(1)} %pad_maximum_fusion), channel_id=1, source_target_pairs={{16,0},{17,1},{18,2},{19,3},{20,4},{21,5},{22,6},{23,7},{24,8},{25... | collective-permute-start | bytes 178184 | tf_op jit(solution)/shard_map/ppermute | solution.py:347
  32.7 6.3 %collective-permute-start.2 = (f16[232,128]{1,0:T(8,128)(2,1)S(1)}, f16[232,128]{1,0:T(8,128)(2,1)S(1)}, u32[]{:S(2)}, u32[]{:S(2)}) collective-permute-start(f16[232,128]{1,0:T(8,128)(2,1)S(1)} %pad_maximum_fusion), channel_id=1, source_target_pairs={{24,0},{25,1},{26,2},{27,3},{28,4},{29,5},{30,6},{31,7},{0,8},{1,9... | collective-permute-start | bytes 178184 | tf_op jit(solution)/shard_map/ppermute | solution.py:347
  33.9 5.1 %collective-permute-start.1 = (f16[232,128]{1,0:T(8,128)(2,1)S(1)}, f16[232,128]{1,0:T(8,128)(2,1)S(1)}, u32[]{:S(2)}, u32[]{:S(2)}) collective-permute-start(f16[232,128]{1,0:T(8,128)(2,1)S(1)} %pad_maximum_fusion), channel_id=1, source_target_pairs={{8,0},{9,1},{10,2},{11,3},{12,4},{13,5},{14,6},{15,7},{16,8},{17,9... | collective-permute-start | bytes 178184 | tf_op jit(solution)/shard_map/ppermute | solution.py:347
  36.3 19.5 %copy-start = (bf16[1,2,512,512]{3,2,1,0:T(8,128)(2,1)S(1)}, bf16[1,2,512,512]{3,2,1,0:T(8,128)(2,1)}, u32[]{:S(2)}) copy-start(bf16[1,2,512,512]{3,2,1,0:T(8,128)(2,1)} %tile_ref.1) | copy-start | bytes 3145732
  36.4 19.5 %copy-start.3 = (s32[1,2]{1,0:T(1,128)S(1)}, s32[1,2]{1,0:T(1,128)}, u32[]{:S(2)}) copy-start(s32[1,2]{1,0:T(1,128)} %param.12) | copy-start | bytes 28
  36.4 19.5 %copy-start.4 = (s32[1,2]{1,0:T(1,128)S(1)}, s32[1,2]{1,0:T(1,128)}, u32[]{:S(2)}) copy-start(s32[1,2]{1,0:T(1,128)} %param.14) | copy-start | bytes 28
  53.1 10.7 %collective-permute-start.4 = (bf16[2,512,256]{2,1,0:T(8,128)(2,1)S(1)}, bf16[2,512,256]{2,1,0:T(8,128)(2,1)S(1)}, u32[]{:S(2)}, u32[]{:S(2)}) collective-permute-start(bf16[2,512,256]{2,1,0:T(8,128)(2,1)S(1)} %get-tuple-element.40), channel_id=1, source_target_pairs={{32,0},{64,32},{96,64},{128,96},{160,128},{192,160},{224,192},{0,2... | collective-permute-start | bytes 1572872 | tf_op jit(solution)/shard_map/ppermute | solution.py:318

commit v6 on v5

--- a/solution.py
+++ b/solution.py
@@ -144,11 +144,12 @@
     )(which, start, panels)
 
 
-def updated_block(start, panels, upper, lower, limit):
+def updated_block(start, panels, upper, lower, limits):
     high, low = panels
     back = start - (dot(high, upper) + (dot(high, lower) + dot(low, upper)))
-    line = lax.broadcasted_iota(jnp.int32, back.shape, 0)
-    return jnp.where(line < limit, back, 0.0).astype(BF16)
+    line = lax.broadcasted_iota(jnp.int32, (BLOCK, back.shape[1]), 0)
+    live = jnp.concatenate([line < limit for limit in limits], axis=0)
+    return jnp.where(live, back, 0.0).astype(BF16)
 
 
 def solve_kernel(
@@ -203,10 +204,16 @@
                 current[k] = current[k] - moved[k * width : (k + 1) * width]
     upper[...] = jnp.concatenate([p[0] for p in parts], axis=0)
     lower[...] = jnp.concatenate([p[1] for p in parts], axis=0)
-    for t in range(out_ref.shape[0]):
-        out_ref[t] = updated_block(
-            start_ref[t], (high_ref[t], low_ref[t]), upper[...], lower[...], limit_ref[want_ref[t]]
-        )
+    shape = out_ref.shape
+    limits = [limit_ref[want_ref[t]] for t in range(shape[0])]
+    tall = (shape[0] * shape[1], -1)
+    out_ref[...] = updated_block(
+        start_ref[...].reshape(tall),
+        (high_ref[...].reshape(tall), low_ref[...].reshape(tall)),
+        upper[...],
+        lower[...],
+        limits,
+    ).reshape(shape)
 
 
 def left_kernel(
@@ -227,7 +234,7 @@
         split(panel_ref[0]),
         upper[...],
         lower[...],
-        limit_ref[left_ref[turn]] * occupied_ref[turn],
+        [limit_ref[left_ref[turn]] * occupied_ref[turn]],
     )
     high_out[...], low_out[...] = split(dot(block, tile_ref[0, 0], ROWS))
 
@@ -322,23 +329,17 @@
     return lax.all_to_all(shares, "row", 0, 0, axis_index_groups=groups, tiled=True)
 
 
-def combined(terms):
-    count = terms.shape[0]
-    terms = terms.astype(F32)
-    exponents = terms[:, BODY:]
-    proj = jnp.sum(terms[:, :PROJ] * jnp.exp2(exponents[:, :1]), axis=0)
-    coup = jnp.sum(terms[:, PROJ:BODY], axis=0) * (1.0 / count)
-    exponent = jnp.max(exponents, axis=0) + float(count.bit_length() - 1)
-    return jnp.concatenate([proj * jnp.exp2(-exponent[:1]), coup, exponent], axis=0)
-
-
-def added(shares):
+def combined(shares):
+    shares = [share.astype(F32) for share in shares]
     exponents = [share[BODY:] for share in shares]
-    proj = sum(s[:PROJ] * jnp.exp2(e[:1]) for s, e in zip(shares, exponents))
-    coup = sum(s[PROJ:BODY] for s in shares) * (1.0 / len(shares))
     exponent = functools.reduce(jnp.maximum, exponents)
     exponent = exponent + float(len(shares).bit_length() - 1)
-    return jnp.concatenate([proj * jnp.exp2(-exponent[:1]), coup, exponent], axis=0)
+    proj = sum(
+        share[:PROJ] * jnp.exp2(own[:1] - exponent[:1])
+        for share, own in zip(shares, exponents)
+    )
+    coup = sum(share[PROJ:BODY] for share in shares) * (1.0 / len(shares))
+    return jnp.concatenate([proj, coup], axis=0), exponent
 
 
 def around(share, step):
@@ -358,15 +359,16 @@
     inside = [[far_at * NEAR + at for at in range(NEAR)] for far_at in range(far)]
     shares = local_grams(vectors, reflectors, NEAR).astype(F16)
     want, shares = lax.optimization_barrier((want, shares))
-    owned = combined(exchanged(shares, inside)).astype(F16)
+    terms = exchanged(shares, inside)
+    owned = jnp.concatenate(combined([terms[at] for at in range(NEAR)]), axis=0)
+    owned = owned.astype(F16)
     want, owned = lax.optimization_barrier((want, owned))
     named = fetched_blocks(want, vectors, reflectors)
     others = [around(owned, NEAR * step) for step in (1, far - 1, *range(2, far - 1))]
     others, named = lax.optimization_barrier((others, named))
-    owned = added([share.astype(F32) for share in (owned, *others)])
-    copies = jnp.broadcast_to(owned[:BODY].astype(F16), (NEAR, BODY, 128))
+    body, exponent = combined([owned, *others])
+    copies = jnp.broadcast_to(body.astype(F16), (NEAR, BODY, 128))
     sums = exchanged(copies, inside).astype(F32)
-    exponent = owned[BODY:]
     packed, upper, lower = solve_and_update(
         want, channels[0], sums, exponent, factors, *named
     )

time: 81.3 us -> 81.3 us (level)
  no operation moved by 1% of the time
where the time goes in v6:
time: 81.3 us; the launch traced here: 81 us
  blocking collectives  41.5 us (51%)
  Pallas kernels  19.4 us (24%)
  starting transfers between devices  14.9 us (18%)
  waiting for transfers between devices  3.72 us (5%)
  other arithmetic  1.13 us (1%)
    all_to_all x3, blocking collectives, exchanged(): lax.all_to_all(shares, 'row', 0, 0, axis_index_groups=groups, tiled=True)  41.5 us
    ppermute x3, starting transfers between devices, around(): return lax.ppermute(share, 'row', route)  9.63 us
    pallas_call x1, Pallas kernels, local_grams(): pl.pallas_call(gram_kernel, out_shape=jax.ShapeDtypeStruct((count, SHARE,...  9.11 us
    ppermute x2, starting transfers between devices, passed_along(): return lax.ppermute(block, axis, route)  5.31 us
    pallas_call x1, Pallas kernels, left_products(): pl.pallas_call(left_kernel, out_shape=(jax.ShapeDtypeStruct((eigen, count...  4.23 us
    ppermute x2, waiting for transfers between devices, passed_along(): return lax.ppermute(block, axis, route)  3.71 us
    pallas_call x1, Pallas kernels, solve_and_update(): pl.pallas_call(solve_kernel, out_shape=(jax.ShapeDtypeStruct((count, BLOC...  2.99 us
    pallas_call x1, Pallas kernels, fetched_blocks(): pl.pallas_call(fetch_kernel, out_shape=(jax.ShapeDtypeStruct((count, BLOC...  2.63 us
  transfers between devices with their start and end apart: 5, of which 1 were waited for; matrix products, arithmetic and copies ran while one was open for 0% of the time, Pallas kernels for 20%

profile of v6, /device:TPU:1, one launch (start us, length us, event | category | flops | bytes accessed | tf_op | source)
XLA Modules:
  0.0 81.0 jit_solution(2450190679098864008)
XLA Ops:
  0.0 2.6 %collective-permute-start = (s32[2]{0:T(128)}, s32[2]{0:T(128)S(1)}, u32[]{:S(2)}, u32[]{:S(2)}) collective-permute-start(s32[2]{0:T(128)} %bitcast.101), channel_id=1, source_target_pairs={{224,0},{0,32},{32,64},{64,96},{96,128},{128,160},{160,192},{192,2... | collective-permute-start | bytes 32 | tf_op jit(solution)/shard_map/ppermute | solution.py:325
  2.6 9.1 %grams.1 = f32[8,232,128]{2,1,0:T(8,128)S(1)} custom-call(f32[1,4096,256]{2,1,0:T(8,128)} %start_ref.5, f32[1,4096,512]{2,1,0:T(8,128)} %panel_ref.5), custom_call_target="tpu_custom_call" | custom-call | flops 6442450944 | bytes 12582912 | tf_op jit(solution)/shard_map/grams/pallas_call | solution.py:84
  11.7 0.1 convert_element_type.55
  11.8 0.0 collective-permute-done.which_ref.want_ref
  11.8 14.6 %all_to_all.15 = f16[8,232,128]{2,1,0:T(8,128)(2,1)S(1)} all-to-all(f16[8,232,128]{2,1,0:T(8,128)(2,1)S(1)} %convert_element_type.55), channel_id=1, replica_groups={{0,1,2,3,4,5,6,7},{8,9,10,11,12,13,14,15},{16,17,18,19,20,21,22,23},{24..., dimensions={0} | all-to-all | bytes 950272 | tf_op jit(solution)/shard_map/all_to_all | solution.py:329
  26.4 0.1 slice_convert_fusion.7
  26.5 0.1 fusion.6
  26.6 0.0 copy-start.1
  26.6 0.0 copy-start.2
  26.7 6.1 %collective-permute-start.3 = (f16[232,128]{1,0:T(8,128)(2,1)S(1)}, f16[232,128]{1,0:T(8,128)(2,1)S(1)}, u32[]{:S(2)}, u32[]{:S(2)}) collective-permute-start(f16[232,128]{1,0:T(8,128)(2,1)S(1)} %pad_maximum_fusion), channel_id=1, source_target_pairs={{16,0},{17,1},{18,2},{19,3},{20,4},{21,5},{22,6},{23,7},{24,8},{25... | collective-permute-start | bytes 178184 | tf_op jit(solution)/shard_map/ppermute | solution.py:348
  32.7 1.2 %collective-permute-start.2 = (f16[232,128]{1,0:T(8,128)(2,1)S(1)}, f16[232,128]{1,0:T(8,128)(2,1)S(1)}, u32[]{:S(2)}, u32[]{:S(2)}) collective-permute-start(f16[232,128]{1,0:T(8,128)(2,1)S(1)} %pad_maximum_fusion), channel_id=1, source_target_pairs={{24,0},{25,1},{26,2},{27,3},{28,4},{29,5},{30,6},{31,7},{0,8},{1,9... | collective-permute-start | bytes 178184 | tf_op jit(solution)/shard_map/ppermute | solution.py:348
  33.9 2.4 %collective-permute-start.1 = (f16[232,128]{1,0:T(8,128)(2,1)S(1)}, f16[232,128]{1,0:T(8,128)(2,1)S(1)}, u32[]{:S(2)}, u32[]{:S(2)}) collective-permute-start(f16[232,128]{1,0:T(8,128)(2,1)S(1)} %pad_maximum_fusion), channel_id=1, source_target_pairs={{8,0},{9,1},{10,2},{11,3},{12,4},{13,5},{14,6},{15,7},{16,8},{17,9... | collective-permute-start | bytes 178184 | tf_op jit(solution)/shard_map/ppermute | solution.py:348
  36.3 0.0 copy-start
  36.3 0.0 copy-start.3
  36.3 0.0 copy-start.4
  36.3 2.6 %fetch.1 = (f32[2,512,256]{2,1,0:T(8,128)S(1)}, bf16[2,512,512]{2,1,0:T(8,128)(2,1)S(1)}, bf16[2,512,512]{2,1,0:T(8,128)(2,1)S(1)}) custom-call(s32[2]{0:T(128)S(1)} %collective-permute-done.which_ref.want_ref, f32[1,4096,256]{2,1,0:T(8,128)} %start_ref.5, f32[1,4096,512]{2,1,0:T(8,128)} %panel_ref.5), custom_call_target="tpu_custom_call" | custom-call | flops 524288 | bytes 6291456 | tf_op jit(solution)/shard_map/fetch/pallas_call | solution.py:124
  39.0 0.0 collective-permute-done.3
  39.0 0.0 collective-permute-done.2
  39.0 0.0 collective-permute-done.1
  39.2 0.1 broadcast_in_dim.6
  39.3 10.7 %all_to_all.16 = f16[8,224,128]{2,1,0:T(8,128)(2,1)S(1)} all-to-all(f16[8,224,128]{2,1,0:T(8,128)(2,1)S(1)} %broadcast_in_dim.6), channel_id=1, replica_groups={{0,1,2,3,4,5,6,7},{8,9,10,11,12,13,14,15},{16,17,18,19,20,21,22,23},{24..., dimensions={0} | all-to-all | bytes 917504 | tf_op jit(solution)/shard_map/all_to_all | solution.py:329
  50.0 0.1 convert_element_type.68.sums_ref
  50.1 0.0 copy-done.1
  50.1 0.0 copy-done.2
  50.1 3.0 %solve.1 = (bf16[2,512,256]{2,1,0:T(8,128)(2,1)S(1)}, bf16[512,256]{1,0:T(8,128)(2,1)S(1)}, bf16[512,256]{1,0:T(8,128)(2,1)S(1)}) custom-call(s32[2]{0:T(128)S(1)} %collective-permute-done.which_ref.want_ref, s32[8]{0:T(128)S(1)} %bitcast.97, f32[8,224,128]{2,1,0:T(8,128)S(1)} %convert_element_type.68.sums_ref, f32[8,128]{1,0:T(8,128)S(1)} %fusion.25.exponent_ref, ...), custom_call_target="tpu_custom_call" | custom-call | flops 805306368 | bytes 3145728 | tf_op jit(solution)/shard_map/solve/pallas_call | solution.py:258
  53.1 2.7 %collective-permute-start.4 = (bf16[2,512,256]{2,1,0:T(8,128)(2,1)S(1)}, bf16[2,512,256]{2,1,0:T(8,128)(2,1)S(1)}, u32[]{:S(2)}, u32[]{:S(2)}) collective-permute-start(bf16[2,512,256]{2,1,0:T(8,128)(2,1)S(1)} %get-tuple-element.40), channel_id=1, source_target_pairs={{32,0},{64,32},{96,64},{128,96},{160,128},{192,160},{224,192},{0,2... | collective-permute-start | bytes 1572872 | tf_op jit(solution)/shard_map/ppermute | solution.py:325
  55.8 0.0 copy-done
  55.8 4.2 %left.1 = (bf16[256,1024]{1,0:T(8,128)(2,1)S(1)}, bf16[256,1024]{1,0:T(8,128)(2,1)S(1)}) custom-call(s32[2]{0:T(128)S(1)} %bitcast.99, s32[2]{0:T(128)S(1)} %bitcast.100, s32[8]{0:T(128)S(1)} %bitcast.98, bf16[512,256]{1,0:T(8,128)(2,1)S(1)} %get-tuple-element.36.upper, bf16[512,256]{1,0:T(8,128)(2,1)S(1)} %get-tuple-element.37.lower, ...), custom_call_target="tpu_custom_call" | custom-call | flops 805306368 | bytes 3145728 | tf_op jit(solution)/shard_map/left/pallas_call | solution.py:284
  60.0 3.7 %collective-permute-done.4.right_ref = bf16[2,512,256]{2,1,0:T(8,128)(2,1)S(1)} collective-permute-done((bf16[2,512,256]{2,1,0:T(8,128)(2,1)S(1)}, bf16[2,512,256]{2,1,0:T(8,128)(2,1)S(1)}, u32[]{:S(2)}, u32[]{:S(2)}) %collective-permute-start.4) | collective-permute-done | bytes 524320 | tf_op jit(solution)/shard_map/ppermute | solution.py:325
  63.7 0.4 dipole.1
  64.2 16.2 %all_to_all.17 = bf16[32,8,256]{2,1,0:T(8,128)(2,1)S(1)} all-to-all(bf16[32,8,256]{2,1,0:T(8,128)(2,1)S(1)} %bitcast.96), channel_id=1, replica_groups=mesh['sym'=8,'row'=32] {'row'}, dimensions={0} | all-to-all | bytes 262144 | tf_op jit(solution)/shard_map/all_to_all | solution.py:329
  80.4 0.6 convert_reduce_fusion
  (15 shorter events, 0.2 us)
Async XLA Ops:
  0.0 11.8 %collective-permute-start = (s32[2]{0:T(128)}, s32[2]{0:T(128)S(1)}, u32[]{:S(2)}, u32[]{:S(2)}) collective-permute-start(s32[2]{0:T(128)} %bitcast.101), channel_id=1, source_target_pairs={{224,0},{0,32},{32,64},{64,96},{96,128},{128,160},{160,192},{192,2... | collective-permute-start | bytes 32 | tf_op jit(solution)/shard_map/ppermute | solution.py:325
  26.6 23.4 %copy-start.1 = (f32[1,4,128,128]{3,2,1,0:T(8,128)S(1)}, f32[1,4,128,128]{3,2,1,0:T(8,128)}, u32[]{:S(2)}) copy-start(f32[1,4,128,128]{3,2,1,0:T(8,128)} %factor_ref.1) | copy-start | bytes 786436
  26.6 23.4 %copy-start.2 = (s32[1,8]{1,0:T(1,128)S(1)}, s32[1,8]{1,0:T(1,128)}, u32[]{:S(2)}) copy-start(s32[1,8]{1,0:T(1,128)} %param.15) | copy-start | bytes 100
  26.7 12.3 %collective-permute-start.3 = (f16[232,128]{1,0:T(8,128)(2,1)S(1)}, f16[232,128]{1,0:T(8,128)(2,1)S(1)}, u32[]{:S(2)}, u32[]{:S(2)}) collective-permute-start(f16[232,128]{1,0:T(8,128)(2,1)S(1)} %pad_maximum_fusion), channel_id=1, source_target_pairs={{16,0},{17,1},{18,2},{19,3},{20,4},{21,5},{22,6},{23,7},{24,8},{25... | collective-permute-start | bytes 178184 | tf_op jit(solution)/shard_map/ppermute | solution.py:348
  32.7 6.3 %collective-permute-start.2 = (f16[232,128]{1,0:T(8,128)(2,1)S(1)}, f16[232,128]{1,0:T(8,128)(2,1)S(1)}, u32[]{:S(2)}, u32[]{:S(2)}) collective-permute-start(f16[232,128]{1,0:T(8,128)(2,1)S(1)} %pad_maximum_fusion), channel_id=1, source_target_pairs={{24,0},{25,1},{26,2},{27,3},{28,4},{29,5},{30,6},{31,7},{0,8},{1,9... | collective-permute-start | bytes 178184 | tf_op jit(solution)/shard_map/ppermute | solution.py:348
  33.9 5.1 %collective-permute-start.1 = (f16[232,128]{1,0:T(8,128)(2,1)S(1)}, f16[232,128]{1,0:T(8,128)(2,1)S(1)}, u32[]{:S(2)}, u32[]{:S(2)}) collective-permute-start(f16[232,128]{1,0:T(8,128)(2,1)S(1)} %pad_maximum_fusion), channel_id=1, source_target_pairs={{8,0},{9,1},{10,2},{11,3},{12,4},{13,5},{14,6},{15,7},{16,8},{17,9... | collective-permute-start | bytes 178184 | tf_op jit(solution)/shard_map/ppermute | solution.py:348
  36.3 19.5 %copy-start = (bf16[1,2,512,512]{3,2,1,0:T(8,128)(2,1)S(1)}, bf16[1,2,512,512]{3,2,1,0:T(8,128)(2,1)}, u32[]{:S(2)}) copy-start(bf16[1,2,512,512]{3,2,1,0:T(8,128)(2,1)} %tile_ref.1) | copy-start | bytes 3145732
  36.3 19.5 %copy-start.3 = (s32[1,2]{1,0:T(1,128)S(1)}, s32[1,2]{1,0:T(1,128)}, u32[]{:S(2)}) copy-start(s32[1,2]{1,0:T(1,128)} %param.12) | copy-start | bytes 28
  36.3 19.5 %copy-start.4 = (s32[1,2]{1,0:T(1,128)S(1)}, s32[1,2]{1,0:T(1,128)}, u32[]{:S(2)}) copy-start(s32[1,2]{1,0:T(1,128)} %param.14) | copy-start | bytes 28
  53.1 10.7 %collective-permute-start.4 = (bf16[2,512,256]{2,1,0:T(8,128)(2,1)S(1)}, bf16[2,512,256]{2,1,0:T(8,128)(2,1)S(1)}, u32[]{:S(2)}, u32[]{:S(2)}) collective-permute-start(bf16[2,512,256]{2,1,0:T(8,128)(2,1)S(1)} %get-tuple-element.40), channel_id=1, source_target_pairs={{32,0},{64,32},{96,64},{128,96},{160,128},{192,160},{224,192},{0,2... | collective-permute-start | bytes 1572872 | tf_op jit(solution)/shard_map/ppermute | solution.py:325

commit v7 on v6

--- a/solution.py
+++ b/solution.py
@@ -156,6 +156,7 @@
     want_ref,
     limit_ref,
     sums_ref,
+    rests_ref,
     exponent_ref,
     factor_ref,
     start_ref,
@@ -165,26 +166,22 @@
     upper,
     lower,
 ):
-    count = sums_ref.shape[0]
     width = factor_ref.shape[2]
-    scale = jnp.exp2(exponent_ref[:1, :])
-    size = (count * HALF, 128)
-    inner = split(
-        jnp.concatenate(
-            [
-                sums_ref[:, :HALF, :].reshape(size) * scale,
-                sums_ref[:, HALF:PROJ, :].reshape(size) * scale,
-            ],
-            axis=1,
-        )
-    )
-    links = split(sums_ref[:, PROJ:BODY, :].reshape(count * COUP, 128))
+    scale = jnp.exp2(exponent_ref[:1, :1])
+
+    def lines(begin, end):
+        return tuple(ref[:, begin:end, :].reshape(-1, 128) for ref in (sums_ref, rests_ref))
+
+    inner = tuple(
+        jnp.concatenate(pair, axis=1) for pair in zip(lines(0, HALF), lines(HALF, PROJ))
+    )
+    links = lines(PROJ, BODY)
 
     def part(pair, k):
         return tuple(p[k * width : (k + 1) * width] for p in pair)
 
     factors = [split(factor_ref[0, level]) for level in range(4)]
-    current = [dot3(factors[level], part(inner, level)) for level in range(4)]
+    current = [dot3(factors[level], part(inner, level)) * scale for level in range(4)]
     turned = ((1,), (1,))
     places = {
         3: ((0, 5, turned), (1, 4, PLAIN), (2, 2, turned)),
@@ -251,7 +248,7 @@
     )
 
 
-def solve_and_update(want, limits, sums, exponent, factors, start, high, low):
+def solve_and_update(want, limits, sums, rests, exponent, factors, start, high, low):
     count = want.shape[0]
     eigen, columns = start.shape[2], high.shape[2]
     coefficients = jax.ShapeDtypeStruct((columns, eigen), BF16)
@@ -262,12 +259,12 @@
             coefficients,
             coefficients,
         ),
-        in_specs=[SCALARS] * 2 + [ARRAY] * 6,
+        in_specs=[SCALARS] * 2 + [ARRAY] * 7,
         out_specs=(ARRAY,) * 3,
         compiler_params=pltpu.CompilerParams(vmem_limit_bytes=12 << 20),
         cost_estimate=update_cost(count, columns, eigen),
         name="solve",
-    )(want, limits, sums, exponent, factors, start, high, low)
+    )(want, limits, sums, rests, exponent, factors, start, high, low)
 
 
 def left_products(left, occupied, limits, upper, lower, start, panels, tiles):
@@ -369,8 +366,11 @@
     body, exponent = combined([owned, *others])
     copies = jnp.broadcast_to(body.astype(F16), (NEAR, BODY, 128))
     sums = exchanged(copies, inside).astype(F32)
+    upper_sums = lax.reduce_precision(sums, exponent_bits=8, mantissa_bits=7)
+    rests = (sums - upper_sums).astype(BF16)
+    sums = upper_sums.astype(BF16)
     packed, upper, lower = solve_and_update(
-        want, channels[0], sums, exponent, factors, *named
+        want, channels[0], sums, rests, exponent, factors, *named
     )
     right = passed_along(packed, "sym", -1)
     left = left_products(

time: 81.3 us -> 81.3 us (level)
  no operation moved by 1% of the time
where the time goes in v7:
time: 81.3 us; the launch traced here: 81.1 us
  blocking collectives  41.5 us (51%)
  Pallas kernels  19.4 us (24%)
  starting transfers between devices  15 us (18%)
  waiting for transfers between devices  3.72 us (5%)
  other arithmetic  1.21 us (1%)
    all_to_all x3, blocking collectives, exchanged(): lax.all_to_all(shares, 'row', 0, 0, axis_index_groups=groups, tiled=True)  41.5 us
    ppermute x3, starting transfers between devices, around(): return lax.ppermute(share, 'row', route)  9.63 us
    pallas_call x1, Pallas kernels, local_grams(): pl.pallas_call(gram_kernel, out_shape=jax.ShapeDtypeStruct((count, SHARE,...  9.11 us
    ppermute x2, starting transfers between devices, passed_along(): return lax.ppermute(block, axis, route)  5.33 us
    pallas_call x1, Pallas kernels, left_products(): pl.pallas_call(left_kernel, out_shape=(jax.ShapeDtypeStruct((eigen, count...  4.23 us
    ppermute x2, waiting for transfers between devices, passed_along(): return lax.ppermute(block, axis, route)  3.71 us
    pallas_call x1, Pallas kernels, solve_and_update(): pl.pallas_call(solve_kernel, out_shape=(jax.ShapeDtypeStruct((count, BLOC...  2.96 us
    pallas_call x1, Pallas kernels, fetched_blocks(): pl.pallas_call(fetch_kernel, out_shape=(jax.ShapeDtypeStruct((count, BLOC...  2.63 us
  transfers between devices with their start and end apart: 5, of which 1 were waited for; matrix products, arithmetic and copies ran while one was open for 0% of the time, Pallas kernels for 20%

profile of v7, /device:TPU:1, one launch (start us, length us, event | category | flops | bytes accessed | tf_op | source)
XLA Modules:
  0.0 81.1 jit_solution(15128913116902887635)
XLA Ops:
  0.0 2.6 %collective-permute-start = (s32[2]{0:T(128)}, s32[2]{0:T(128)S(1)}, u32[]{:S(2)}, u32[]{:S(2)}) collective-permute-start(s32[2]{0:T(128)} %bitcast.101), channel_id=1, source_target_pairs={{224,0},{0,32},{32,64},{64,96},{96,128},{128,160},{160,192},{192,2... | collective-permute-start | bytes 32 | tf_op jit(solution)/shard_map/ppermute | solution.py:322
  2.6 9.1 %grams.1 = f32[8,232,128]{2,1,0:T(8,128)S(1)} custom-call(f32[1,4096,256]{2,1,0:T(8,128)} %start_ref.5, f32[1,4096,512]{2,1,0:T(8,128)} %panel_ref.5), custom_call_target="tpu_custom_call" | custom-call | flops 6442450944 | bytes 12582912 | tf_op jit(solution)/shard_map/grams/pallas_call | solution.py:84
  11.7 0.1 convert_element_type.61
  11.8 0.0 collective-permute-done.which_ref.want_ref
  11.8 14.6 %all_to_all.15 = f16[8,232,128]{2,1,0:T(8,128)(2,1)S(1)} all-to-all(f16[8,232,128]{2,1,0:T(8,128)(2,1)S(1)} %convert_element_type.61), channel_id=1, replica_groups={{0,1,2,3,4,5,6,7},{8,9,10,11,12,13,14,15},{16,17,18,19,20,21,22,23},{24..., dimensions={0} | all-to-all | bytes 950272 | tf_op jit(solution)/shard_map/all_to_all | solution.py:326
  26.4 0.1 slice_convert_fusion.7
  26.5 0.1 fusion.7
  26.6 0.0 copy-start.1
  26.6 0.0 copy-start.2
  26.7 6.1 %collective-permute-start.3 = (f16[232,128]{1,0:T(8,128)(2,1)S(1)}, f16[232,128]{1,0:T(8,128)(2,1)S(1)}, u32[]{:S(2)}, u32[]{:S(2)}) collective-permute-start(f16[232,128]{1,0:T(8,128)(2,1)S(1)} %pad_maximum_fusion), channel_id=1, source_target_pairs={{16,0},{17,1},{18,2},{19,3},{20,4},{21,5},{22,6},{23,7},{24,8},{25... | collective-permute-start | bytes 178184 | tf_op jit(solution)/shard_map/ppermute | solution.py:345
  32.7 1.2 %collective-permute-start.2 = (f16[232,128]{1,0:T(8,128)(2,1)S(1)}, f16[232,128]{1,0:T(8,128)(2,1)S(1)}, u32[]{:S(2)}, u32[]{:S(2)}) collective-permute-start(f16[232,128]{1,0:T(8,128)(2,1)S(1)} %pad_maximum_fusion), channel_id=1, source_target_pairs={{24,0},{25,1},{26,2},{27,3},{28,4},{29,5},{30,6},{31,7},{0,8},{1,9... | collective-permute-start | bytes 178184 | tf_op jit(solution)/shard_map/ppermute | solution.py:345
  33.9 2.4 %collective-permute-start.1 = (f16[232,128]{1,0:T(8,128)(2,1)S(1)}, f16[232,128]{1,0:T(8,128)(2,1)S(1)}, u32[]{:S(2)}, u32[]{:S(2)}) collective-permute-start(f16[232,128]{1,0:T(8,128)(2,1)S(1)} %pad_maximum_fusion), channel_id=1, source_target_pairs={{8,0},{9,1},{10,2},{11,3},{12,4},{13,5},{14,6},{15,7},{16,8},{17,9... | collective-permute-start | bytes 178184 | tf_op jit(solution)/shard_map/ppermute | solution.py:345
  36.3 0.0 copy-start
  36.3 0.0 copy-start.3
  36.3 0.0 copy-start.4
  36.3 2.6 %fetch.1 = (f32[2,512,256]{2,1,0:T(8,128)S(1)}, bf16[2,512,512]{2,1,0:T(8,128)(2,1)S(1)}, bf16[2,512,512]{2,1,0:T(8,128)(2,1)S(1)}) custom-call(s32[2]{0:T(128)S(1)} %collective-permute-done.which_ref.want_ref, f32[1,4096,256]{2,1,0:T(8,128)} %start_ref.5, f32[1,4096,512]{2,1,0:T(8,128)} %panel_ref.5), custom_call_target="tpu_custom_call" | custom-call | flops 524288 | bytes 6291456 | tf_op jit(solution)/shard_map/fetch/pallas_call | solution.py:124
  39.0 0.0 collective-permute-done.3
  39.0 0.0 collective-permute-done.2
  39.0 0.0 collective-permute-done.1
  39.2 0.1 broadcast_in_dim.6
  39.3 10.7 %all_to_all.16 = f16[8,224,128]{2,1,0:T(8,128)(2,1)S(1)} all-to-all(f16[8,224,128]{2,1,0:T(8,128)(2,1)S(1)} %broadcast_in_dim.6), channel_id=1, replica_groups={{0,1,2,3,4,5,6,7},{8,9,10,11,12,13,14,15},{16,17,18,19,20,21,22,23},{24..., dimensions={0} | all-to-all | bytes 917504 | tf_op jit(solution)/shard_map/all_to_all | solution.py:326
  50.0 0.2 fusion
  50.2 0.0 copy-done.1
  50.2 0.0 copy-done.2
  50.2 3.0 %solve.1 = (bf16[2,512,256]{2,1,0:T(8,128)(2,1)S(1)}, bf16[512,256]{1,0:T(8,128)(2,1)S(1)}, bf16[512,256]{1,0:T(8,128)(2,1)S(1)}) custom-call(s32[2]{0:T(128)S(1)} %collective-permute-done.which_ref.want_ref, s32[8]{0:T(128)S(1)} %bitcast.97, bf16[8,224,128]{2,1,0:T(8,128)(2,1)S(1)} %get-tuple-element.52.sums_ref, ...), custom_call_target="tpu_custom_call" | custom-call | flops 805306368 | bytes 3145728 | tf_op jit(solution)/shard_map/solve/pallas_call | solution.py:255
  53.1 2.7 %collective-permute-start.4 = (bf16[2,512,256]{2,1,0:T(8,128)(2,1)S(1)}, bf16[2,512,256]{2,1,0:T(8,128)(2,1)S(1)}, u32[]{:S(2)}, u32[]{:S(2)}) collective-permute-start(bf16[2,512,256]{2,1,0:T(8,128)(2,1)S(1)} %get-tuple-element.40), channel_id=1, source_target_pairs={{32,0},{64,32},{96,64},{128,96},{160,128},{192,160},{224,192},{0,2... | collective-permute-start | bytes 1572872 | tf_op jit(solution)/shard_map/ppermute | solution.py:322
  55.9 0.0 copy-done
  55.9 4.2 %left.1 = (bf16[256,1024]{1,0:T(8,128)(2,1)S(1)}, bf16[256,1024]{1,0:T(8,128)(2,1)S(1)}) custom-call(s32[2]{0:T(128)S(1)} %bitcast.99, s32[2]{0:T(128)S(1)} %bitcast.100, s32[8]{0:T(128)S(1)} %bitcast.98, bf16[512,256]{1,0:T(8,128)(2,1)S(1)} %get-tuple-element.36.upper, bf16[512,256]{1,0:T(8,128)(2,1)S(1)} %get-tuple-element.37.lower, ...), custom_call_target="tpu_custom_call" | custom-call | flops 805306368 | bytes 3145728 | tf_op jit(solution)/shard_map/left/pallas_call | solution.py:281
  60.1 3.7 %collective-permute-done.4.right_ref = bf16[2,512,256]{2,1,0:T(8,128)(2,1)S(1)} collective-permute-done((bf16[2,512,256]{2,1,0:T(8,128)(2,1)S(1)}, bf16[2,512,256]{2,1,0:T(8,128)(2,1)S(1)}, u32[]{:S(2)}, u32[]{:S(2)}) %collective-permute-start.4) | collective-permute-done | bytes 524320 | tf_op jit(solution)/shard_map/ppermute | solution.py:322
  63.8 0.4 dipole.1
  64.3 16.2 %all_to_all.17 = bf16[32,8,256]{2,1,0:T(8,128)(2,1)S(1)} all-to-all(bf16[32,8,256]{2,1,0:T(8,128)(2,1)S(1)} %bitcast.96), channel_id=1, replica_groups=mesh['sym'=8,'row'=32] {'row'}, dimensions={0} | all-to-all | bytes 262144 | tf_op jit(solution)/shard_map/all_to_all | solution.py:326
  80.4 0.6 convert_reduce_fusion
  (15 shorter events, 0.2 us)
Async XLA Ops:
  0.0 11.8 %collective-permute-start = (s32[2]{0:T(128)}, s32[2]{0:T(128)S(1)}, u32[]{:S(2)}, u32[]{:S(2)}) collective-permute-start(s32[2]{0:T(128)} %bitcast.101), channel_id=1, source_target_pairs={{224,0},{0,32},{32,64},{64,96},{96,128},{128,160},{160,192},{192,2... | collective-permute-start | bytes 32 | tf_op jit(solution)/shard_map/ppermute | solution.py:322
  26.6 23.5 %copy-start.1 = (f32[1,4,128,128]{3,2,1,0:T(8,128)S(1)}, f32[1,4,128,128]{3,2,1,0:T(8,128)}, u32[]{:S(2)}) copy-start(f32[1,4,128,128]{3,2,1,0:T(8,128)} %factor_ref.1) | copy-start | bytes 786436
  26.6 23.5 %copy-start.2 = (s32[1,8]{1,0:T(1,128)S(1)}, s32[1,8]{1,0:T(1,128)}, u32[]{:S(2)}) copy-start(s32[1,8]{1,0:T(1,128)} %param.15) | copy-start | bytes 100
  26.7 12.3 %collective-permute-start.3 = (f16[232,128]{1,0:T(8,128)(2,1)S(1)}, f16[232,128]{1,0:T(8,128)(2,1)S(1)}, u32[]{:S(2)}, u32[]{:S(2)}) collective-permute-start(f16[232,128]{1,0:T(8,128)(2,1)S(1)} %pad_maximum_fusion), channel_id=1, source_target_pairs={{16,0},{17,1},{18,2},{19,3},{20,4},{21,5},{22,6},{23,7},{24,8},{25... | collective-permute-start | bytes 178184 | tf_op jit(solution)/shard_map/ppermute | solution.py:345
  32.7 6.3 %collective-permute-start.2 = (f16[232,128]{1,0:T(8,128)(2,1)S(1)}, f16[232,128]{1,0:T(8,128)(2,1)S(1)}, u32[]{:S(2)}, u32[]{:S(2)}) collective-permute-start(f16[232,128]{1,0:T(8,128)(2,1)S(1)} %pad_maximum_fusion), channel_id=1, source_target_pairs={{24,0},{25,1},{26,2},{27,3},{28,4},{29,5},{30,6},{31,7},{0,8},{1,9... | collective-permute-start | bytes 178184 | tf_op jit(solution)/shard_map/ppermute | solution.py:345
  33.9 5.1 %collective-permute-start.1 = (f16[232,128]{1,0:T(8,128)(2,1)S(1)}, f16[232,128]{1,0:T(8,128)(2,1)S(1)}, u32[]{:S(2)}, u32[]{:S(2)}) collective-permute-start(f16[232,128]{1,0:T(8,128)(2,1)S(1)} %pad_maximum_fusion), channel_id=1, source_target_pairs={{8,0},{9,1},{10,2},{11,3},{12,4},{13,5},{14,6},{15,7},{16,8},{17,9... | collective-permute-start | bytes 178184 | tf_op jit(solution)/shard_map/ppermute | solution.py:345
  36.3 19.6 %copy-start = (bf16[1,2,512,512]{3,2,1,0:T(8,128)(2,1)S(1)}, bf16[1,2,512,512]{3,2,1,0:T(8,128)(2,1)}, u32[]{:S(2)}) copy-start(bf16[1,2,512,512]{3,2,1,0:T(8,128)(2,1)} %tile_ref.1) | copy-start | bytes 3145732
  36.3 19.6 %copy-start.3 = (s32[1,2]{1,0:T(1,128)S(1)}, s32[1,2]{1,0:T(1,128)}, u32[]{:S(2)}) copy-start(s32[1,2]{1,0:T(1,128)} %param.12) | copy-start | bytes 28
  36.3 19.6 %copy-start.4 = (s32[1,2]{1,0:T(1,128)S(1)}, s32[1,2]{1,0:T(1,128)}, u32[]{:S(2)}) copy-start(s32[1,2]{1,0:T(1,128)} %param.14) | copy-start | bytes 28
  53.1 10.7 %collective-permute-start.4 = (bf16[2,512,256]{2,1,0:T(8,128)(2,1)S(1)}, bf16[2,512,256]{2,1,0:T(8,128)(2,1)S(1)}, u32[]{:S(2)}, u32[]{:S(2)}) collective-permute-start(bf16[2,512,256]{2,1,0:T(8,128)(2,1)S(1)} %get-tuple-element.40), channel_id=1, source_target_pairs={{32,0},{64,32},{96,64},{128,96},{160,128},{192,160},{224,192},{0,2... | collective-permute-start | bytes 1572872 | tf_op jit(solution)/shard_map/ppermute | solution.py:322

commit v8 on v6

--- a/solution.py
+++ b/solution.py
@@ -35,6 +35,16 @@
 def dot3(a, b, dims=PLAIN):
     (ah, al), (bh, bl) = a, b
     return dot(ah, bh, dims) + (dot(ah, bl, dims) + dot(al, bh, dims))
+
+
+def joined3(a, b, dims=PLAIN):
+    (ah, al), (bh, bl) = a, b
+    (left,), (right,) = dims
+    return dot(
+        jnp.concatenate([ah, ah, al], axis=left),
+        jnp.concatenate([bh, bl, bh], axis=right),
+        dims,
+    )
 
 
 def gram_kernel(start_ref, panel_ref, out_ref, proj, coup):
@@ -184,7 +194,7 @@
         return tuple(p[k * width : (k + 1) * width] for p in pair)
 
     factors = [split(factor_ref[0, level]) for level in range(4)]
-    current = [dot3(factors[level], part(inner, level)) for level in range(4)]
+    current = [joined3(factors[level], part(inner, level)) for level in range(4)]
     turned = ((1,), (1,))
     places = {
         3: ((0, 5, turned), (1, 4, PLAIN), (2, 2, turned)),
@@ -193,13 +203,13 @@
     }
     chained = {}
     for later, entries in places.items():
-        products = [dot3(factors[k], part(links, at), dims) for k, at, dims in entries]
+        products = [joined3(factors[k], part(links, at), dims) for k, at, dims in entries]
         chained[later] = split(jnp.concatenate(products, axis=0))
     parts = [None] * 4
     for level in (3, 2, 1, 0):
         parts[level] = split(current[level])
         if level:
-            moved = dot3(chained[level], parts[level])
+            moved = joined3(chained[level], parts[level])
             for k in range(level):
                 current[k] = current[k] - moved[k * width : (k + 1) * width]
     upper[...] = jnp.concatenate([p[0] for p in parts], axis=0)

time: 81.3 us -> 81 us (level)
  no operation moved by 1% of the time
where the time goes in v8:
time: 81 us; the launch traced here: 80.8 us
  blocking collectives  41.5 us (51%)
  Pallas kernels  19.1 us (24%)
  starting transfers between devices  15 us (19%)
  waiting for transfers between devices  3.72 us (5%)
  other arithmetic  1.13 us (1%)
    all_to_all x3, blocking collectives, exchanged(): lax.all_to_all(shares, 'row', 0, 0, axis_index_groups=groups, tiled=True)  41.5 us
    ppermute x3, starting transfers between devices, around(): return lax.ppermute(share, 'row', route)  9.63 us
    pallas_call x1, Pallas kernels, local_grams(): pl.pallas_call(gram_kernel, out_shape=jax.ShapeDtypeStruct((count, SHARE,...  9.11 us
    ppermute x2, starting transfers between devices, passed_along(): return lax.ppermute(block, axis, route)  5.32 us
    pallas_call x1, Pallas kernels, left_products(): pl.pallas_call(left_kernel, out_shape=(jax.ShapeDtypeStruct((eigen, count...  4.23 us
    ppermute x2, waiting for transfers between devices, passed_along(): return lax.ppermute(block, axis, route)  3.71 us
    pallas_call x1, Pallas kernels, solve_and_update(): pl.pallas_call(solve_kernel, out_shape=(jax.ShapeDtypeStruct((count, BLOC...  2.74 us
    pallas_call x1, Pallas kernels, fetched_blocks(): pl.pallas_call(fetch_kernel, out_shape=(jax.ShapeDtypeStruct((count, BLOC...  2.63 us
  transfers between devices with their start and end apart: 5, of which 1 were waited for; matrix products, arithmetic and copies ran while one was open for 0% of the time, Pallas kernels for 20%

profile of v8, /device:TPU:1, one launch (start us, length us, event | category | flops | bytes accessed | tf_op | source)
XLA Modules:
  0.0 80.8 jit_solution(8318924389423160449)
XLA Ops:
  0.0 2.6 %collective-permute-start = (s32[2]{0:T(128)}, s32[2]{0:T(128)S(1)}, u32[]{:S(2)}, u32[]{:S(2)}) collective-permute-start(s32[2]{0:T(128)} %bitcast.101), channel_id=1, source_target_pairs={{224,0},{0,32},{32,64},{64,96},{96,128},{128,160},{160,192},{192,2... | collective-permute-start | bytes 32 | tf_op jit(solution)/shard_map/ppermute | solution.py:335
  2.6 9.1 %grams.1 = f32[8,232,128]{2,1,0:T(8,128)S(1)} custom-call(f32[1,4096,256]{2,1,0:T(8,128)} %start_ref.5, f32[1,4096,512]{2,1,0:T(8,128)} %panel_ref.5), custom_call_target="tpu_custom_call" | custom-call | flops 6442450944 | bytes 12582912 | tf_op jit(solution)/shard_map/grams/pallas_call | solution.py:94
  11.7 0.1 convert_element_type.55
  11.8 0.0 collective-permute-done.which_ref.want_ref
  11.8 14.6 %all_to_all.15 = f16[8,232,128]{2,1,0:T(8,128)(2,1)S(1)} all-to-all(f16[8,232,128]{2,1,0:T(8,128)(2,1)S(1)} %convert_element_type.55), channel_id=1, replica_groups={{0,1,2,3,4,5,6,7},{8,9,10,11,12,13,14,15},{16,17,18,19,20,21,22,23},{24..., dimensions={0} | all-to-all | bytes 950272 | tf_op jit(solution)/shard_map/all_to_all | solution.py:339
  26.4 0.1 slice_convert_fusion.7
  26.5 0.1 fusion.6
  26.6 0.0 copy-start.1
  26.6 0.0 copy-start.2
  26.7 6.1 %collective-permute-start.3 = (f16[232,128]{1,0:T(8,128)(2,1)S(1)}, f16[232,128]{1,0:T(8,128)(2,1)S(1)}, u32[]{:S(2)}, u32[]{:S(2)}) collective-permute-start(f16[232,128]{1,0:T(8,128)(2,1)S(1)} %pad_maximum_fusion), channel_id=1, source_target_pairs={{16,0},{17,1},{18,2},{19,3},{20,4},{21,5},{22,6},{23,7},{24,8},{25... | collective-permute-start | bytes 178184 | tf_op jit(solution)/shard_map/ppermute | solution.py:358
  32.7 1.2 %collective-permute-start.2 = (f16[232,128]{1,0:T(8,128)(2,1)S(1)}, f16[232,128]{1,0:T(8,128)(2,1)S(1)}, u32[]{:S(2)}, u32[]{:S(2)}) collective-permute-start(f16[232,128]{1,0:T(8,128)(2,1)S(1)} %pad_maximum_fusion), channel_id=1, source_target_pairs={{24,0},{25,1},{26,2},{27,3},{28,4},{29,5},{30,6},{31,7},{0,8},{1,9... | collective-permute-start | bytes 178184 | tf_op jit(solution)/shard_map/ppermute | solution.py:358
  33.9 2.4 %collective-permute-start.1 = (f16[232,128]{1,0:T(8,128)(2,1)S(1)}, f16[232,128]{1,0:T(8,128)(2,1)S(1)}, u32[]{:S(2)}, u32[]{:S(2)}) collective-permute-start(f16[232,128]{1,0:T(8,128)(2,1)S(1)} %pad_maximum_fusion), channel_id=1, source_target_pairs={{8,0},{9,1},{10,2},{11,3},{12,4},{13,5},{14,6},{15,7},{16,8},{17,9... | collective-permute-start | bytes 178184 | tf_op jit(solution)/shard_map/ppermute | solution.py:358
  36.3 0.0 copy-start
  36.3 0.0 copy-start.3
  36.3 0.0 copy-start.4
  36.3 2.6 %fetch.1 = (f32[2,512,256]{2,1,0:T(8,128)S(1)}, bf16[2,512,512]{2,1,0:T(8,128)(2,1)S(1)}, bf16[2,512,512]{2,1,0:T(8,128)(2,1)S(1)}) custom-call(s32[2]{0:T(128)S(1)} %collective-permute-done.which_ref.want_ref, f32[1,4096,256]{2,1,0:T(8,128)} %start_ref.5, f32[1,4096,512]{2,1,0:T(8,128)} %panel_ref.5), custom_call_target="tpu_custom_call" | custom-call | flops 524288 | bytes 6291456 | tf_op jit(solution)/shard_map/fetch/pallas_call | solution.py:134
  39.0 0.0 collective-permute-done.3
  39.0 0.0 collective-permute-done.2
  39.0 0.0 collective-permute-done.1
  39.2 0.1 broadcast_in_dim.6
  39.3 10.7 %all_to_all.16 = f16[8,224,128]{2,1,0:T(8,128)(2,1)S(1)} all-to-all(f16[8,224,128]{2,1,0:T(8,128)(2,1)S(1)} %broadcast_in_dim.6), channel_id=1, replica_groups={{0,1,2,3,4,5,6,7},{8,9,10,11,12,13,14,15},{16,17,18,19,20,21,22,23},{24..., dimensions={0} | all-to-all | bytes 917504 | tf_op jit(solution)/shard_map/all_to_all | solution.py:339
  50.0 0.1 convert_element_type.68.sums_ref
  50.1 0.0 copy-done.1
  50.1 0.0 copy-done.2
  50.1 2.7 %solve.1 = (bf16[2,512,256]{2,1,0:T(8,128)(2,1)S(1)}, bf16[512,256]{1,0:T(8,128)(2,1)S(1)}, bf16[512,256]{1,0:T(8,128)(2,1)S(1)}) custom-call(s32[2]{0:T(128)S(1)} %collective-permute-done.which_ref.want_ref, s32[8]{0:T(128)S(1)} %bitcast.97, f32[8,224,128]{2,1,0:T(8,128)S(1)} %convert_element_type.68.sums_ref, f32[8,128]{1,0:T(8,128)S(1)} %fusion.25.exponent_ref, ...), custom_call_target="tpu_custom_call" | custom-call | flops 805306368 | bytes 3145728 | tf_op jit(solution)/shard_map/solve/pallas_call | solution.py:268
  52.8 2.7 %collective-permute-start.4 = (bf16[2,512,256]{2,1,0:T(8,128)(2,1)S(1)}, bf16[2,512,256]{2,1,0:T(8,128)(2,1)S(1)}, u32[]{:S(2)}, u32[]{:S(2)}) collective-permute-start(bf16[2,512,256]{2,1,0:T(8,128)(2,1)S(1)} %get-tuple-element.40), channel_id=1, source_target_pairs={{32,0},{64,32},{96,64},{128,96},{160,128},{192,160},{224,192},{0,2... | collective-permute-start | bytes 1572872 | tf_op jit(solution)/shard_map/ppermute | solution.py:335
  55.6 0.0 copy-done.3
  55.6 4.2 %left.1 = (bf16[256,1024]{1,0:T(8,128)(2,1)S(1)}, bf16[256,1024]{1,0:T(8,128)(2,1)S(1)}) custom-call(s32[2]{0:T(128)S(1)} %bitcast.99, s32[2]{0:T(128)S(1)} %bitcast.100, s32[8]{0:T(128)S(1)} %bitcast.98, bf16[512,256]{1,0:T(8,128)(2,1)S(1)} %get-tuple-element.36.upper, bf16[512,256]{1,0:T(8,128)(2,1)S(1)} %get-tuple-element.37.lower, ...), custom_call_target="tpu_custom_call" | custom-call | flops 805306368 | bytes 3145728 | tf_op jit(solution)/shard_map/left/pallas_call | solution.py:294
  59.8 3.7 %collective-permute-done.4.right_ref = bf16[2,512,256]{2,1,0:T(8,128)(2,1)S(1)} collective-permute-done((bf16[2,512,256]{2,1,0:T(8,128)(2,1)S(1)}, bf16[2,512,256]{2,1,0:T(8,128)(2,1)S(1)}, u32[]{:S(2)}, u32[]{:S(2)}) %collective-permute-start.4) | collective-permute-done | bytes 524320 | tf_op jit(solution)/shard_map/ppermute | solution.py:335
  63.5 0.4 dipole.1
  64.0 16.2 %all_to_all.17 = bf16[32,8,256]{2,1,0:T(8,128)(2,1)S(1)} all-to-all(bf16[32,8,256]{2,1,0:T(8,128)(2,1)S(1)} %bitcast.96), channel_id=1, replica_groups=mesh['sym'=8,'row'=32] {'row'}, dimensions={0} | all-to-all | bytes 262144 | tf_op jit(solution)/shard_map/all_to_all | solution.py:339
  80.1 0.6 convert_reduce_fusion
  (15 shorter events, 0.2 us)
Async XLA Ops:
  0.0 11.8 %collective-permute-start = (s32[2]{0:T(128)}, s32[2]{0:T(128)S(1)}, u32[]{:S(2)}, u32[]{:S(2)}) collective-permute-start(s32[2]{0:T(128)} %bitcast.101), channel_id=1, source_target_pairs={{224,0},{0,32},{32,64},{64,96},{96,128},{128,160},{160,192},{192,2... | collective-permute-start | bytes 32 | tf_op jit(solution)/shard_map/ppermute | solution.py:335
  26.6 23.4 %copy-start.1 = (f32[1,4,128,128]{3,2,1,0:T(8,128)S(1)}, f32[1,4,128,128]{3,2,1,0:T(8,128)}, u32[]{:S(2)}) copy-start(f32[1,4,128,128]{3,2,1,0:T(8,128)} %factor_ref.1) | copy-start | bytes 786436
  26.6 23.4 %copy-start.2 = (s32[1,8]{1,0:T(1,128)S(1)}, s32[1,8]{1,0:T(1,128)}, u32[]{:S(2)}) copy-start(s32[1,8]{1,0:T(1,128)} %param.15) | copy-start | bytes 100
  26.7 12.3 %collective-permute-start.3 = (f16[232,128]{1,0:T(8,128)(2,1)S(1)}, f16[232,128]{1,0:T(8,128)(2,1)S(1)}, u32[]{:S(2)}, u32[]{:S(2)}) collective-permute-start(f16[232,128]{1,0:T(8,128)(2,1)S(1)} %pad_maximum_fusion), channel_id=1, source_target_pairs={{16,0},{17,1},{18,2},{19,3},{20,4},{21,5},{22,6},{23,7},{24,8},{25... | collective-permute-start | bytes 178184 | tf_op jit(solution)/shard_map/ppermute | solution.py:358
  32.7 6.3 %collective-permute-start.2 = (f16[232,128]{1,0:T(8,128)(2,1)S(1)}, f16[232,128]{1,0:T(8,128)(2,1)S(1)}, u32[]{:S(2)}, u32[]{:S(2)}) collective-permute-start(f16[232,128]{1,0:T(8,128)(2,1)S(1)} %pad_maximum_fusion), channel_id=1, source_target_pairs={{24,0},{25,1},{26,2},{27,3},{28,4},{29,5},{30,6},{31,7},{0,8},{1,9... | collective-permute-start | bytes 178184 | tf_op jit(solution)/shard_map/ppermute | solution.py:358
  33.9 5.1 %collective-permute-start.1 = (f16[232,128]{1,0:T(8,128)(2,1)S(1)}, f16[232,128]{1,0:T(8,128)(2,1)S(1)}, u32[]{:S(2)}, u32[]{:S(2)}) collective-permute-start(f16[232,128]{1,0:T(8,128)(2,1)S(1)} %pad_maximum_fusion), channel_id=1, source_target_pairs={{8,0},{9,1},{10,2},{11,3},{12,4},{13,5},{14,6},{15,7},{16,8},{17,9... | collective-permute-start | bytes 178184 | tf_op jit(solution)/shard_map/ppermute | solution.py:358
  36.3 19.3 %copy-start = (bf16[1,2,512,512]{3,2,1,0:T(8,128)(2,1)S(1)}, bf16[1,2,512,512]{3,2,1,0:T(8,128)(2,1)}, u32[]{:S(2)}) copy-start(bf16[1,2,512,512]{3,2,1,0:T(8,128)(2,1)} %tile_ref.1) | copy-start | bytes 3145732
  36.3 19.3 %copy-start.3 = (s32[1,2]{1,0:T(1,128)S(1)}, s32[1,2]{1,0:T(1,128)}, u32[]{:S(2)}) copy-start(s32[1,2]{1,0:T(1,128)} %param.12) | copy-start | bytes 28
  36.3 19.2 %copy-start.4 = (s32[1,2]{1,0:T(1,128)S(1)}, s32[1,2]{1,0:T(1,128)}, u32[]{:S(2)}) copy-start(s32[1,2]{1,0:T(1,128)} %param.14) | copy-start | bytes 28
  52.8 10.7 %collective-permute-start.4 = (bf16[2,512,256]{2,1,0:T(8,128)(2,1)S(1)}, bf16[2,512,256]{2,1,0:T(8,128)(2,1)S(1)}, u32[]{:S(2)}, u32[]{:S(2)}) collective-permute-start(bf16[2,512,256]{2,1,0:T(8,128)(2,1)S(1)} %get-tuple-element.40), channel_id=1, source_target_pairs={{32,0},{64,32},{96,64},{128,96},{160,128},{192,160},{224,192},{0,2... | collective-permute-start | bytes 1572872 | tf_op jit(solution)/shard_map/ppermute | solution.py:335

commit v9 on v8

--- a/solution.py
+++ b/solution.py
@@ -196,15 +196,23 @@
     factors = [split(factor_ref[0, level]) for level in range(4)]
     current = [joined3(factors[level], part(inner, level)) for level in range(4)]
     turned = ((1,), (1,))
-    places = {
-        3: ((0, 5, turned), (1, 4, PLAIN), (2, 2, turned)),
-        2: ((0, 3, PLAIN), (1, 1, PLAIN)),
-        1: ((0, 0, PLAIN),),
+
+    def both(k, one, other):
+        wide = tuple(
+            jnp.concatenate(pair, axis=1) for pair in zip(part(links, one), part(links, other))
+        )
+        product = joined3(factors[k], wide)
+        return product[:, :width], product[:, width:]
+
+    to_01, to_02 = both(0, 0, 3)
+    to_12, to_13 = both(1, 1, 4)
+    to_23 = joined3(factors[2], part(links, 2), turned)
+    to_03 = joined3(factors[0], part(links, 5), turned)
+    chained = {
+        3: split(jnp.concatenate([to_03, to_13, to_23], axis=0)),
+        2: split(jnp.concatenate([to_02, to_12], axis=0)),
+        1: split(to_01),
     }
-    chained = {}
-    for later, entries in places.items():
-        products = [joined3(factors[k], part(links, at), dims) for k, at, dims in entries]
-        chained[later] = split(jnp.concatenate(products, axis=0))
     parts = [None] * 4
     for level in (3, 2, 1, 0):
         parts[level] = split(current[level])

time: 81 us -> 81 us (level)
  no operation moved by 1% of the time
where the time goes in v9:
time: 81 us; the launch traced here: 80.8 us
  blocking collectives  41.5 us (51%)
  Pallas kernels  19.2 us (24%)
  starting transfers between devices  15 us (19%)
  waiting for transfers between devices  3.71 us (5%)
  other arithmetic  1.13 us (1%)
    all_to_all x3, blocking collectives, exchanged(): lax.all_to_all(shares, 'row', 0, 0, axis_index_groups=groups, tiled=True)  41.5 us
    ppermute x3, starting transfers between devices, around(): return lax.ppermute(share, 'row', route)  9.63 us
    pallas_call x1, Pallas kernels, local_grams(): pl.pallas_call(gram_kernel, out_shape=jax.ShapeDtypeStruct((count, SHARE,...  9.11 us
    ppermute x2, starting transfers between devices, passed_along(): return lax.ppermute(block, axis, route)  5.32 us
    pallas_call x1, Pallas kernels, left_products(): pl.pallas_call(left_kernel, out_shape=(jax.ShapeDtypeStruct((eigen, count...  4.23 us
    ppermute x2, waiting for transfers between devices, passed_along(): return lax.ppermute(block, axis, route)  3.71 us
    pallas_call x1, Pallas kernels, solve_and_update(): pl.pallas_call(solve_kernel, out_shape=(jax.ShapeDtypeStruct((count, BLOC...  2.77 us
    pallas_call x1, Pallas kernels, fetched_blocks(): pl.pallas_call(fetch_kernel, out_shape=(jax.ShapeDtypeStruct((count, BLOC...  2.63 us
  transfers between devices with their start and end apart: 5, of which 1 were waited for; matrix products, arithmetic and copies ran while one was open for 0% of the time, Pallas kernels for 20%

profile of v9, /device:TPU:1, one launch (start us, length us, event | category | flops | bytes accessed | tf_op | source)
XLA Modules:
  0.0 80.8 jit_solution(10404043180297234400)
XLA Ops:
  0.0 2.6 %collective-permute-start = (s32[2]{0:T(128)}, s32[2]{0:T(128)S(1)}, u32[]{:S(2)}, u32[]{:S(2)}) collective-permute-start(s32[2]{0:T(128)} %bitcast.101), channel_id=1, source_target_pairs={{224,0},{0,32},{32,64},{64,96},{96,128},{128,160},{160,192},{192,2... | collective-permute-start | bytes 32 | tf_op jit(solution)/shard_map/ppermute | solution.py:343
  2.6 9.1 %grams.1 = f32[8,232,128]{2,1,0:T(8,128)S(1)} custom-call(f32[1,4096,256]{2,1,0:T(8,128)} %start_ref.5, f32[1,4096,512]{2,1,0:T(8,128)} %panel_ref.5), custom_call_target="tpu_custom_call" | custom-call | flops 6442450944 | bytes 12582912 | tf_op jit(solution)/shard_map/grams/pallas_call | solution.py:94
  11.7 0.1 convert_element_type.55
  11.8 0.0 collective-permute-done.which_ref.want_ref
  11.8 14.6 %all_to_all.15 = f16[8,232,128]{2,1,0:T(8,128)(2,1)S(1)} all-to-all(f16[8,232,128]{2,1,0:T(8,128)(2,1)S(1)} %convert_element_type.55), channel_id=1, replica_groups={{0,1,2,3,4,5,6,7},{8,9,10,11,12,13,14,15},{16,17,18,19,20,21,22,23},{24..., dimensions={0} | all-to-all | bytes 950272 | tf_op jit(solution)/shard_map/all_to_all | solution.py:347
  26.4 0.1 slice_convert_fusion.7
  26.5 0.1 fusion.6
  26.6 0.0 copy-start.1
  26.6 0.0 copy-start.2
  26.7 6.1 %collective-permute-start.3 = (f16[232,128]{1,0:T(8,128)(2,1)S(1)}, f16[232,128]{1,0:T(8,128)(2,1)S(1)}, u32[]{:S(2)}, u32[]{:S(2)}) collective-permute-start(f16[232,128]{1,0:T(8,128)(2,1)S(1)} %pad_maximum_fusion), channel_id=1, source_target_pairs={{16,0},{17,1},{18,2},{19,3},{20,4},{21,5},{22,6},{23,7},{24,8},{25... | collective-permute-start | bytes 178184 | tf_op jit(solution)/shard_map/ppermute | solution.py:366
  32.7 1.2 %collective-permute-start.2 = (f16[232,128]{1,0:T(8,128)(2,1)S(1)}, f16[232,128]{1,0:T(8,128)(2,1)S(1)}, u32[]{:S(2)}, u32[]{:S(2)}) collective-permute-start(f16[232,128]{1,0:T(8,128)(2,1)S(1)} %pad_maximum_fusion), channel_id=1, source_target_pairs={{24,0},{25,1},{26,2},{27,3},{28,4},{29,5},{30,6},{31,7},{0,8},{1,9... | collective-permute-start | bytes 178184 | tf_op jit(solution)/shard_map/ppermute | solution.py:366
  33.9 2.4 %collective-permute-start.1 = (f16[232,128]{1,0:T(8,128)(2,1)S(1)}, f16[232,128]{1,0:T(8,128)(2,1)S(1)}, u32[]{:S(2)}, u32[]{:S(2)}) collective-permute-start(f16[232,128]{1,0:T(8,128)(2,1)S(1)} %pad_maximum_fusion), channel_id=1, source_target_pairs={{8,0},{9,1},{10,2},{11,3},{12,4},{13,5},{14,6},{15,7},{16,8},{17,9... | collective-permute-start | bytes 178184 | tf_op jit(solution)/shard_map/ppermute | solution.py:366
  36.3 0.0 copy-start
  36.3 0.0 copy-start.3
  36.3 0.0 copy-start.4
  36.3 2.6 %fetch.1 = (f32[2,512,256]{2,1,0:T(8,128)S(1)}, bf16[2,512,512]{2,1,0:T(8,128)(2,1)S(1)}, bf16[2,512,512]{2,1,0:T(8,128)(2,1)S(1)}) custom-call(s32[2]{0:T(128)S(1)} %collective-permute-done.which_ref.want_ref, f32[1,4096,256]{2,1,0:T(8,128)} %start_ref.5, f32[1,4096,512]{2,1,0:T(8,128)} %panel_ref.5), custom_call_target="tpu_custom_call" | custom-call | flops 524288 | bytes 6291456 | tf_op jit(solution)/shard_map/fetch/pallas_call | solution.py:134
  39.0 0.0 collective-permute-done.3
  39.0 0.0 collective-permute-done.2
  39.0 0.0 collective-permute-done.1
  39.2 0.1 broadcast_in_dim.6
  39.3 10.7 %all_to_all.16 = f16[8,224,128]{2,1,0:T(8,128)(2,1)S(1)} all-to-all(f16[8,224,128]{2,1,0:T(8,128)(2,1)S(1)} %broadcast_in_dim.6), channel_id=1, replica_groups={{0,1,2,3,4,5,6,7},{8,9,10,11,12,13,14,15},{16,17,18,19,20,21,22,23},{24..., dimensions={0} | all-to-all | bytes 917504 | tf_op jit(solution)/shard_map/all_to_all | solution.py:347
  50.0 0.1 convert_element_type.68.sums_ref
  50.1 0.0 copy-done.1
  50.1 0.0 copy-done.2
  50.1 2.8 %solve.1 = (bf16[2,512,256]{2,1,0:T(8,128)(2,1)S(1)}, bf16[512,256]{1,0:T(8,128)(2,1)S(1)}, bf16[512,256]{1,0:T(8,128)(2,1)S(1)}) custom-call(s32[2]{0:T(128)S(1)} %collective-permute-done.which_ref.want_ref, s32[8]{0:T(128)S(1)} %bitcast.97, f32[8,224,128]{2,1,0:T(8,128)S(1)} %convert_element_type.68.sums_ref, f32[8,128]{1,0:T(8,128)S(1)} %fusion.25.exponent_ref, ...), custom_call_target="tpu_custom_call" | custom-call | flops 805306368 | bytes 3145728 | tf_op jit(solution)/shard_map/solve/pallas_call | solution.py:276
  52.9 2.7 %collective-permute-start.4 = (bf16[2,512,256]{2,1,0:T(8,128)(2,1)S(1)}, bf16[2,512,256]{2,1,0:T(8,128)(2,1)S(1)}, u32[]{:S(2)}, u32[]{:S(2)}) collective-permute-start(bf16[2,512,256]{2,1,0:T(8,128)(2,1)S(1)} %get-tuple-element.40), channel_id=1, source_target_pairs={{32,0},{64,32},{96,64},{128,96},{160,128},{192,160},{224,192},{0,2... | collective-permute-start | bytes 1572872 | tf_op jit(solution)/shard_map/ppermute | solution.py:343
  55.6 0.0 copy-done.3
  55.6 4.2 %left.1 = (bf16[256,1024]{1,0:T(8,128)(2,1)S(1)}, bf16[256,1024]{1,0:T(8,128)(2,1)S(1)}) custom-call(s32[2]{0:T(128)S(1)} %bitcast.99, s32[2]{0:T(128)S(1)} %bitcast.100, s32[8]{0:T(128)S(1)} %bitcast.98, bf16[512,256]{1,0:T(8,128)(2,1)S(1)} %get-tuple-element.36.upper, bf16[512,256]{1,0:T(8,128)(2,1)S(1)} %get-tuple-element.37.lower, ...), custom_call_target="tpu_custom_call" | custom-call | flops 805306368 | bytes 3145728 | tf_op jit(solution)/shard_map/left/pallas_call | solution.py:302
  59.8 3.7 %collective-permute-done.4.right_ref = bf16[2,512,256]{2,1,0:T(8,128)(2,1)S(1)} collective-permute-done((bf16[2,512,256]{2,1,0:T(8,128)(2,1)S(1)}, bf16[2,512,256]{2,1,0:T(8,128)(2,1)S(1)}, u32[]{:S(2)}, u32[]{:S(2)}) %collective-permute-start.4) | collective-permute-done | bytes 524320 | tf_op jit(solution)/shard_map/ppermute | solution.py:343
  63.5 0.4 dipole.1
  64.0 16.2 %all_to_all.17 = bf16[32,8,256]{2,1,0:T(8,128)(2,1)S(1)} all-to-all(bf16[32,8,256]{2,1,0:T(8,128)(2,1)S(1)} %bitcast.96), channel_id=1, replica_groups=mesh['sym'=8,'row'=32] {'row'}, dimensions={0} | all-to-all | bytes 262144 | tf_op jit(solution)/shard_map/all_to_all | solution.py:347
  80.2 0.6 convert_reduce_fusion
  (15 shorter events, 0.2 us)
Async XLA Ops:
  0.0 11.8 %collective-permute-start = (s32[2]{0:T(128)}, s32[2]{0:T(128)S(1)}, u32[]{:S(2)}, u32[]{:S(2)}) collective-permute-start(s32[2]{0:T(128)} %bitcast.101), channel_id=1, source_target_pairs={{224,0},{0,32},{32,64},{64,96},{96,128},{128,160},{160,192},{192,2... | collective-permute-start | bytes 32 | tf_op jit(solution)/shard_map/ppermute | solution.py:343
  26.6 23.4 %copy-start.1 = (f32[1,4,128,128]{3,2,1,0:T(8,128)S(1)}, f32[1,4,128,128]{3,2,1,0:T(8,128)}, u32[]{:S(2)}) copy-start(f32[1,4,128,128]{3,2,1,0:T(8,128)} %factor_ref.1) | copy-start | bytes 786436
  26.6 23.4 %copy-start.2 = (s32[1,8]{1,0:T(1,128)S(1)}, s32[1,8]{1,0:T(1,128)}, u32[]{:S(2)}) copy-start(s32[1,8]{1,0:T(1,128)} %param.15) | copy-start | bytes 100
  26.7 12.3 %collective-permute-start.3 = (f16[232,128]{1,0:T(8,128)(2,1)S(1)}, f16[232,128]{1,0:T(8,128)(2,1)S(1)}, u32[]{:S(2)}, u32[]{:S(2)}) collective-permute-start(f16[232,128]{1,0:T(8,128)(2,1)S(1)} %pad_maximum_fusion), channel_id=1, source_target_pairs={{16,0},{17,1},{18,2},{19,3},{20,4},{21,5},{22,6},{23,7},{24,8},{25... | collective-permute-start | bytes 178184 | tf_op jit(solution)/shard_map/ppermute | solution.py:366
  32.7 6.3 %collective-permute-start.2 = (f16[232,128]{1,0:T(8,128)(2,1)S(1)}, f16[232,128]{1,0:T(8,128)(2,1)S(1)}, u32[]{:S(2)}, u32[]{:S(2)}) collective-permute-start(f16[232,128]{1,0:T(8,128)(2,1)S(1)} %pad_maximum_fusion), channel_id=1, source_target_pairs={{24,0},{25,1},{26,2},{27,3},{28,4},{29,5},{30,6},{31,7},{0,8},{1,9... | collective-permute-start | bytes 178184 | tf_op jit(solution)/shard_map/ppermute | solution.py:366
  33.9 5.1 %collective-permute-start.1 = (f16[232,128]{1,0:T(8,128)(2,1)S(1)}, f16[232,128]{1,0:T(8,128)(2,1)S(1)}, u32[]{:S(2)}, u32[]{:S(2)}) collective-permute-start(f16[232,128]{1,0:T(8,128)(2,1)S(1)} %pad_maximum_fusion), channel_id=1, source_target_pairs={{8,0},{9,1},{10,2},{11,3},{12,4},{13,5},{14,6},{15,7},{16,8},{17,9... | collective-permute-start | bytes 178184 | tf_op jit(solution)/shard_map/ppermute | solution.py:366
  36.3 19.3 %copy-start = (bf16[1,2,512,512]{3,2,1,0:T(8,128)(2,1)S(1)}, bf16[1,2,512,512]{3,2,1,0:T(8,128)(2,1)}, u32[]{:S(2)}) copy-start(bf16[1,2,512,512]{3,2,1,0:T(8,128)(2,1)} %tile_ref.1) | copy-start | bytes 3145732
  36.3 19.3 %copy-start.3 = (s32[1,2]{1,0:T(1,128)S(1)}, s32[1,2]{1,0:T(1,128)}, u32[]{:S(2)}) copy-start(s32[1,2]{1,0:T(1,128)} %param.12) | copy-start | bytes 28
  36.3 19.3 %copy-start.4 = (s32[1,2]{1,0:T(1,128)S(1)}, s32[1,2]{1,0:T(1,128)}, u32[]{:S(2)}) copy-start(s32[1,2]{1,0:T(1,128)} %param.14) | copy-start | bytes 28
  52.9 10.7 %collective-permute-start.4 = (bf16[2,512,256]{2,1,0:T(8,128)(2,1)S(1)}, bf16[2,512,256]{2,1,0:T(8,128)(2,1)S(1)}, u32[]{:S(2)}, u32[]{:S(2)}) collective-permute-start(bf16[2,512,256]{2,1,0:T(8,128)(2,1)S(1)} %get-tuple-element.40), channel_id=1, source_target_pairs={{32,0},{64,32},{96,64},{128,96},{160,128},{192,160},{224,192},{0,2... | collective-permute-start | bytes 1572872 | tf_op jit(solution)/shard_map/ppermute | solution.py:343

commit v10 on v8

--- a/solution.py
+++ b/solution.py
@@ -155,8 +155,7 @@
 
 
 def updated_block(start, panels, upper, lower, limits):
-    high, low = panels
-    back = start - (dot(high, upper) + (dot(high, lower) + dot(low, upper)))
+    back = start - joined3(panels, (upper, lower))
     line = lax.broadcasted_iota(jnp.int32, (BLOCK, back.shape[1]), 0)
     live = jnp.concatenate([line < limit for limit in limits], axis=0)
     return jnp.where(live, back, 0.0).astype(BF16)

time: 81 us -> 81 us (level)
  no operation moved by 1% of the time
where the time goes in v10:
time: 81 us; the launch traced here: 80.8 us
  blocking collectives  41.5 us (51%)
  Pallas kernels  19.2 us (24%)
  starting transfers between devices  15 us (19%)
  waiting for transfers between devices  3.71 us (5%)
  other arithmetic  1.13 us (1%)
    all_to_all x3, blocking collectives, exchanged(): lax.all_to_all(shares, 'row', 0, 0, axis_index_groups=groups, tiled=True)  41.5 us
    ppermute x3, starting transfers between devices, around(): return lax.ppermute(share, 'row', route)  9.63 us
    pallas_call x1, Pallas kernels, local_grams(): pl.pallas_call(gram_kernel, out_shape=jax.ShapeDtypeStruct((count, SHARE,...  9.11 us
    ppermute x2, starting transfers between devices, passed_along(): return lax.ppermute(block, axis, route)  5.32 us
    pallas_call x1, Pallas kernels, left_products(): pl.pallas_call(left_kernel, out_shape=(jax.ShapeDtypeStruct((eigen, count...  4.24 us
    ppermute x2, waiting for transfers between devices, passed_along(): return lax.ppermute(block, axis, route)  3.7 us
    pallas_call x1, Pallas kernels, solve_and_update(): pl.pallas_call(solve_kernel, out_shape=(jax.ShapeDtypeStruct((count, BLOC...  2.74 us
    pallas_call x1, Pallas kernels, fetched_blocks(): pl.pallas_call(fetch_kernel, out_shape=(jax.ShapeDtypeStruct((count, BLOC...  2.63 us
  transfers between devices with their start and end apart: 5, of which 1 were waited for; matrix products, arithmetic and copies ran while one was open for 0% of the time, Pallas kernels for 20%

profile of v10, /device:TPU:1, one launch (start us, length us, event | category | flops | bytes accessed | tf_op | source)
XLA Modules:
  0.0 80.8 jit_solution(15360871427510228111)
XLA Ops:
  0.0 2.6 %collective-permute-start = (s32[2]{0:T(128)}, s32[2]{0:T(128)S(1)}, u32[]{:S(2)}, u32[]{:S(2)}) collective-permute-start(s32[2]{0:T(128)} %bitcast.101), channel_id=1, source_target_pairs={{224,0},{0,32},{32,64},{64,96},{96,128},{128,160},{160,192},{192,2... | collective-permute-start | bytes 32 | tf_op jit(solution)/shard_map/ppermute | solution.py:334
  2.6 9.1 %grams.1 = f32[8,232,128]{2,1,0:T(8,128)S(1)} custom-call(f32[1,4096,256]{2,1,0:T(8,128)} %start_ref.5, f32[1,4096,512]{2,1,0:T(8,128)} %panel_ref.5), custom_call_target="tpu_custom_call" | custom-call | flops 6442450944 | bytes 12582912 | tf_op jit(solution)/shard_map/grams/pallas_call | solution.py:94
  11.7 0.1 convert_element_type.55
  11.8 0.0 collective-permute-done.which_ref.want_ref
  11.8 14.6 %all_to_all.15 = f16[8,232,128]{2,1,0:T(8,128)(2,1)S(1)} all-to-all(f16[8,232,128]{2,1,0:T(8,128)(2,1)S(1)} %convert_element_type.55), channel_id=1, replica_groups={{0,1,2,3,4,5,6,7},{8,9,10,11,12,13,14,15},{16,17,18,19,20,21,22,23},{24..., dimensions={0} | all-to-all | bytes 950272 | tf_op jit(solution)/shard_map/all_to_all | solution.py:338
  26.4 0.1 slice_convert_fusion.7
  26.5 0.1 fusion.6
  26.6 0.0 copy-start.1
  26.6 0.0 copy-start.2
  26.7 6.1 %collective-permute-start.3 = (f16[232,128]{1,0:T(8,128)(2,1)S(1)}, f16[232,128]{1,0:T(8,128)(2,1)S(1)}, u32[]{:S(2)}, u32[]{:S(2)}) collective-permute-start(f16[232,128]{1,0:T(8,128)(2,1)S(1)} %pad_maximum_fusion), channel_id=1, source_target_pairs={{16,0},{17,1},{18,2},{19,3},{20,4},{21,5},{22,6},{23,7},{24,8},{25... | collective-permute-start | bytes 178184 | tf_op jit(solution)/shard_map/ppermute | solution.py:357
  32.7 1.2 %collective-permute-start.2 = (f16[232,128]{1,0:T(8,128)(2,1)S(1)}, f16[232,128]{1,0:T(8,128)(2,1)S(1)}, u32[]{:S(2)}, u32[]{:S(2)}) collective-permute-start(f16[232,128]{1,0:T(8,128)(2,1)S(1)} %pad_maximum_fusion), channel_id=1, source_target_pairs={{24,0},{25,1},{26,2},{27,3},{28,4},{29,5},{30,6},{31,7},{0,8},{1,9... | collective-permute-start | bytes 178184 | tf_op jit(solution)/shard_map/ppermute | solution.py:357
  33.9 2.4 %collective-permute-start.1 = (f16[232,128]{1,0:T(8,128)(2,1)S(1)}, f16[232,128]{1,0:T(8,128)(2,1)S(1)}, u32[]{:S(2)}, u32[]{:S(2)}) collective-permute-start(f16[232,128]{1,0:T(8,128)(2,1)S(1)} %pad_maximum_fusion), channel_id=1, source_target_pairs={{8,0},{9,1},{10,2},{11,3},{12,4},{13,5},{14,6},{15,7},{16,8},{17,9... | collective-permute-start | bytes 178184 | tf_op jit(solution)/shard_map/ppermute | solution.py:357
  36.3 0.0 copy-start
  36.3 0.0 copy-start.3
  36.3 0.0 copy-start.4
  36.3 2.6 %fetch.1 = (f32[2,512,256]{2,1,0:T(8,128)S(1)}, bf16[2,512,512]{2,1,0:T(8,128)(2,1)S(1)}, bf16[2,512,512]{2,1,0:T(8,128)(2,1)S(1)}) custom-call(s32[2]{0:T(128)S(1)} %collective-permute-done.which_ref.want_ref, f32[1,4096,256]{2,1,0:T(8,128)} %start_ref.5, f32[1,4096,512]{2,1,0:T(8,128)} %panel_ref.5), custom_call_target="tpu_custom_call" | custom-call | flops 524288 | bytes 6291456 | tf_op jit(solution)/shard_map/fetch/pallas_call | solution.py:134
  39.0 0.0 collective-permute-done.3
  39.0 0.0 collective-permute-done.2
  39.0 0.0 collective-permute-done.1
  39.2 0.1 broadcast_in_dim.6
  39.3 10.7 %all_to_all.16 = f16[8,224,128]{2,1,0:T(8,128)(2,1)S(1)} all-to-all(f16[8,224,128]{2,1,0:T(8,128)(2,1)S(1)} %broadcast_in_dim.6), channel_id=1, replica_groups={{0,1,2,3,4,5,6,7},{8,9,10,11,12,13,14,15},{16,17,18,19,20,21,22,23},{24..., dimensions={0} | all-to-all | bytes 917504 | tf_op jit(solution)/shard_map/all_to_all | solution.py:338
  50.0 0.1 convert_element_type.68.sums_ref
  50.1 0.0 copy-done.1
  50.1 0.0 copy-done.2
  50.1 2.7 %solve.1 = (bf16[2,512,256]{2,1,0:T(8,128)(2,1)S(1)}, bf16[512,256]{1,0:T(8,128)(2,1)S(1)}, bf16[512,256]{1,0:T(8,128)(2,1)S(1)}) custom-call(s32[2]{0:T(128)S(1)} %collective-permute-done.which_ref.want_ref, s32[8]{0:T(128)S(1)} %bitcast.97, f32[8,224,128]{2,1,0:T(8,128)S(1)} %convert_element_type.68.sums_ref, f32[8,128]{1,0:T(8,128)S(1)} %fusion.25.exponent_ref, ...), custom_call_target="tpu_custom_call" | custom-call | flops 805306368 | bytes 3145728 | tf_op jit(solution)/shard_map/solve/pallas_call | solution.py:267
  52.8 2.7 %collective-permute-start.4 = (bf16[2,512,256]{2,1,0:T(8,128)(2,1)S(1)}, bf16[2,512,256]{2,1,0:T(8,128)(2,1)S(1)}, u32[]{:S(2)}, u32[]{:S(2)}) collective-permute-start(bf16[2,512,256]{2,1,0:T(8,128)(2,1)S(1)} %get-tuple-element.40), channel_id=1, source_target_pairs={{32,0},{64,32},{96,64},{128,96},{160,128},{192,160},{224,192},{0,2... | collective-permute-start | bytes 1572872 | tf_op jit(solution)/shard_map/ppermute | solution.py:334
  55.6 0.0 copy-done.3
  55.6 4.2 %left.1 = (bf16[256,1024]{1,0:T(8,128)(2,1)S(1)}, bf16[256,1024]{1,0:T(8,128)(2,1)S(1)}) custom-call(s32[2]{0:T(128)S(1)} %bitcast.99, s32[2]{0:T(128)S(1)} %bitcast.100, s32[8]{0:T(128)S(1)} %bitcast.98, bf16[512,256]{1,0:T(8,128)(2,1)S(1)} %get-tuple-element.36.upper, bf16[512,256]{1,0:T(8,128)(2,1)S(1)} %get-tuple-element.37.lower, ...), custom_call_target="tpu_custom_call" | custom-call | flops 805306368 | bytes 3145728 | tf_op jit(solution)/shard_map/left/pallas_call | solution.py:293
  59.8 3.7 %collective-permute-done.4.right_ref = bf16[2,512,256]{2,1,0:T(8,128)(2,1)S(1)} collective-permute-done((bf16[2,512,256]{2,1,0:T(8,128)(2,1)S(1)}, bf16[2,512,256]{2,1,0:T(8,128)(2,1)S(1)}, u32[]{:S(2)}, u32[]{:S(2)}) %collective-permute-start.4) | collective-permute-done | bytes 524320 | tf_op jit(solution)/shard_map/ppermute | solution.py:334
  63.5 0.4 dipole.1
  64.0 16.2 %all_to_all.17 = bf16[32,8,256]{2,1,0:T(8,128)(2,1)S(1)} all-to-all(bf16[32,8,256]{2,1,0:T(8,128)(2,1)S(1)} %bitcast.96), channel_id=1, replica_groups=mesh['sym'=8,'row'=32] {'row'}, dimensions={0} | all-to-all | bytes 262144 | tf_op jit(solution)/shard_map/all_to_all | solution.py:338
  80.1 0.6 convert_reduce_fusion
  (15 shorter events, 0.2 us)
Async XLA Ops:
  0.0 11.8 %collective-permute-start = (s32[2]{0:T(128)}, s32[2]{0:T(128)S(1)}, u32[]{:S(2)}, u32[]{:S(2)}) collective-permute-start(s32[2]{0:T(128)} %bitcast.101), channel_id=1, source_target_pairs={{224,0},{0,32},{32,64},{64,96},{96,128},{128,160},{160,192},{192,2... | collective-permute-start | bytes 32 | tf_op jit(solution)/shard_map/ppermute | solution.py:334
  26.6 23.4 %copy-start.1 = (f32[1,4,128,128]{3,2,1,0:T(8,128)S(1)}, f32[1,4,128,128]{3,2,1,0:T(8,128)}, u32[]{:S(2)}) copy-start(f32[1,4,128,128]{3,2,1,0:T(8,128)} %factor_ref.1) | copy-start | bytes 786436
  26.6 23.4 %copy-start.2 = (s32[1,8]{1,0:T(1,128)S(1)}, s32[1,8]{1,0:T(1,128)}, u32[]{:S(2)}) copy-start(s32[1,8]{1,0:T(1,128)} %param.15) | copy-start | bytes 100
  26.7 12.3 %collective-permute-start.3 = (f16[232,128]{1,0:T(8,128)(2,1)S(1)}, f16[232,128]{1,0:T(8,128)(2,1)S(1)}, u32[]{:S(2)}, u32[]{:S(2)}) collective-permute-start(f16[232,128]{1,0:T(8,128)(2,1)S(1)} %pad_maximum_fusion), channel_id=1, source_target_pairs={{16,0},{17,1},{18,2},{19,3},{20,4},{21,5},{22,6},{23,7},{24,8},{25... | collective-permute-start | bytes 178184 | tf_op jit(solution)/shard_map/ppermute | solution.py:357
  32.7 6.3 %collective-permute-start.2 = (f16[232,128]{1,0:T(8,128)(2,1)S(1)}, f16[232,128]{1,0:T(8,128)(2,1)S(1)}, u32[]{:S(2)}, u32[]{:S(2)}) collective-permute-start(f16[232,128]{1,0:T(8,128)(2,1)S(1)} %pad_maximum_fusion), channel_id=1, source_target_pairs={{24,0},{25,1},{26,2},{27,3},{28,4},{29,5},{30,6},{31,7},{0,8},{1,9... | collective-permute-start | bytes 178184 | tf_op jit(solution)/shard_map/ppermute | solution.py:357
  33.9 5.1 %collective-permute-start.1 = (f16[232,128]{1,0:T(8,128)(2,1)S(1)}, f16[232,128]{1,0:T(8,128)(2,1)S(1)}, u32[]{:S(2)}, u32[]{:S(2)}) collective-permute-start(f16[232,128]{1,0:T(8,128)(2,1)S(1)} %pad_maximum_fusion), channel_id=1, source_target_pairs={{8,0},{9,1},{10,2},{11,3},{12,4},{13,5},{14,6},{15,7},{16,8},{17,9... | collective-permute-start | bytes 178184 | tf_op jit(solution)/shard_map/ppermute | solution.py:357
  36.3 19.3 %copy-start = (bf16[1,2,512,512]{3,2,1,0:T(8,128)(2,1)S(1)}, bf16[1,2,512,512]{3,2,1,0:T(8,128)(2,1)}, u32[]{:S(2)}) copy-start(bf16[1,2,512,512]{3,2,1,0:T(8,128)(2,1)} %tile_ref.1) | copy-start | bytes 3145732
  36.3 19.3 %copy-start.3 = (s32[1,2]{1,0:T(1,128)S(1)}, s32[1,2]{1,0:T(1,128)}, u32[]{:S(2)}) copy-start(s32[1,2]{1,0:T(1,128)} %param.12) | copy-start | bytes 28
  36.3 19.2 %copy-start.4 = (s32[1,2]{1,0:T(1,128)S(1)}, s32[1,2]{1,0:T(1,128)}, u32[]{:S(2)}) copy-start(s32[1,2]{1,0:T(1,128)} %param.14) | copy-start | bytes 28
  52.8 10.7 %collective-permute-start.4 = (bf16[2,512,256]{2,1,0:T(8,128)(2,1)S(1)}, bf16[2,512,256]{2,1,0:T(8,128)(2,1)S(1)}, u32[]{:S(2)}, u32[]{:S(2)}) collective-permute-start(bf16[2,512,256]{2,1,0:T(8,128)(2,1)S(1)} %get-tuple-element.40), channel_id=1, source_target_pairs={{32,0},{64,32},{96,64},{128,96},{160,128},{192,160},{224,192},{0,2... | collective-permute-start | bytes 1572872 | tf_op jit(solution)/shard_map/ppermute | solution.py:334
